TPU v7x, 32 devices: a whole 2x2x4 slice. The times are simulated.
32 devices in a mesh: seq: 8 (over z, y), fsdp: 4 (over x, core).
Axes of the slice: x: 2, y: 2, z: 4, core: 2. Of those that a mesh axis runs over, the one named last changes fastest.
Arguments:
- inputs: bfloat16 [4, 1024, 2048], P('fsdp', 'seq'), may hold values from -6 to 6
- qkv_weight: bfloat16 [2048, 4096], P(None, 'fsdp'), may hold values from -0.125 to 0.125
- gate_weight: bfloat16 [2048, 32], replicated, may hold values from -0.125 to 0.125
- conv_weight: bfloat16 [4, 4096], replicated, may hold values from -3 to 3
- head_rate: float32 [16], replicated, may hold values from 0 to 1, as said below
- dt_bias: float32 [16], replicated, may hold values from -2 to 1
- norm_gain: float32 [128], replicated, may hold values from 0.5 to 1.5
Outputs:
- output: bfloat16 [4, 1024, 2048], P('fsdp', 'seq')
Inputs may be any that keep to these rules, and one draw needn't show every extreme that they name: `head_rate`: positive decay rates of the value heads.
All inputs are finite; a program needn't handle non-finite values.
Results may differ from a plain program's by a relative error of at most 0.0063.
Values may be sent and summed in bfloat16 or wider, within the bound.
No kernel may reach another device: no remote copies, remote signals or barrier semaphores. Data moves between devices by JAX's collectives and lax.ppermute only.
A program may use at most 192 MiB of HBM per device.

v0:
```python
import jax
import jax.numpy as jnp
from jax import lax
from jax.sharding import PartitionSpec as P

HEAD = 128
HK = 8
HV = 16
KERNEL = 4
GROUP = 64


exact_products = lax.Precision.HIGHEST


def passed_along(value, axis, steps):
    count = lax.axis_size(axis)
    leading, last = (max(0, -steps), min(count, count - steps))
    return lax.ppermute(value, axis, [(source, source + steps) for source in range(leading, last)])


def prefix_2(part, axis, combine, identity):
    place = lax.axis_index(axis)
    gathered = jax.tree.map(lambda a: lax.all_gather(a, axis), part)
    state = jax.tree.map(lambda a, e: jnp.zeros_like(a) + jnp.asarray(e, a.dtype), part, identity)

    def one(hop, state):
        return combine(
            state, jax.tree.map(lambda a: lax.dynamic_index_in_dim(a, hop, 0, False), gathered)
        )

    return lax.fori_loop(0, place, one, state)


def convolve(extended, conv_weight, length):
    running = jnp.zeros((length, extended.shape[1]), jnp.float32)
    for tap_index in range(conv_weight.shape[0]):
        running = running + conv_weight[tap_index].astype(jnp.float32) * extended[
            tap_index : tap_index + length
        ].astype(jnp.float32)
    return jax.nn.silu(running)


def unit_rows(vectors):
    return vectors / jnp.sqrt(jnp.sum(vectors * vectors, axis=-1, keepdims=True) + 1e-06)


def head_inputs(activated, gates, head_rate, dt_bias):
    length = activated.shape[0]
    key_width = HK * HEAD
    blocks = length // GROUP
    query_heads = unit_rows(activated[:, :key_width].reshape(length, HK, HEAD)) * HEAD ** (-0.5)
    key_heads = unit_rows(activated[:, key_width : 2 * key_width].reshape(length, HK, HEAD))
    value_heads = activated[:, 2 * key_width :].reshape(length, HV, HEAD)
    query_heads = jnp.repeat(query_heads, HV // HK, axis=1)
    key_heads = jnp.repeat(key_heads, HV // HK, axis=1)
    strength = jax.nn.sigmoid(gates[:, :HV])
    log_decay = -head_rate * jax.nn.softplus(gates[:, HV:] + dt_bias)

    def arrange(array):
        return jnp.transpose(array.reshape(blocks, GROUP, HV, HEAD), (2, 0, 1, 3))

    def arrange_flat(array):
        return jnp.transpose(array.reshape(blocks, GROUP, HV), (2, 0, 1))

    return (
        arrange(query_heads),
        arrange(key_heads),
        arrange(value_heads),
        arrange_flat(log_decay),
        arrange_flat(strength),
    )


def group_parts(query_blocks, key_blocks, value_blocks, decay_blocks, strength_blocks):
    cumulative = jnp.cumsum(decay_blocks, axis=-1)
    spread = cumulative[..., :, None] - cumulative[..., None, :]
    row_index = jnp.arange(GROUP)[:, None]
    col_index = jnp.arange(GROUP)[None, :]
    strict = row_index > col_index
    within = row_index >= col_index
    key_key = jnp.einsum("hnid,hnjd->hnij", key_blocks, key_blocks, precision=exact_products)
    lower_part = jnp.where(
        strict,
        strength_blocks[..., :, None] * jnp.exp(jnp.where(strict, spread, 0.0)) * key_key,
        0.0,
    )
    system = lower_part + jnp.eye(GROUP, dtype=jnp.float32)
    scaled = jnp.concatenate(
        [
            (strength_blocks * jnp.exp(cumulative))[..., None] * key_blocks,
            strength_blocks[..., None] * value_blocks,
        ],
        axis=-1,
    )
    solved = lax.linalg.triangular_solve(
        system, scaled, left_side=True, lower=True, unit_diagonal=True
    )
    weighted_keys = solved[..., :HEAD]
    weighted_values = solved[..., HEAD:]
    query_key = jnp.einsum("hnid,hnjd->hnij", query_blocks, key_blocks, precision=exact_products)
    mixing = jnp.where(within, jnp.exp(jnp.where(within, spread, 0.0)) * query_key, 0.0)
    return (cumulative, weighted_keys, weighted_values, mixing)


def normalize(reads, norm_gain):
    square_mean = jnp.mean(reads * reads, axis=-1, keepdims=True)
    scaled = reads / jnp.sqrt(square_mean + 1e-06) * norm_gain
    return jnp.transpose(scaled, (0, 2, 1, 3)).reshape(-1, HV * HEAD).astype(jnp.bfloat16)


def matmul_heads(left, right):
    return jnp.einsum("hij,hjk->hik", left, right, precision=exact_products)


def combine_blocks(earlier, later):
    return (matmul_heads(earlier[0], later[0]), matmul_heads(earlier[1], later[0]) + later[1])


def body(inputs, qkv_weight, gate_weight, conv_weight, head_rate, dt_bias, norm_gain):
    tokens = inputs[0]
    length = tokens.shape[0]
    rim_rows = KERNEL - 1
    mixed = jnp.dot(
        tokens,
        lax.all_gather(qkv_weight, "fsdp", axis=1, tiled=True),
        preferred_element_type=jnp.float32,
    ).astype(jnp.bfloat16)
    before_values = passed_along(mixed[length - rim_rows :], "seq", 1)
    extended = jnp.concatenate([before_values, mixed], axis=0)
    gates = jnp.dot(tokens, gate_weight, preferred_element_type=jnp.float32)
    activated = convolve(extended, conv_weight, length)
    query_blocks, key_blocks, value_blocks, decay_blocks, strength_blocks = head_inputs(
        activated, gates, head_rate, dt_bias
    )
    cumulative, weighted_keys, weighted_values, mixing = group_parts(
        query_blocks, key_blocks, value_blocks, decay_blocks, strength_blocks
    )
    growth = jnp.exp(cumulative)
    trailing = jnp.exp(cumulative[..., -1:] - cumulative)
    identity_map = jnp.broadcast_to(jnp.eye(HEAD, dtype=jnp.float32), (HV, HEAD, HEAD))
    empty_state = jnp.zeros((HV, HEAD, HEAD), jnp.float32)

    def compose(running, items):
        key_c, wkey_c, wval_c, grow_c, trail_c = items
        map_c = grow_c[:, -1, None, None] * identity_map - jnp.einsum(
            "hjd,hj,hje->hde", wkey_c, trail_c, key_c, precision=exact_products
        )
        add_c = jnp.einsum("hjv,hj,hje->hve", wval_c, trail_c, key_c, precision=exact_products)
        return (combine_blocks(running, (map_c, add_c)), None)

    block_items = tuple(
        (
            jnp.moveaxis(array, 1, 0)
            for array in (key_blocks, weighted_keys, weighted_values, growth, trailing)
        )
    )
    block_total = lax.scan(compose, (identity_map, empty_state), block_items)[0]
    prefix = prefix_2(block_total, "seq", combine_blocks, (identity_map, empty_state))

    def advance(state, items):
        query_c, key_c, wkey_c, wval_c, mix_c, grow_c, trail_c = items
        fresh = wval_c - jnp.einsum("hcd,hvd->hcv", wkey_c, state, precision=exact_products)
        reads = grow_c[..., None] * jnp.einsum(
            "hcd,hvd->hcv", query_c, state, precision=exact_products
        )
        reads = reads + jnp.einsum("hij,hjv->hiv", mix_c, fresh, precision=exact_products)
        state = grow_c[:, -1, None, None] * state + jnp.einsum(
            "hjv,hj,hjd->hvd", fresh, trail_c, key_c, precision=exact_products
        )
        return (state, reads)

    items = tuple(
        (
            jnp.moveaxis(array, 1, 0)
            for array in (
                query_blocks,
                key_blocks,
                weighted_keys,
                weighted_values,
                mixing,
                growth,
                trailing,
            )
        )
    )
    reads = lax.scan(advance, prefix[1], items)[1]
    return normalize(reads, norm_gain)[None]


def solution(mesh):
    in_specs = (P("fsdp", "seq", None), P(None, "fsdp"), P(), P(), P(), P(), P())
    out_specs = P("fsdp", "seq", None)
    return jax.shard_map(body, mesh=mesh, in_specs=in_specs, out_specs=out_specs, check_vma=False)
```

profile of v0, /device:TPU:29, one launch (start us, length us, event | category | flops | bytes accessed | tf_op | source)
XLA Modules:
  0.0 651.7 jit_solution(17452189207774878748)
XLA Ops:
  9.0 107.2 %all-gather.6.cloned.1.call-done = bf16[2048,4096]{1,0:T(8,128)(2,1)} async-done(((bf16[2048,1024]{1,0:T(8,128)(2,1)}), bf16[2048,4096]{1,0:T(8,128)(2,1)}) %all-gather.6.cloned.1.call-update) | async-done | bytes 16777232 | tf_op jit(solution)/shard_map/all_gather | solution.py:126
  116.2 8.1 %convolution_convert_fusion = bf16[128,4096]{1,0:T(8,128)(2,1)S(1)} fusion(bf16[2048,4096]{1,0:T(8,128)(2,1)} %all-gather.6.cloned.1.call-done, bf16[1,128,2048]{2,1,0:T(8,128)(2,1)S(1)} %copy-done), kind=kOutput, calls=%fused_computation.50 | convolution fusion | flops 2148007936 | bytes 18350080 | tf_op jit(solution)/shard_map/dot_general | solution.py:124
  125.9 3.1 collective-permute-done
  134.3 158.0 %custom-call.3 = f32[16,2,1,64,64]{3,4,2,1,0:T(8,128)} custom-call(f32[16,2,1,64,64]{4,3,2,1,0:T(8,128)S(1)} %fusion.44), custom_call_target="InvertDiagBlocksLowerTriangular" | custom-call | tf_op jit(solution)/shard_map/triangular_solve | solution.py:96
  298.1 21.5 %while.39 = (s32[]{:T(128)}, f32[16,128,128]{1,2,0:T(8,128)S(1)}, f32[16,128,128]{1,2,0:T(8,128)}, f32[2,16,64]{1,2,0:T(8,128)S(1)}, f32[2,16,64,128]{3,2,1,0:T(...) while((s32[]{:T(128)}, f32[16,128,128]{1,2,0:T(8,128)S(1)}, ...), condition=%wide.region_3.4_spmd.clone, body=%wide.region_2.3_spmd.clone.sunk | while | flops 1209270272 | bytes 17926940 | solution.py:158
  298.3 3.1 convolution_subtract_fusion.5
  308.3 3.1 convolution_subtract_fusion.5
  311.4 3.1 convolution_bitcast_fusion.7
  314.6 3.0 convolution_add_fusion.5
  326.9 116.6 %all-gather.8.cloned.1.call-done = f32[128,128,128]{2,1,0:T(8,128)} async-done(((f32[16,128,128]{2,1,0:T(8,128)}), f32[128,128,128]{2,1,0:T(8,128)}) %all-gather.8.cloned.1.call-update) | async-done | bytes 8388624 | tf_op jit(solution)/shard_map/all_gather | solution.py:24
  443.5 124.8 %all-gather.10.cloned.1.call-done = f32[128,128,128]{2,1,0:T(8,128)} async-done(((f32[16,128,128]{2,1,0:T(8,128)}), f32[128,128,128]{2,1,0:T(8,128)}) %all-gather.10.cloned.1.call-update) | async-done | bytes 8388624 | tf_op jit(solution)/shard_map/all_gather | solution.py:24
  569.4 48.8 %while.37 = (s32[]{:T(128)}, f32[16,128,128]{1,2,0:T(8,128)}, s32[]{:T(128)}, f32[8,16,128,128]{3,2,1,0:T(8,128)}, f32[8,16,128,128]{3,2,1,0:T(8,128)}, /*index=5*/s32[]{:T(128)}, s32[]{:T(128)}, s32[]{:T(128)}) while((s32[]{:T(128)}, f32[16,128,128]{1,2,0:T(8,128)}, s32[]{:T(128)}, f32[8,16,128,128]{3,2,1,0:T(8,128)}, ...), condition=%wide.region_5.6_spmd, body=%wide.region_4.5_spmd.sunk | while | flops 402915328 | bytes 10485887 | solution.py:32
  572.3 4.1 fusion.94
  579.3 4.1 fusion.94
  586.2 4.1 fusion.94
  593.2 4.1 fusion.94
  600.2 4.1 fusion.94
  607.1 4.1 fusion.94
  614.1 4.1 fusion.94
  619.8 20.8 %while.38 = (s32[]{:T(128)}, f32[16,128,128]{2,1,0:T(8,128)S(1)}, f32[2,16,64,128]{3,2,1,0:T(8,128)}, f32[2,16,64]{1,2,0:T(8,128)S(1)}, f32[2,16,64,128]{3,2,1,0...) while((s32[]{:T(128)}, f32[16,128,128]{2,1,0:T(8,128)S(1)}, ...), condition=%wide.region_8.9_spmd, body=%wide.region_7.8_spmd.sunk | while | flops 705691648 | bytes 12098329 | solution.py:187
  619.8 3.4 convolution_subtract_fusion.4
  624.0 4.0 fusion.103
  630.2 3.4 convolution_subtract_fusion.4
  634.4 4.0 fusion.103
  (146 shorter events, 64.0 us)
Async XLA Ops:
  6.5 1.1 copy-start
  6.5 0.8 copy-start.14
  6.5 1.1 copy-start.11
  6.5 1.4 copy-start.12
  6.5 2.4 copy-start.10
  6.5 109.6 %all-gather.6.cloned.1.call-start = ((), (), s32[]{:S(2)}) async-start(), calls=%async_computation | async-start | bytes 20971520 | tf_op jit(solution)/shard_map/all_gather | solution.py:126
  7.3 436.2 %all-gather.8.cloned.1.call-start = ((), (), s32[]{:S(2)}) async-start(), calls=%async_computation.1 | async-start | bytes 9437184 | tf_op jit(solution)/shard_map/all_gather | solution.py:24
  124.3 4.7 collective-permute-start
  132.4 165.4 %copy-start.5 = (f32[128,8,2,128]{3,0,2,1:T(8,128)}, f32[128,8,2,128]{3,0,2,1:T(8,128)S(1)}, u32[]{:S(2)}) copy-start(f32[128,8,2,128]{3,0,2,1:T(8,128)S(1)} %broadcast_in_dim.67) | copy-start | bytes 3145732
  292.3 1.2 copy-start.9
  301.4 1.9 copy-start.3
  311.4 3.2 copy-start.3
  319.5 1.4 copy-start.2
  320.9 1.5 copy-start.8
  320.9 247.4 %all-gather.10.cloned.1.call-start = ((), (), s32[]{:S(2)}) async-start(), calls=%async_computation.2 | async-start | bytes 9437184 | tf_op jit(solution)/shard_map/all_gather | solution.py:24
  322.5 1.7 copy-start.6
  323.2 1.0 copy-start.4
  619.8 22.5 %copy-start.13 = (f32[128]{0:T(128)S(1)}, f32[128]{0:T(128)}, u32[]{:S(2)}) copy-start(f32[128]{0:T(128)} %param.19) | copy-start | bytes 1540
  619.8 3.4 copy-start.7
  630.2 3.4 copy-start.7
  640.6 4.6 copy-start.1
Sparse Core Ops, SparseCore 0:
  8.9 107.2 all-gather.5
  321.0 122.4 all-gather.7
  445.6 122.6 all-gather.9
where the time goes:
time: 653 us; the launch traced here: 652 us
  waiting for transfers between devices  352 us (54%)
  other arithmetic  165 us (25%)
  matrix products  85.2 us (13%)
  local copies, waits for them, and re-layouts  33.5 us (5%)
  between operations  13.6 us (2%)
    all_gather x2, waiting for transfers between devices, prefix_2(): gathered = jax.tree.map(lambda a: lax.all_gather(a, axis), part)  241 us
    another operation x2, other arithmetic, group_parts(): lax.linalg.triangular_solve(system, scaled, left_side=True, lower=True, u...  158 us
    all_gather x1, waiting for transfers between devices, body(): lax.all_gather(qkv_weight, 'fsdp', axis=1, tiled=True)  107 us
    dot_general x11, matrix products, matmul_heads(): return jnp.einsum('hij,hjk->hik', left, right, precision=exact_products)  37.4 us
  transfers between devices with their start and end apart: 4, of which 4 were waited for; matrix products, arithmetic and copies ran while one was open for 1% of the time, Pallas kernels for 0%

commit v1 on v0

v1 whole, which is shorter than its diff:
```python
import jax
import jax.numpy as jnp
import numpy as np
from jax import lax
from jax.experimental import pallas as pl
from jax.experimental.pallas import tpu as pltpu
from jax.sharding import Mesh
from jax.sharding import PartitionSpec as P

HEAD = 128
HK = 8
HV = 16
KERNEL = 4
PAIR = 2
SPLIT = HK // PAIR
CHUNK = 128
BASE = 32
EXTRA = 16
RIM = 8
UNITS = HV // SPLIT
F32 = jnp.float32
BF16 = jnp.bfloat16
HIGHEST = lax.Precision.HIGHEST


def shifted(value, axes, pairs):
    return lax.ppermute(value, axes, pairs)


def swapped(value, axis, bit):
    count = lax.axis_size(axis)
    return lax.ppermute(value, axis, [(i, i ^ bit) for i in range(count)])


def dot(a, b):
    return jnp.dot(a, b, preferred_element_type=F32)


def halves(a):
    high = a.astype(BF16)
    return high, (a - high.astype(F32)).astype(BF16)


def dot3(a, b):
    return dot(a[0], b[0]) + (dot(a[0], b[1]) + dot(a[1], b[0]))


def split3(a):
    high = a.astype(BF16).astype(F32)
    rest = a - high
    middle = rest.astype(BF16).astype(F32)
    return high, middle, rest - middle


def iota(shape, dim):
    return lax.broadcasted_iota(jnp.int32, shape, dim)


def project_kernel(place, x0, x1, x2, x3, rims, gate_t, w_a, w_b, out, lhs, gates):
    step = pl.program_id(0)
    rows = x0.shape[0]
    me = place[0]

    @pl.when(step == 0)
    def _():
        for k, x in enumerate((x0, x1, x2, x3)):
            lhs[k * rows : (k + 1) * rows, :] = x[...]
        lhs[4 * rows :, :] = rims[...]
        raw = lax.dot_general(
            gate_t[...], lhs[: 4 * rows, :], (((1,), (1,)), ((), ())), preferred_element_type=F32
        )
        for part, value in enumerate(split3(raw)):
            for j in range(SPLIT):
                for k in range(4):
                    both = value[2 * j : 2 * j + 2, k * rows : (k + 1) * rows]
                    gates[j, k, part : part + 1, :] = jnp.concatenate([both[0:1], both[1:2]], axis=1)

    weights = jnp.concatenate([w_a[...], w_b[...]], axis=1)
    mixed = dot(lhs[...], weights)
    for k in range(4):
        target = jnp.bitwise_xor(me, k)
        out[0, target, :rows, :] = mixed[k * rows : (k + 1) * rows].astype(BF16)
        before = mixed[4 * rows + k * EXTRA : 4 * rows + (k + 1) * EXTRA]
        before = jnp.where(iota(before.shape, 0) < 3, gates[step, k], before)
        out[0, target, rows:, :] = before.astype(BF16)


def project(place, xs, rims, gate_t, weight):
    rows, depth = xs[0].shape
    width = 2 * HEAD
    whole = lambda shape: pl.BlockSpec(shape, lambda j, s: (0,) * len(shape))
    grid_spec = pltpu.PrefetchScalarGridSpec(
        num_scalar_prefetch=1,
        grid=(SPLIT,),
        in_specs=[whole((rows, depth))] * 4
        + [
            whole(rims.shape),
            whole(gate_t.shape),
            pl.BlockSpec((depth, HEAD), lambda j, s: (0, jnp.where(s[0] < 2, j, 2 * j))),
            pl.BlockSpec((depth, HEAD), lambda j, s: (0, jnp.where(s[0] < 2, SPLIT + j, 2 * j + 1))),
        ],
        out_specs=pl.BlockSpec((1, 4, rows + EXTRA, width), lambda j, s: (j, 0, 0, 0)),
        scratch_shapes=[
            pltpu.VMEM((4 * rows + 4 * EXTRA, depth), BF16),
            pltpu.VMEM((SPLIT, 4, EXTRA, width), F32),
        ],
    )
    return pl.pallas_call(
        project_kernel,
        grid_spec=grid_spec,
        out_shape=jax.ShapeDtypeStruct((SPLIT, 4, rows + EXTRA, width), BF16),
        name="project",
    )(place, *xs, rims, gate_t, weight, weight)


def base_inverse(lower):
    count = CHUNK // BASE
    tiles = BASE // 8
    lane_block = iota((8, CHUNK), 1) // BASE
    packed, result = [], []
    for t in range(tiles):
        tile = jnp.zeros((8, CHUNK), F32)
        for b in range(count):
            start = b * BASE + 8 * t
            tile = jnp.where(lane_block == b, lower[start : start + 8], tile)
        packed.append(tile)
        inside = iota((8, CHUNK), 1) % BASE
        result.append(jnp.where(inside == iota((8, CHUNK), 0) + 8 * t, 1.0, 0.0))
    for j in range(BASE - 1):
        row = jnp.broadcast_to(result[j // 8][j % 8 : j % 8 + 1], (8, CHUNK))
        source = lane_block * BASE + j
        for t in range((j + 1) // 8, tiles):
            column = jnp.take_along_axis(packed[t], source, axis=1)
            result[t] = result[t] - column * row
    side = jnp.concatenate(result, axis=0)
    block = iota((BASE, CHUNK), 1) // BASE
    return jnp.concatenate([jnp.where(block == b, side, 0.0) for b in range(count)], axis=0)


def inverse(lower):
    total = base_inverse(lower)
    row, column = iota((CHUNK, CHUNK), 0), iota((CHUNK, CHUNK), 1)
    size = BASE
    while size < CHUNK:
        inside = (row // (2 * size) == column // (2 * size)) & (row // size > column // size)
        corner = halves(jnp.where(inside, lower, 0.0))
        parts = halves(total)
        total = total - dot3(parts, halves(dot3(corner, parts)))
        size *= 2
    return total


def prepare_kernel(seg_product, place, rate, bias, message, taps, carry_out, add_out, final, *rest):
    if seg_product:
        product_out, tail, state, product = rest
    else:
        tail, state = rest
    step = pl.program_id(0)
    j = place[0]
    rows = CHUNK

    @pl.when(step == 0)
    def _():
        state[...] = jnp.zeros_like(state)
        for f in range(4):
            tail[f] = message[f, rows + EXTRA - RIM :, :].astype(F32)

    row, column = iota((rows, rows), 0), iota((rows, rows), 1)
    strict, within = row > column, row >= column
    eye = jnp.where(row == column, 1.0, 0.0)
    if seg_product:

        @pl.when(step == 0)
        def _():
            product[...] = jnp.broadcast_to(eye, product.shape)

    def activated(f, half, first):
        lanes = slice(half * HEAD, (half + 1) * HEAD)
        here = message[f, :rows, lanes].astype(F32)
        extended = jnp.concatenate([tail[f, :, lanes], here], axis=0)
        start = pl.multiple_of(first * HEAD, HEAD)
        weights = taps[:, pl.ds(start, HEAD)].astype(F32)
        total = jnp.zeros((rows, HEAD), F32)
        for tap in range(KERNEL):
            begin = RIM - (KERNEL - 1) + tap
            total = total + weights[tap : tap + 1] * extended[begin : begin + rows]
        tail[f, :, lanes] = here[rows - RIM :]
        return total / (1.0 + jnp.exp(-total))

    def unit(vectors):
        return vectors * lax.rsqrt(jnp.sum(vectors * vectors, axis=-1, keepdims=True) + 1e-06)

    decay_rows, strength_rows = [], []
    for u in range(UNITS):
        h, a = u // 2, u % 2
        head = 2 * (SPLIT * h + j) + a
        lanes = slice(a * HEAD, (a + 1) * HEAD)

        def gate(f):
            parts = message[f, rows : rows + EXTRA, lanes].astype(F32)
            return (parts[0:1] + parts[1:2]) + parts[2:3]

        strength_rows.append(1.0 / (1.0 + jnp.exp(-gate(h))))
        shift = gate(2 + h) + bias[head]
        soft = jnp.maximum(shift, 0.0) + jnp.log1p(jnp.exp(-jnp.abs(shift)))
        decay_rows.append(-rate[head] * soft)
    table = jnp.concatenate(decay_rows + strength_rows, axis=0)
    upper = jnp.where(row <= column, 1.0, 0.0)
    cum_rows = jnp.dot(table, upper, precision=HIGHEST, preferred_element_type=F32)
    lower_eye = jnp.concatenate([jnp.where(within, 1.0, 0.0), eye], axis=0)
    columns = lax.dot_general(
        lower_eye, table, (((1,), (1,)), ((), ())), precision=HIGHEST, preferred_element_type=F32
    )

    for h in range(PAIR):
        head = SPLIT * h + j
        query = unit(activated(0, h, head)) * HEAD ** (-0.5)
        key = unit(activated(1, h, HK + head))
        key_t = key.T
        key_t_parts = halves(key_t)
        both = halves(jnp.concatenate([key, query], axis=0))
        scores = dot3(both, key_t_parts)
        key_key, query_key = scores[:rows], scores[rows:]
        for a in range(2):
            u = 2 * h + a
            value = activated(2 + h, a, 2 * HK + 2 * head + a)
            cum_c = columns[:rows, u : u + 1]
            strength = columns[rows:, UNITS + u : UNITS + u + 1]
            cum_r = cum_rows[u : u + 1]
            last = cum_rows[u : u + 1, rows - 1 : rows]
            ratio = jnp.exp(jnp.minimum(cum_c - cum_r, 0.0))
            growth = jnp.exp(cum_c)
            trailing = jnp.exp(jnp.minimum(last - cum_r, 0.0))
            lower = jnp.where(strict, strength * ratio * key_key, 0.0)
            mixing = jnp.where(within, ratio * query_key, 0.0)
            solve = inverse(lower)
            scaled = jnp.concatenate([(strength * growth) * key, strength * value], axis=1)
            weighted = dot3(halves(solve), halves(scaled))
            left = jnp.concatenate([trailing * key_t, mixing], axis=0)
            mixed = dot3(halves(left), halves(weighted))
            carry = jnp.exp(last) * eye - mixed[:rows, :HEAD]
            read = growth * query - mixed[rows:, :HEAD]
            carry_out[0, u, :rows] = carry
            carry_out[0, u, rows:] = read
            add_out[0, u] = mixed[:, HEAD:]
            carry_parts = halves(carry)
            state[u] = dot3(carry_parts, halves(state[u])) + mixed[:rows, HEAD:]
            if seg_product:
                product[u] = dot3(carry_parts, halves(product[u]))

    @pl.when(step == pl.num_programs(0) - 1)
    def _():
        final[...] = state[...].astype(final.dtype)
        if seg_product:
            product_out[...] = product[...].astype(product_out.dtype)


def prepare(place, rate, bias, message, taps, seg_product):
    blocks = message.shape[0] // 4
    rows = message.shape[1] - EXTRA
    assert rows == CHUNK
    whole = lambda shape: pl.BlockSpec(shape, lambda b, *s: (0,) * len(shape))
    state_shape = (UNITS, HEAD, HEAD)
    out_shape = [
        jax.ShapeDtypeStruct((blocks, UNITS, 2 * rows, HEAD), F32),
        jax.ShapeDtypeStruct((blocks, UNITS, 2 * rows, HEAD), F32),
        jax.ShapeDtypeStruct(state_shape, BF16),
    ]
    stream = pl.BlockSpec((1, UNITS, 2 * rows, HEAD), lambda b, *s: (b, 0, 0, 0))
    out_specs = [stream, stream, whole(state_shape)]
    scratch = [pltpu.VMEM((4, RIM, 2 * HEAD), F32), pltpu.VMEM(state_shape, F32)]
    if seg_product:
        out_shape.append(jax.ShapeDtypeStruct(state_shape, F32))
        out_specs.append(whole(state_shape))
        scratch.append(pltpu.VMEM(state_shape, F32))
    grid_spec = pltpu.PrefetchScalarGridSpec(
        num_scalar_prefetch=3,
        grid=(blocks,),
        in_specs=[
            pl.BlockSpec((4, rows + EXTRA, 2 * HEAD), lambda b, *s: (b, 0, 0)),
            whole(taps.shape),
        ],
        out_specs=out_specs,
        scratch_shapes=scratch,
    )
    return pl.pallas_call(
        lambda *refs: prepare_kernel(seg_product, *refs),
        grid_spec=grid_spec,
        out_shape=out_shape,
        name="prepare",
    )(place, rate, bias, message, taps)


def read_kernel(place, carry, add, start, gain, out, state):
    @pl.when(pl.program_id(0) == 0)
    def _():
        state[...] = start[...].astype(F32)

    rows = CHUNK
    for u in range(UNITS):
        both = dot3(halves(carry[0, u]), halves(state[u])) + add[0, u]
        state[u] = both[:rows]
        reads = both[rows:]
        mean = jnp.mean(reads * reads, axis=-1, keepdims=True)
        out[0, :, u * HEAD : (u + 1) * HEAD] = (
            reads / jnp.sqrt(mean + 1e-06) * gain[...]
        ).astype(BF16)


def read(place, carry, add, start, gain):
    blocks, _, double, _ = carry.shape
    rows = double // 2
    whole = lambda shape: pl.BlockSpec(shape, lambda b, *s: (0,) * len(shape))
    stream = pl.BlockSpec((1, UNITS, double, HEAD), lambda b, *s: (b, 0, 0, 0))
    grid_spec = pltpu.PrefetchScalarGridSpec(
        num_scalar_prefetch=1,
        grid=(blocks,),
        in_specs=[stream, stream, whole(start.shape), whole(gain.shape)],
        out_specs=pl.BlockSpec(
            (1, rows, UNITS * HEAD), lambda b, s: (jnp.bitwise_xor(b, s[0]), 0, 0)
        ),
        scratch_shapes=[pltpu.VMEM(start.shape, F32)],
    )
    return pl.pallas_call(
        read_kernel,
        grid_spec=grid_spec,
        out_shape=jax.ShapeDtypeStruct((blocks, rows, UNITS * HEAD), BF16),
        name="read",
    )(place, carry, add, start, gain)


def assemble_kernel(place, *refs):
    out = refs[-1]
    width = 2 * HEAD
    for k, piece in enumerate(refs[:-1]):
        source = jnp.bitwise_xor(place[0], k)
        for h in range(PAIR):
            first = pl.multiple_of((h * SPLIT + source) * width, width)
            out[0, :, pl.ds(first, width)] = piece[:, h * width : (h + 1) * width]


def assemble(place, pieces):
    rows = pieces[0].shape[0]
    return pl.pallas_call(
        assemble_kernel,
        in_specs=[pl.BlockSpec(memory_space=pltpu.SMEM)]
        + [pl.BlockSpec(memory_space=pltpu.VMEM)] * len(pieces),
        out_specs=pl.BlockSpec(memory_space=pltpu.VMEM),
        out_shape=jax.ShapeDtypeStruct((1, rows, HV * HEAD), BF16),
        name="assemble",
    )(place, *pieces)


def messages_direct(tokens, qkv_weight, gate_weight, seq_count):
    me = lax.axis_index("fsdp")
    rim_rows = tokens[tokens.shape[0] - EXTRA :]
    far = swapped(tokens, "fsdp", 2)
    near = swapped(tokens, "fsdp", 1)
    rim_0 = shifted(rim_rows, ("seg", "sq"), [(i, i + 1) for i in range(seq_count - 1)])
    rim_2 = swapped(rim_0, "fsdp", 2)
    third = swapped(far, "fsdp", 1)
    rims_other = swapped(jnp.concatenate([rim_0, rim_2], axis=0), "fsdp", 1)
    rims = jnp.concatenate([rim_0, rims_other[:EXTRA], rim_2, rims_other[EXTRA:]], axis=0)
    share = 2 * HV // 4
    gate_t = lax.dynamic_slice_in_dim(gate_weight, me * share, share, 1).T
    place = me.astype(jnp.int32)[None]
    message = project(place, (tokens, near, far, third), rims, gate_t, qkv_weight)
    message = message.reshape((SPLIT * 4,) + message.shape[2:])
    return lax.all_to_all(message, ("sq", "fsdp"), 0, 0, tiled=True)


def messages_staged(tokens, qkv_weight, gate_weight, seq_count):
    length = tokens.shape[0]
    every = lax.all_gather(tokens, "fsdp", axis=0)
    mixed = jnp.einsum("ild,dc->ilc", every, qkv_weight, preferred_element_type=F32).astype(BF16)
    mixed = lax.all_to_all(mixed, "fsdp", 0, 2, tiled=True)[0]
    rim = shifted(
        mixed[length - RIM :], ("seg", "sq"), [(i, i + 1) for i in range(seq_count - 1)]
    )
    gates = jnp.dot(tokens, gate_weight, preferred_element_type=F32)
    high = lax.reduce_precision(gates, 8, 7)
    middle = lax.reduce_precision(gates - high, 8, 7)
    parts = jnp.stack([high, middle, (gates - high) - middle]).astype(BF16)
    parts = parts.reshape(3, length, 4, SPLIT, 2).transpose(3, 2, 0, 4, 1)
    parts = parts.reshape(SPLIT, 4, 3, 2 * length)

    def by_target(rows):
        count = rows.shape[0]
        query_key = rows[:, : 2 * HK * HEAD].reshape(count, 2, PAIR, SPLIT, HEAD)
        query_key = query_key.transpose(3, 1, 0, 2, 4).reshape(SPLIT, 2, count, 2 * HEAD)
        value = rows[:, 2 * HK * HEAD :].reshape(count, PAIR, SPLIT, 2 * HEAD)
        return jnp.concatenate([query_key, value.transpose(2, 1, 0, 3)], axis=1)

    blank = jnp.zeros((SPLIT, 4, EXTRA - RIM - 3, 2 * HEAD), BF16)
    message = jnp.concatenate([by_target(mixed), parts, blank, by_target(rim)], axis=2)
    message = lax.all_to_all(message, "sq", 0, 0, tiled=True)
    return message.reshape((SPLIT * 4,) + message.shape[2:])


def body(inputs, qkv_weight, gate_weight, conv_weight, head_rate, dt_bias, norm_gain):
    segments = lax.axis_size("seg")
    tokens = inputs[0]
    build = messages_direct if lax.axis_size("fsdp") == 4 else messages_staged
    message = build(tokens, qkv_weight, gate_weight, segments * SPLIT)
    place = lax.axis_index("sq").astype(jnp.int32)[None]
    outs = prepare(place, head_rate, dt_bias, message, conv_weight, segments > 2)
    carry, add, final = outs[:3]
    onward = [(i, i + 1) for i in range(segments - 1)]
    if segments == 1:
        start = jnp.zeros_like(final)
    elif segments == 2:
        start = shifted(final, "seg", onward)
    else:
        start = jnp.zeros_like(final)
        for _ in range(segments - 1):
            ahead = jnp.einsum("hij,hjk->hik", outs[3], start.astype(F32), precision=HIGHEST)
            start = shifted((ahead + final.astype(F32)).astype(BF16), "seg", onward)
    pieces = read(place, carry, add, start, norm_gain[None])
    received = [pieces[0]] + [swapped(pieces[k], "sq", k) for k in range(1, SPLIT)]
    return assemble(place, received)


def solution(mesh):
    seq, fsdp = mesh.shape["seq"], mesh.shape["fsdp"]
    parts = Mesh(mesh.devices.reshape(seq // SPLIT, SPLIT, fsdp), ("seg", "sq", "fsdp"))
    split = P("fsdp", ("seg", "sq"), None)
    in_specs = (split, P(None, "fsdp"), P(), P(), P(), P(), P())
    return jax.shard_map(body, mesh=parts, in_specs=in_specs, out_specs=split, check_vma=False)
```

time: 653 us -> 111 us (0.17)
  waiting for transfers between devices: 352 us -> 42.9 us
  other arithmetic: 165 us -> 0.73 us
  matrix products: 85.2 us -> 0 us
  Pallas kernels: 0 us -> 42.1 us
  local copies, waits for them, and re-layouts: 33.5 us -> 6.44 us
  starting transfers between devices: 1.41 us -> 17.2 us
  between operations: 13.6 us -> 0.05 us
    all_gather x3 -> x0, waiting for transfers between devices: 349 us -> none  [the longest x2 241 us: prefix_2(): gathered = jax.tree.map(lambda a: lax.all_gather(a, axis), part)]
    another operation x3 -> x0, other arithmetic: 158 us -> none  [the longest x2 158 us: group_parts(): lax.linalg.triangular_solve(system, scaled, left_side=True, lower=True, u...]
    dot_general x27 -> x0, matrix products: 83.2 us -> none  [the longest x11 37.4 us: matmul_heads(): return jnp.einsum('hij,hjk->hik', left, right, precision=exact_products)]
    pallas_call x0 -> x4, Pallas kernels: none -> 42.1 us  [the longest x1 28 us: prepare(): pl.pallas_call(lambda *refs: prepare_kernel(seg_product, *refs), grid_spe...]
    ppermute x1 -> x10, waiting for transfers between devices: 3.09 us -> 27.1 us  [the longest x8 14.9 us: swapped(): return lax.ppermute(value, axis, [(i, i ^ bit) for i in range(count)])]
    all_to_all x0 -> x1, waiting for transfers between devices: none -> 15.8 us  [messages_direct(): return lax.all_to_all(message, ('sq', 'fsdp'), 0, 0, tiled=True)]
    while x20 -> x0, local copies, waits for them, and re-layouts: 13 us -> none
    dynamic_slice x14 -> x0, local copies, waits for them, and re-layouts: 11.4 us -> none  [one(): lax.dynamic_index_in_dim(a, hop, 0, False)]
  transfers between devices with their start and end apart: 4 -> 11, of which waited for: 4 -> 9; matrix products, arithmetic and copies ran while one was open for 1% -> 1% of each run, Pallas kernels for 0% -> 0%
where the time goes in v1:
time: 111 us; the launch traced here: 109 us
  waiting for transfers between devices  42.9 us (39%)
  Pallas kernels  42.1 us (38%)
  starting transfers between devices  17.2 us (15%)
  local copies, waits for them, and re-layouts  6.44 us (6%)
    pallas_call x1, Pallas kernels, prepare(): pl.pallas_call(lambda *refs: prepare_kernel(seg_product, *refs), grid_spe...  28 us
    all_to_all x1, waiting for transfers between devices, messages_direct(): return lax.all_to_all(message, ('sq', 'fsdp'), 0, 0, tiled=True)  15.8 us
    ppermute x8, waiting for transfers between devices, swapped(): return lax.ppermute(value, axis, [(i, i ^ bit) for i in range(count)])  14.9 us
    ppermute x2, waiting for transfers between devices, shifted(): return lax.ppermute(value, axes, pairs)  12.2 us
    ppermute x8, starting transfers between devices, swapped(): return lax.ppermute(value, axis, [(i, i ^ bit) for i in range(count)])  8.87 us
    pallas_call x1, Pallas kernels, project(): pl.pallas_call(project_kernel, grid_spec=grid_spec, out_shape=jax.ShapeDt...  7.25 us
    all_to_all x1, starting transfers between devices, messages_direct(): return lax.all_to_all(message, ('sq', 'fsdp'), 0, 0, tiled=True)  5.79 us
    pallas_call x1, Pallas kernels, read(): pl.pallas_call(read_kernel, grid_spec=grid_spec, out_shape=jax.ShapeDtype...  4.85 us
  transfers between devices with their start and end apart: 11, of which 9 were waited for; matrix products, arithmetic and copies ran while one was open for 1% of the time, Pallas kernels for 0%

profile of v1, /device:TPU:29, one launch (start us, length us, event | category | flops | bytes accessed | tf_op | source)
XLA Modules:
  0.0 109.4 jit_solution(13080367536261665650)
XLA Ops:
  0.0 0.9 slice_bitcast_fusion.4
  0.9 1.3 %collective-permute-start.3 = (bf16[16,2048]{1,0:T(8,128)(2,1)S(1)}, bf16[16,2048]{1,0:T(8,128)(2,1)S(1)}, u32[]{:S(2)}, u32[]{:S(2)}) collective-permute-start(bf16[16,2048]{1,0:T(8,128)(2,1)S(1)} %slice_bitcast_fusion.4), channel_id=1, source_target_pairs={{0,4},{4,8},{8,12},{12,16},{16,20},{20,24},{24,28},{1,5},{5,9},{9,... | collective-permute-start | bytes 196616 | tf_op jit(solution)/shard_map/ppermute | solution.py:27
  2.2 1.3 %collective-permute-start.1 = (bf16[128,2048]{1,0:T(8,128)(2,1)}, bf16[128,2048]{1,0:T(8,128)(2,1)S(1)}, u32[]{:S(2)}, u32[]{:S(2)}) collective-permute-start(bf16[128,2048]{1,0:T(8,128)(2,1)} %bitcast.18), channel_id=1, source_target_pairs={{0,2},{1,3},{2,0},{3,1},{4,6},{5,7},{6,4},{7,5},{8,10},{9,11},{10,... | collective-permute-start | bytes 1572872 | tf_op jit(solution)/shard_map/ppermute | solution.py:32
  3.4 2.4 %collective-permute-done.3 = bf16[16,2048]{1,0:T(8,128)(2,1)S(1)} collective-permute-done((bf16[16,2048]{1,0:T(8,128)(2,1)S(1)}, bf16[16,2048]{1,0:T(8,128)(2,1)S(1)}, u32[]{:S(2)}, u32[]{:S(2)}) %collective-permute-start.3) | collective-permute-done | bytes 65568 | tf_op jit(solution)/shard_map/ppermute | solution.py:27
  5.9 1.2 %collective-permute-start.4 = (bf16[16,2048]{1,0:T(8,128)(2,1)S(1)}, bf16[16,2048]{1,0:T(8,128)(2,1)S(1)}, u32[]{:S(2)}, u32[]{:S(2)}) collective-permute-start(bf16[16,2048]{1,0:T(8,128)(2,1)S(1)} %collective-permute-done.3), channel_id=1, source_target_pairs={{0,2},{1,3},{2,0},{3,1},{4,6},{5,7},{6,4},{7,5},{8,10},{9,11},{10,... | collective-permute-start | bytes 196616 | tf_op jit(solution)/shard_map/ppermute | solution.py:32
  7.1 2.1 %collective-permute-start = (bf16[128,2048]{1,0:T(8,128)(2,1)}, bf16[128,2048]{1,0:T(8,128)(2,1)S(1)}, u32[]{:S(2)}, u32[]{:S(2)}) collective-permute-start(bf16[128,2048]{1,0:T(8,128)(2,1)} %bitcast.19), channel_id=1, source_target_pairs={{0,1},{1,0},{2,3},{3,2},{4,5},{5,4},{6,7},{7,6},{8,9},{9,8},{10,11... | collective-permute-start | bytes 1572872 | tf_op jit(solution)/shard_map/ppermute | solution.py:32
  9.2 7.5 %collective-permute-done.4 = bf16[16,2048]{1,0:T(8,128)(2,1)S(1)} collective-permute-done((bf16[16,2048]{1,0:T(8,128)(2,1)S(1)}, bf16[16,2048]{1,0:T(8,128)(2,1)S(1)}, u32[]{:S(2)}, u32[]{:S(2)}) %collective-permute-start.4) | collective-permute-done | bytes 65568 | tf_op jit(solution)/shard_map/ppermute | solution.py:32
  16.7 1.6 %collective-permute-start.5 = (bf16[32,2048]{1,0:T(8,128)(2,1)S(1)}, bf16[32,2048]{1,0:T(8,128)(2,1)S(1)}, u32[]{:S(2)}, u32[]{:S(2)}) collective-permute-start(bf16[32,2048]{1,0:T(8,128)(2,1)S(1)} %pad_maximum_fusion.1), channel_id=1, source_target_pairs={{0,1},{1,0},{2,3},{3,2},{4,5},{5,4},{6,7},{7,6},{8,9},{9,8},{10,11... | collective-permute-start | bytes 393224 | tf_op jit(solution)/shard_map/ppermute | solution.py:32
  19.3 0.7 pad_maximum_fusion.rims
  20.0 0.8 collective-permute-done.2.x3
  20.8 0.8 copy-done.4
  21.6 7.3 %project.1 = bf16[4,4,144,256]{3,2,1,0:T(8,128)(2,1)} custom-call(s32[1]{0:T(128)} %bitcast.1.place, bf16[128,2048]{1,0:T(8,128)(2,1)} %bitcast.20, bf16[128,2048]{1,0:T(8,128)(2,1)} %copy-done.3, bf16[128,2048]{1,0:T(8,128)(2,1)} %copy-done.2, bf16[128,2048]{1,0:T(8,128)(2,1)} %copy-done.4, bf16[64,2048]{1,0:T(8,128)(2,1)} %pad_maximum_fusion.rims, ...), custom_call_target="tpu_custom_call" | custom-call | tf_op jit(solution)/shard_map/project/pallas_call | solution.py:108
  28.8 5.8 %all-to-all-start = ((bf16[16,144,256]{2,1,0:T(8,128)(2,1)}), bf16[16,144,256]{2,1,0:T(8,128)(2,1)S(1)}, u32[]{:S(2)}, u32[]{:S(2)}) async-start(bf16[16,144,256]{2,1,0:T(8,128)(2,1)} %bitcast.17), calls=%async_computation | async-start | bytes 2359296 | tf_op jit(solution)/shard_map/all_to_all | solution.py:369
  34.6 15.8 %all-to-all-done.refs_3_ = bf16[16,144,256]{2,1,0:T(8,128)(2,1)S(1)} async-done(((bf16[16,144,256]{2,1,0:T(8,128)(2,1)}), bf16[16,144,256]{2,1,0:T(8,128)(2,1)S(1)}, u32[]{:S(2)}, u32[]{:S(2)}) %all-to-all-start) | async-done | bytes 1179680 | tf_op jit(solution)/shard_map/all_to_all | solution.py:369
  50.4 1.1 copy-done.1
  51.5 28.0 %prepare.1 = (f32[4,4,256,128]{3,2,1,0:T(8,128)}, f32[4,4,256,128]{3,2,1,0:T(8,128)}, bf16[4,128,128]{2,1,0:T(8,128)(2,1)}) custom-call(s32[1]{0:T(128)} %bitcast.refs_0_.place, f32[16]{0:T(128)} %refs_1_.1, f32[16]{0:T(128)} %refs_2_.1, bf16[16,144,256]{2,1,0:T(8,128)(2,1)} %copy-done.1, bf16[4,4096]{1,0:T(4,128)(2,1)} %refs_4_.1), custom_call_target="tpu_custom_call" | custom-call | tf_op jit(solution)/shard_map/prepare/pallas_call | solution.py:286
  79.5 1.3 %collective-permute-start.6 = (bf16[4,128,128]{2,1,0:T(8,128)(2,1)}, bf16[4,128,128]{2,1,0:T(8,128)(2,1)S(1)}, u32[]{:S(2)}, u32[]{:S(2)}) collective-permute-start(bf16[4,128,128]{2,1,0:T(8,128)(2,1)} %get-tuple-element.10), channel_id=1, source_target_pairs={{0,16},{1,17},{2,18},{3,19},{4,20},{5,21},{6,22},{7,23},{8,24},{9,... | collective-permute-start | bytes 393224 | tf_op jit(solution)/shard_map/ppermute | solution.py:27
  80.8 9.7 %collective-permute-done.6.start = bf16[4,128,128]{2,1,0:T(8,128)(2,1)S(1)} collective-permute-done((bf16[4,128,128]{2,1,0:T(8,128)(2,1)}, bf16[4,128,128]{2,1,0:T(8,128)(2,1)S(1)}, u32[]{:S(2)}, u32[]{:S(2)}) %collective-permute-start.6) | collective-permute-done | bytes 131104 | tf_op jit(solution)/shard_map/ppermute | solution.py:27
  91.2 4.9 %read.1 = bf16[4,128,512]{2,1,0:T(8,128)(2,1)} custom-call(s32[1]{0:T(128)} %bitcast.refs_0_.place, f32[4,4,256,128]{3,2,1,0:T(8,128)} %get-tuple-element.8.carry, f32[4,4,256,128]{3,2,1,0:T(8,128)} %get-tuple-element.9.add, bf16[4,128,128]{2,1,0:T(8,128)(2,1)} %copy-done.8, f32[1,128]{1,0:T(1,128)} %bitcast.21), custom_call_target="tpu_custom_call" | custom-call | tf_op jit(solution)/shard_map/read/pallas_call | solution.py:324
  96.0 1.8 %slice_bitcast_fusion = (bf16[128,512]{1,0:T(8,128)(2,1)S(1)}, bf16[128,512]{1,0:T(8,128)(2,1)S(1)}, bf16[128,512]{1,0:T(8,128)(2,1)S(1)}, bf16[128,512]{1,0:T(8,128)(2,1)}) fusion(bf16[4,128,512]{2,1,0:T(8,128)(2,1)} %read.1), kind=kLoop, calls=%fused_computation.1 | loop fusion | bytes 1048576 | tf_op jit(solution)/shard_map/squeeze | solution.py:419
  98.4 2.0 %collective-permute-start.7 = (bf16[128,512]{1,0:T(8,128)(2,1)S(1)}, bf16[128,512]{1,0:T(8,128)(2,1)S(1)}, u32[]{:S(2)}, u32[]{:S(2)}) collective-permute-start(bf16[128,512]{1,0:T(8,128)(2,1)S(1)} %get-tuple-element.13), channel_id=1, source_target_pairs={{0,4},{4,0},{8,12},{12,8},{1,5},{5,1},{9,13},{13,9},{2,6},{6,2},{1... | collective-permute-start | bytes 393224 | tf_op jit(solution)/shard_map/ppermute | solution.py:32
  100.5 2.6 %collective-permute-done.9.refs_3_ = bf16[128,512]{1,0:T(8,128)(2,1)S(1)} collective-permute-done((bf16[128,512]{1,0:T(8,128)(2,1)S(1)}, bf16[128,512]{1,0:T(8,128)(2,1)S(1)}, u32[]{:S(2)}, u32[]{:S(2)}) %collective-permute-start.9) | collective-permute-done | bytes 131104 | tf_op jit(solution)/shard_map/ppermute | solution.py:32
  103.4 3.4 %collective-permute-done.7.refs_1_ = bf16[128,512]{1,0:T(8,128)(2,1)S(1)} collective-permute-done((bf16[128,512]{1,0:T(8,128)(2,1)S(1)}, bf16[128,512]{1,0:T(8,128)(2,1)S(1)}, u32[]{:S(2)}, u32[]{:S(2)}) %collective-permute-start.7) | collective-permute-done | bytes 131104 | tf_op jit(solution)/shard_map/ppermute | solution.py:32
  107.5 2.0 %assemble.1 = bf16[1,128,2048]{2,1,0:T(8,128)(2,1)} custom-call(s32[1]{0:T(128)} %bitcast.refs_0_.place, bf16[128,512]{1,0:T(8,128)(2,1)} %get-tuple-element.14.refs_0_, bf16[128,512]{1,0:T(8,128)(2,1)} %copy-done.7, bf16[128,512]{1,0:T(8,128)(2,1)} %copy-done.6, bf16[128,512]{1,0:T(8,128)(2,1)} %copy-done.5), custom_call_target="tpu_custom_call" | custom-call | tf_op jit(solution)/shard_map/assemble/pallas_call | solution.py:344
  (26 shorter events, 3.3 us)
Async XLA Ops:
  0.0 18.3 %copy-start = (bf16[2048,32]{0,1:T(8,128)(2,1)S(1)}, bf16[2048,32]{0,1:T(8,128)(2,1)}, u32[]{:S(2)}) copy-start(bf16[2048,32]{0,1:T(8,128)(2,1)} %param.9) | copy-start | bytes 393220
  0.9 5.0 %collective-permute-start.3 = (bf16[16,2048]{1,0:T(8,128)(2,1)S(1)}, bf16[16,2048]{1,0:T(8,128)(2,1)S(1)}, u32[]{:S(2)}, u32[]{:S(2)}) collective-permute-start(bf16[16,2048]{1,0:T(8,128)(2,1)S(1)} %slice_bitcast_fusion.4), channel_id=1, source_target_pairs={{0,4},{4,8},{8,12},{12,16},{16,20},{20,24},{24,28},{1,5},{5,9},{9,... | collective-permute-start | bytes 196616 | tf_op jit(solution)/shard_map/ppermute | solution.py:27
  2.2 16.7 %collective-permute-start.1 = (bf16[128,2048]{1,0:T(8,128)(2,1)}, bf16[128,2048]{1,0:T(8,128)(2,1)S(1)}, u32[]{:S(2)}, u32[]{:S(2)}) collective-permute-start(bf16[128,2048]{1,0:T(8,128)(2,1)} %bitcast.18), channel_id=1, source_target_pairs={{0,2},{1,3},{2,0},{3,1},{4,6},{5,7},{6,4},{7,5},{8,10},{9,11},{10,... | collective-permute-start | bytes 1572872 | tf_op jit(solution)/shard_map/ppermute | solution.py:32
  5.9 10.8 %collective-permute-start.4 = (bf16[16,2048]{1,0:T(8,128)(2,1)S(1)}, bf16[16,2048]{1,0:T(8,128)(2,1)S(1)}, u32[]{:S(2)}, u32[]{:S(2)}) collective-permute-start(bf16[16,2048]{1,0:T(8,128)(2,1)S(1)} %collective-permute-done.3), channel_id=1, source_target_pairs={{0,2},{1,3},{2,0},{3,1},{4,6},{5,7},{6,4},{7,5},{8,10},{9,11},{10,... | collective-permute-start | bytes 196616 | tf_op jit(solution)/shard_map/ppermute | solution.py:32
  7.1 12.9 %collective-permute-start = (bf16[128,2048]{1,0:T(8,128)(2,1)}, bf16[128,2048]{1,0:T(8,128)(2,1)S(1)}, u32[]{:S(2)}, u32[]{:S(2)}) collective-permute-start(bf16[128,2048]{1,0:T(8,128)(2,1)} %bitcast.19), channel_id=1, source_target_pairs={{0,1},{1,0},{2,3},{3,2},{4,5},{5,4},{6,7},{7,6},{8,9},{9,8},{10,11... | collective-permute-start | bytes 1572872 | tf_op jit(solution)/shard_map/ppermute | solution.py:32
  16.7 2.6 %collective-permute-start.5 = (bf16[32,2048]{1,0:T(8,128)(2,1)S(1)}, bf16[32,2048]{1,0:T(8,128)(2,1)S(1)}, u32[]{:S(2)}, u32[]{:S(2)}) collective-permute-start(bf16[32,2048]{1,0:T(8,128)(2,1)S(1)} %pad_maximum_fusion.1), channel_id=1, source_target_pairs={{0,1},{1,0},{2,3},{3,2},{4,5},{5,4},{6,7},{7,6},{8,9},{9,8},{10,11... | collective-permute-start | bytes 393224 | tf_op jit(solution)/shard_map/ppermute | solution.py:32
  18.9 1.9 %copy-start.2 = (bf16[128,2048]{1,0:T(8,128)(2,1)}, bf16[128,2048]{1,0:T(8,128)(2,1)S(1)}, u32[]{:S(2)}) copy-start(bf16[128,2048]{1,0:T(8,128)(2,1)S(1)} %collective-permute-done.1.x2) | copy-start | bytes 1572868
  18.9 1.9 %collective-permute-start.2 = (bf16[128,2048]{1,0:T(8,128)(2,1)S(1)}, bf16[128,2048]{1,0:T(8,128)(2,1)S(1)}, u32[]{:S(2)}, u32[]{:S(2)}) collective-permute-start(bf16[128,2048]{1,0:T(8,128)(2,1)S(1)} %collective-permute-done.1.x2), channel_id=1, source_target_pairs={{0,1},{1,0},{2,3},{3,2},{4,5},{5,4},{6,7},{7,6},{8,9},{9,8},{10,11... | collective-permute-start | bytes 1572872 | tf_op jit(solution)/shard_map/ppermute | solution.py:32
  20.0 0.8 copy-start.3
  20.8 0.8 copy-start.4
  28.8 21.6 %all-to-all-start = ((bf16[16,144,256]{2,1,0:T(8,128)(2,1)}), bf16[16,144,256]{2,1,0:T(8,128)(2,1)S(1)}, u32[]{:S(2)}, u32[]{:S(2)}) async-start(bf16[16,144,256]{2,1,0:T(8,128)(2,1)} %bitcast.17), calls=%async_computation | async-start | bytes 2359296 | tf_op jit(solution)/shard_map/all_to_all | solution.py:369
  50.4 1.1 copy-start.1
  79.5 11.0 %collective-permute-start.6 = (bf16[4,128,128]{2,1,0:T(8,128)(2,1)}, bf16[4,128,128]{2,1,0:T(8,128)(2,1)S(1)}, u32[]{:S(2)}, u32[]{:S(2)}) collective-permute-start(bf16[4,128,128]{2,1,0:T(8,128)(2,1)} %get-tuple-element.10), channel_id=1, source_target_pairs={{0,16},{1,17},{2,18},{3,19},{4,20},{5,21},{6,22},{7,23},{8,24},{9,... | collective-permute-start | bytes 393224 | tf_op jit(solution)/shard_map/ppermute | solution.py:27
  90.5 0.7 copy-start.8
  97.8 5.3 %collective-permute-start.9 = (bf16[128,512]{1,0:T(8,128)(2,1)S(1)}, bf16[128,512]{1,0:T(8,128)(2,1)S(1)}, u32[]{:S(2)}, u32[]{:S(2)}) collective-permute-start(bf16[128,512]{1,0:T(8,128)(2,1)S(1)} %get-tuple-element.11), channel_id=1, source_target_pairs={{0,12},{4,8},{8,4},{12,0},{1,13},{5,9},{9,5},{13,1},{2,14},{6,10},... | collective-permute-start | bytes 393224 | tf_op jit(solution)/shard_map/ppermute | solution.py:32
  97.8 5.6 %collective-permute-start.8 = (bf16[128,512]{1,0:T(8,128)(2,1)S(1)}, bf16[128,512]{1,0:T(8,128)(2,1)S(1)}, u32[]{:S(2)}, u32[]{:S(2)}) collective-permute-start(bf16[128,512]{1,0:T(8,128)(2,1)S(1)} %get-tuple-element.12), channel_id=1, source_target_pairs={{0,8},{4,12},{8,0},{12,4},{1,9},{5,13},{9,1},{13,5},{2,10},{6,14},... | collective-permute-start | bytes 393224 | tf_op jit(solution)/shard_map/ppermute | solution.py:32
  98.4 8.4 %collective-permute-start.7 = (bf16[128,512]{1,0:T(8,128)(2,1)S(1)}, bf16[128,512]{1,0:T(8,128)(2,1)S(1)}, u32[]{:S(2)}, u32[]{:S(2)}) collective-permute-start(bf16[128,512]{1,0:T(8,128)(2,1)S(1)} %get-tuple-element.13), channel_id=1, source_target_pairs={{0,4},{4,0},{8,12},{12,8},{1,5},{5,1},{9,13},{13,9},{2,6},{6,2},{1... | collective-permute-start | bytes 393224 | tf_op jit(solution)/shard_map/ppermute | solution.py:32
  103.1 3.7 %copy-start.5 = (bf16[128,512]{1,0:T(8,128)(2,1)}, bf16[128,512]{1,0:T(8,128)(2,1)S(1)}, u32[]{:S(2)}) copy-start(bf16[128,512]{1,0:T(8,128)(2,1)S(1)} %collective-permute-done.9.refs_3_) | copy-start | bytes 393220
  103.4 3.4 %copy-start.6 = (bf16[128,512]{1,0:T(8,128)(2,1)}, bf16[128,512]{1,0:T(8,128)(2,1)S(1)}, u32[]{:S(2)}) copy-start(bf16[128,512]{1,0:T(8,128)(2,1)S(1)} %collective-permute-done.8.refs_2_) | copy-start | bytes 393220
  106.8 0.7 copy-start.7

commit v2 on v1

--- a/solution.py
+++ b/solution.py
@@ -1,11 +1,11 @@
 import jax
 import jax.numpy as jnp
-import numpy as np
 from jax import lax
 from jax.experimental import pallas as pl
 from jax.experimental.pallas import tpu as pltpu
 from jax.sharding import Mesh
 from jax.sharding import PartitionSpec as P
+
 
 HEAD = 128
 HK = 8
@@ -14,7 +14,9 @@
 PAIR = 2
 SPLIT = HK // PAIR
 CHUNK = 128
-BASE = 32
+BASE = 16
+PROJECT_VMEM = 24 << 20
+VMEM_LIMIT = 67_043_328
 EXTRA = 16
 RIM = 8
 UNITS = HV // SPLIT
@@ -42,7 +44,10 @@
 
 
 def dot3(a, b):
-    return dot(a[0], b[0]) + (dot(a[0], b[1]) + dot(a[1], b[0]))
+    right = jnp.concatenate([jnp.concatenate(b, axis=1), jnp.concatenate([b[0], jnp.zeros_like(b[0])], axis=1)], axis=0)
+    both = dot(jnp.concatenate(a, axis=1), right)
+    width = b[0].shape[1]
+    return both[:, :width] + both[:, width:]
 
 
 def split3(a):
@@ -56,98 +61,125 @@
     return lax.broadcasted_iota(jnp.int32, shape, dim)
 
 
-def project_kernel(place, x0, x1, x2, x3, rims, gate_t, w_a, w_b, out, lhs, gates):
-    step = pl.program_id(0)
+def project_kernel(other, place, x0, x1, rim_0, rim_1, gate_t, weight, *rest):
+    out, lhs, stage, sems = rest[-4:]
     rows = x0.shape[0]
     me = place[0]
-
-    @pl.when(step == 0)
-    def _():
-        for k, x in enumerate((x0, x1, x2, x3)):
-            lhs[k * rows : (k + 1) * rows, :] = x[...]
-        lhs[4 * rows :, :] = rims[...]
-        raw = lax.dot_general(
-            gate_t[...], lhs[: 4 * rows, :], (((1,), (1,)), ((), ())), preferred_element_type=F32
-        )
-        for part, value in enumerate(split3(raw)):
-            for j in range(SPLIT):
-                for k in range(4):
-                    both = value[2 * j : 2 * j + 2, k * rows : (k + 1) * rows]
-                    gates[j, k, part : part + 1, :] = jnp.concatenate([both[0:1], both[1:2]], axis=1)
-
-    weights = jnp.concatenate([w_a[...], w_b[...]], axis=1)
-    mixed = dot(lhs[...], weights)
-    for k in range(4):
-        target = jnp.bitwise_xor(me, k)
-        out[0, target, :rows, :] = mixed[k * rows : (k + 1) * rows].astype(BF16)
-        before = mixed[4 * rows + k * EXTRA : 4 * rows + (k + 1) * EXTRA]
-        before = jnp.where(iota(before.shape, 0) < 3, gates[step, k], before)
-        out[0, target, rows:, :] = before.astype(BF16)
-
-
-def project(place, xs, rims, gate_t, weight):
+    pair = 1 - me // 2 if other else me // 2
+    contiguous = me >= 2
+
+    lhs[:rows, :] = x0[...]
+    lhs[rows : 2 * rows, :] = x1[...]
+    lhs[2 * rows :, :] = jnp.concatenate([rim_0[...], rim_1[...]], axis=0)
+    raw = lax.dot_general(
+        gate_t[...], lhs[: 2 * rows, :], (((1,), (1,)), ((), ())), preferred_element_type=F32
+    )
+    parts = split3(raw)
+    blank = jnp.zeros((EXTRA - RIM - 3, 2 * HEAD), F32)
+    copies = []
+    for j in range(SPLIT):
+        lanes = [
+            pl.multiple_of(jnp.where(contiguous, 2 * j + a, SPLIT * a + j) * HEAD, HEAD)
+            for a in range(2)
+        ]
+        columns = jnp.concatenate([weight[:, pl.ds(lane, HEAD)] for lane in lanes], axis=1)
+        mixed = dot(lhs[...], columns)
+        for k in range(2):
+            target = jnp.bitwise_xor(me % 2, k)
+            stage[j, target, :rows, :] = mixed[k * rows : (k + 1) * rows].astype(BF16)
+            tokens = slice(k * rows, (k + 1) * rows)
+            gate = [
+                jnp.concatenate([p[2 * j : 2 * j + 1, tokens], p[2 * j + 1 : 2 * j + 2, tokens]], 1)
+                for p in parts
+            ]
+            before = mixed[2 * rows + k * RIM : 2 * rows + (k + 1) * RIM]
+            stage[j, target, rows:, :] = jnp.concatenate(gate + [blank, before], axis=0).astype(BF16)
+        copy = pltpu.make_async_copy(stage.at[j], out.at[j, pl.ds(2 * pair, 2)], sems.at[j])
+        copy.start()
+        copies.append(copy)
+    for copy in copies:
+        copy.wait()
+
+
+def project(place, xs, rims, gate_t, weight, other, message):
     rows, depth = xs[0].shape
-    width = 2 * HEAD
-    whole = lambda shape: pl.BlockSpec(shape, lambda j, s: (0,) * len(shape))
-    grid_spec = pltpu.PrefetchScalarGridSpec(
-        num_scalar_prefetch=1,
-        grid=(SPLIT,),
-        in_specs=[whole((rows, depth))] * 4
-        + [
-            whole(rims.shape),
-            whole(gate_t.shape),
-            pl.BlockSpec((depth, HEAD), lambda j, s: (0, jnp.where(s[0] < 2, j, 2 * j))),
-            pl.BlockSpec((depth, HEAD), lambda j, s: (0, jnp.where(s[0] < 2, SPLIT + j, 2 * j + 1))),
+    width = weight.shape[1]
+    operands = [place, *xs, *rims, gate_t, weight]
+    in_specs = [pl.BlockSpec(memory_space=pltpu.SMEM)]
+    in_specs += [pl.BlockSpec(memory_space=pltpu.VMEM)] * (len(operands) - 1)
+    aliases = {}
+    if message is not None:
+        aliases = {len(operands): 0}
+        operands.append(message)
+        in_specs.append(pl.BlockSpec(memory_space=pl.ANY))
+    block = (SPLIT, 2, rows + EXTRA, 2 * HEAD)
+    return pl.pallas_call(
+        lambda *refs: project_kernel(other, *refs),
+        in_specs=in_specs,
+        out_specs=pl.BlockSpec(memory_space=pl.ANY),
+        out_shape=jax.ShapeDtypeStruct((SPLIT, 4, rows + EXTRA, 2 * HEAD), BF16),
+        scratch_shapes=[
+            pltpu.VMEM((2 * rows + 2 * RIM, depth), BF16),
+            pltpu.VMEM(block, BF16),
+            pltpu.SemaphoreType.DMA((SPLIT,)),
         ],
-        out_specs=pl.BlockSpec((1, 4, rows + EXTRA, width), lambda j, s: (j, 0, 0, 0)),
-        scratch_shapes=[
-            pltpu.VMEM((4 * rows + 4 * EXTRA, depth), BF16),
-            pltpu.VMEM((SPLIT, 4, EXTRA, width), F32),
-        ],
-    )
-    return pl.pallas_call(
-        project_kernel,
-        grid_spec=grid_spec,
-        out_shape=jax.ShapeDtypeStruct((SPLIT, 4, rows + EXTRA, width), BF16),
-        name="project",
-    )(place, *xs, rims, gate_t, weight, weight)
-
-
-def base_inverse(lower):
+        input_output_aliases=aliases,
+        cost_estimate=pl.CostEstimate(
+            flops=4 * rows * depth * width,
+            bytes_accessed=2 * weight.size + 8 * xs[0].size,
+            transcendentals=0,
+        ),
+        compiler_params=pltpu.CompilerParams(vmem_limit_bytes=PROJECT_VMEM),
+        name="project_other" if other else "project_own",
+    )(*operands)
+
+
+def base_inverses(lowers):
     count = CHUNK // BASE
     tiles = BASE // 8
     lane_block = iota((8, CHUNK), 1) // BASE
-    packed, result = [], []
-    for t in range(tiles):
-        tile = jnp.zeros((8, CHUNK), F32)
-        for b in range(count):
-            start = b * BASE + 8 * t
-            tile = jnp.where(lane_block == b, lower[start : start + 8], tile)
-        packed.append(tile)
-        inside = iota((8, CHUNK), 1) % BASE
-        result.append(jnp.where(inside == iota((8, CHUNK), 0) + 8 * t, 1.0, 0.0))
+    inside = iota((8, CHUNK), 1) % BASE
+    packed, results = [], []
+    for lower in lowers:
+        pack, result = [], []
+        for t in range(tiles):
+            tile = jnp.zeros((8, CHUNK), F32)
+            for b in range(count):
+                start = b * BASE + 8 * t
+                tile = jnp.where(lane_block == b, lower[start : start + 8], tile)
+            pack.append(tile)
+            result.append(jnp.where(inside == iota((8, CHUNK), 0) + 8 * t, 1.0, 0.0))
+        packed.append(pack)
+        results.append(result)
     for j in range(BASE - 1):
-        row = jnp.broadcast_to(result[j // 8][j % 8 : j % 8 + 1], (8, CHUNK))
         source = lane_block * BASE + j
-        for t in range((j + 1) // 8, tiles):
-            column = jnp.take_along_axis(packed[t], source, axis=1)
-            result[t] = result[t] - column * row
-    side = jnp.concatenate(result, axis=0)
+        for pack, result in zip(packed, results):
+            row = jnp.broadcast_to(result[j // 8][j % 8 : j % 8 + 1], (8, CHUNK))
+            for t in range((j + 1) // 8, tiles):
+                column = jnp.take_along_axis(pack[t], source, axis=1)
+                result[t] = result[t] - column * row
     block = iota((BASE, CHUNK), 1) // BASE
-    return jnp.concatenate([jnp.where(block == b, side, 0.0) for b in range(count)], axis=0)
-
-
-def inverse(lower):
-    total = base_inverse(lower)
+    totals = []
+    for result in results:
+        side = jnp.concatenate(result, axis=0)
+        totals.append(
+            jnp.concatenate([jnp.where(block == b, side, 0.0) for b in range(count)], axis=0)
+        )
+    return totals
+
+
+def inverses(lowers):
+    totals = base_inverses(lowers)
     row, column = iota((CHUNK, CHUNK), 0), iota((CHUNK, CHUNK), 1)
     size = BASE
     while size < CHUNK:
         inside = (row // (2 * size) == column // (2 * size)) & (row // size > column // size)
-        corner = halves(jnp.where(inside, lower, 0.0))
-        parts = halves(total)
-        total = total - dot3(parts, halves(dot3(corner, parts)))
+        parts = [halves(total) for total in totals]
+        corners = [halves(jnp.where(inside, lower, 0.0)) for lower in lowers]
+        inner = [halves(dot3(c, p)) for c, p in zip(corners, parts)]
+        totals = [t - dot3(p, i) for t, p, i in zip(totals, parts, inner)]
         size *= 2
-    return total
+    return totals
 
 
 def prepare_kernel(seg_product, place, rate, bias, message, taps, carry_out, add_out, final, *rest):
@@ -212,41 +244,48 @@
         lower_eye, table, (((1,), (1,)), ((), ())), precision=HIGHEST, preferred_element_type=F32
     )
 
-    for h in range(PAIR):
-        head = SPLIT * h + j
-        query = unit(activated(0, h, head)) * HEAD ** (-0.5)
-        key = unit(activated(1, h, HK + head))
-        key_t = key.T
-        key_t_parts = halves(key_t)
-        both = halves(jnp.concatenate([key, query], axis=0))
-        scores = dot3(both, key_t_parts)
-        key_key, query_key = scores[:rows], scores[rows:]
-        for a in range(2):
-            u = 2 * h + a
-            value = activated(2 + h, a, 2 * HK + 2 * head + a)
-            cum_c = columns[:rows, u : u + 1]
-            strength = columns[rows:, UNITS + u : UNITS + u + 1]
-            cum_r = cum_rows[u : u + 1]
-            last = cum_rows[u : u + 1, rows - 1 : rows]
-            ratio = jnp.exp(jnp.minimum(cum_c - cum_r, 0.0))
-            growth = jnp.exp(cum_c)
-            trailing = jnp.exp(jnp.minimum(last - cum_r, 0.0))
-            lower = jnp.where(strict, strength * ratio * key_key, 0.0)
-            mixing = jnp.where(within, ratio * query_key, 0.0)
-            solve = inverse(lower)
-            scaled = jnp.concatenate([(strength * growth) * key, strength * value], axis=1)
-            weighted = dot3(halves(solve), halves(scaled))
-            left = jnp.concatenate([trailing * key_t, mixing], axis=0)
-            mixed = dot3(halves(left), halves(weighted))
-            carry = jnp.exp(last) * eye - mixed[:rows, :HEAD]
-            read = growth * query - mixed[rows:, :HEAD]
-            carry_out[0, u, :rows] = carry
-            carry_out[0, u, rows:] = read
-            add_out[0, u] = mixed[:, HEAD:]
-            carry_parts = halves(carry)
-            state[u] = dot3(carry_parts, halves(state[u])) + mixed[:rows, HEAD:]
-            if seg_product:
-                product[u] = dot3(carry_parts, halves(product[u]))
+    heads = [SPLIT * h + j for h in range(PAIR)]
+    queries = [unit(activated(0, h, heads[h])) * HEAD ** (-0.5) for h in range(PAIR)]
+    keys = [unit(activated(1, h, HK + heads[h])) for h in range(PAIR)]
+    keys_t = [key.T for key in keys]
+    scores = [
+        dot3(halves(jnp.concatenate([keys[h], queries[h]], axis=0)), halves(keys_t[h]))
+        for h in range(PAIR)
+    ]
+    growths, strengths, lasts, lowers, mixings = [], [], [], [], []
+    for u in range(UNITS):
+        cum_c = columns[:rows, u : u + 1]
+        strength = columns[rows:, UNITS + u : UNITS + u + 1]
+        cum_r = cum_rows[u : u + 1]
+        ratio = jnp.exp(jnp.minimum(cum_c - cum_r, 0.0))
+        growths.append(jnp.exp(cum_c))
+        strengths.append(strength)
+        lasts.append(cum_rows[u : u + 1, rows - 1 : rows])
+        lowers.append(jnp.where(strict, strength * ratio * scores[u // 2][:rows], 0.0))
+        mixings.append(jnp.where(within, ratio * scores[u // 2][rows:], 0.0))
+    solves = inverses(lowers)
+    weighted = []
+    for u in range(UNITS):
+        h, a = u // 2, u % 2
+        value = activated(2 + h, a, 2 * HK + 2 * heads[h] + a)
+        scaled = jnp.concatenate(
+            [(strengths[u] * growths[u]) * keys[h], strengths[u] * value], axis=1
+        )
+        weighted.append(halves(dot3(halves(solves[u]), halves(scaled))))
+    mixed = []
+    for u in range(UNITS):
+        trailing = jnp.exp(jnp.minimum(lasts[u] - cum_rows[u : u + 1], 0.0))
+        left = jnp.concatenate([trailing * keys_t[u // 2], mixings[u]], axis=0)
+        mixed.append(dot3(halves(left), weighted[u]))
+    for u in range(UNITS):
+        carry = jnp.exp(lasts[u]) * eye - mixed[u][:rows, :HEAD]
+        carry_out[0, u, :rows] = carry
+        carry_out[0, u, rows:] = growths[u] * queries[u // 2] - mixed[u][rows:, :HEAD]
+        add_out[0, u] = mixed[u][:, HEAD:]
+        carry_parts = halves(carry)
+        state[u] = dot3(carry_parts, halves(state[u])) + mixed[u][:rows, HEAD:]
+        if seg_product:
+            product[u] = dot3(carry_parts, halves(product[u]))
 
     @pl.when(step == pl.num_programs(0) - 1)
     def _():
@@ -287,11 +326,14 @@
         lambda *refs: prepare_kernel(seg_product, *refs),
         grid_spec=grid_spec,
         out_shape=out_shape,
+        compiler_params=pltpu.CompilerParams(vmem_limit_bytes=VMEM_LIMIT),
         name="prepare",
     )(place, rate, bias, message, taps)
 
 
-def read_kernel(place, carry, add, start, gain, out, state):
+def read_kernel(place, carry, add, start, gain, *rest):
+    outs, result, state = rest[:-2], rest[-2], rest[-1]
+
     @pl.when(pl.program_id(0) == 0)
     def _():
         state[...] = start[...].astype(F32)
@@ -302,9 +344,15 @@
         state[u] = both[:rows]
         reads = both[rows:]
         mean = jnp.mean(reads * reads, axis=-1, keepdims=True)
-        out[0, :, u * HEAD : (u + 1) * HEAD] = (
+        result[:, u * HEAD : (u + 1) * HEAD] = (
             reads / jnp.sqrt(mean + 1e-06) * gain[...]
         ).astype(BF16)
+    slot = jnp.bitwise_xor(pl.program_id(0), place[0])
+    for k, out in enumerate(outs):
+
+        @pl.when(slot == k)
+        def _(out=out):
+            out[...] = result[...]
 
 
 def read(place, carry, add, start, gain):
@@ -316,15 +364,14 @@
         num_scalar_prefetch=1,
         grid=(blocks,),
         in_specs=[stream, stream, whole(start.shape), whole(gain.shape)],
-        out_specs=pl.BlockSpec(
-            (1, rows, UNITS * HEAD), lambda b, s: (jnp.bitwise_xor(b, s[0]), 0, 0)
-        ),
-        scratch_shapes=[pltpu.VMEM(start.shape, F32)],
+        out_specs=[whole((rows, UNITS * HEAD))] * blocks,
+        scratch_shapes=[pltpu.VMEM((rows, UNITS * HEAD), BF16), pltpu.VMEM(start.shape, F32)],
     )
     return pl.pallas_call(
         read_kernel,
         grid_spec=grid_spec,
-        out_shape=jax.ShapeDtypeStruct((blocks, rows, UNITS * HEAD), BF16),
+        out_shape=[jax.ShapeDtypeStruct((rows, UNITS * HEAD), BF16)] * blocks,
+        compiler_params=pltpu.CompilerParams(vmem_limit_bytes=VMEM_LIMIT),
         name="read",
     )(place, carry, add, start, gain)
 
@@ -347,24 +394,30 @@
         + [pl.BlockSpec(memory_space=pltpu.VMEM)] * len(pieces),
         out_specs=pl.BlockSpec(memory_space=pltpu.VMEM),
         out_shape=jax.ShapeDtypeStruct((1, rows, HV * HEAD), BF16),
+        compiler_params=pltpu.CompilerParams(vmem_limit_bytes=VMEM_LIMIT),
         name="assemble",
     )(place, *pieces)
 
 
 def messages_direct(tokens, qkv_weight, gate_weight, seq_count):
     me = lax.axis_index("fsdp")
-    rim_rows = tokens[tokens.shape[0] - EXTRA :]
+    rim_rows = tokens[tokens.shape[0] - RIM :]
     far = swapped(tokens, "fsdp", 2)
     near = swapped(tokens, "fsdp", 1)
     rim_0 = shifted(rim_rows, ("seg", "sq"), [(i, i + 1) for i in range(seq_count - 1)])
+    rim_1 = swapped(rim_0, "fsdp", 1)
     rim_2 = swapped(rim_0, "fsdp", 2)
-    third = swapped(far, "fsdp", 1)
-    rims_other = swapped(jnp.concatenate([rim_0, rim_2], axis=0), "fsdp", 1)
-    rims = jnp.concatenate([rim_0, rims_other[:EXTRA], rim_2, rims_other[EXTRA:]], axis=0)
     share = 2 * HV // 4
     gate_t = lax.dynamic_slice_in_dim(gate_weight, me * share, share, 1).T
     place = me.astype(jnp.int32)[None]
-    message = project(place, (tokens, near, far, third), rims, gate_t, qkv_weight)
+    message = project(
+        place, (tokens, near), (rim_0, rim_1), gate_t, qkv_weight, False, None
+    )
+    third = swapped(far, "fsdp", 1)
+    rim_3 = swapped(rim_2, "fsdp", 1)
+    message = project(
+        place, (far, third), (rim_2, rim_3), gate_t, qkv_weight, True, message
+    )
     message = message.reshape((SPLIT * 4,) + message.shape[2:])
     return lax.all_to_all(message, ("sq", "fsdp"), 0, 0, tiled=True)
 
@@ -397,7 +450,7 @@
     return message.reshape((SPLIT * 4,) + message.shape[2:])
 
 
-def body(inputs, qkv_weight, gate_weight, conv_weight, head_rate, dt_bias, norm_gain):
+def layer(inputs, qkv_weight, gate_weight, conv_weight, head_rate, dt_bias, norm_gain):
     segments = lax.axis_size("seg")
     tokens = inputs[0]
     build = messages_direct if lax.axis_size("fsdp") == 4 else messages_staged
@@ -425,4 +478,4 @@
     parts = Mesh(mesh.devices.reshape(seq // SPLIT, SPLIT, fsdp), ("seg", "sq", "fsdp"))
     split = P("fsdp", ("seg", "sq"), None)
     in_specs = (split, P(None, "fsdp"), P(), P(), P(), P(), P())
-    return jax.shard_map(body, mesh=parts, in_specs=in_specs, out_specs=split, check_vma=False)
+    return jax.shard_map(layer, mesh=parts, in_specs=in_specs, out_specs=split, check_vma=False)

time: 111 us -> 96.5 us (0.87)
  the two profiles are of different devices: /device:TPU:29 before, /device:TPU:0 now
where the time goes in v2:
time: 96.5 us; the launch traced here: 96 us
  waiting for transfers between devices  41.4 us (43%)
  Pallas kernels  25.6 us (27%)
  starting transfers between devices  24.2 us (25%)
  local copies, waits for them, and re-layouts  4.75 us (5%)
    ppermute x9, waiting for transfers between devices, swapped(): return lax.ppermute(value, axis, [(i, i ^ bit) for i in range(count)])  20 us
    all_to_all x1, waiting for transfers between devices, messages_direct(): return lax.all_to_all(message, ('sq', 'fsdp'), 0, 0, tiled=True)  17.7 us
    pallas_call x1, Pallas kernels, prepare(): pl.pallas_call(lambda *refs: prepare_kernel(seg_product, *refs), grid_spe...  14.1 us
    ppermute x9, starting transfers between devices, swapped(): return lax.ppermute(value, axis, [(i, i ^ bit) for i in range(count)])  9.29 us
    ppermute x2, starting transfers between devices, shifted(): return lax.ppermute(value, axes, pairs)  9.1 us
    all_to_all x1, starting transfers between devices, messages_direct(): return lax.all_to_all(message, ('sq', 'fsdp'), 0, 0, tiled=True)  5.78 us
    pallas_call x2, Pallas kernels, project(): pl.pallas_call(lambda *refs: project_kernel(other, *refs), in_specs=in_sp...  4.79 us
    pallas_call x1, Pallas kernels, read(): pl.pallas_call(read_kernel, grid_spec=grid_spec, out_shape=[jax.ShapeDtyp...  4.71 us
  transfers between devices with their start and end apart: 12, of which 8 were waited for; matrix products, arithmetic and copies ran while one was open for 2% of the time, Pallas kernels for 2%

profile of v2, /device:TPU:0, one launch (start us, length us, event | category | flops | bytes accessed | tf_op | source)
XLA Modules:
  0.0 96.0 jit_solution(16586735160907793430)
XLA Ops:
  0.0 3.0 %collective-permute-start = (bf16[128,2048]{1,0:T(8,128)(2,1)}, bf16[128,2048]{1,0:T(8,128)(2,1)S(1)}, u32[]{:S(2)}, u32[]{:S(2)}) collective-permute-start(bf16[128,2048]{1,0:T(8,128)(2,1)} %bitcast.9), channel_id=1, source_target_pairs={{0,2},{1,3},{2,0},{3,1},{4,6},{5,7},{6,4},{7,5},{8,10},{9,11},{10,... | collective-permute-start | bytes 1572872 | tf_op jit(solution)/shard_map/ppermute | solution.py:34
  3.0 12.1 %collective-permute-done.refs_1_ = bf16[128,2048]{1,0:T(8,128)(2,1)S(1)} collective-permute-done((bf16[128,2048]{1,0:T(8,128)(2,1)}, bf16[128,2048]{1,0:T(8,128)(2,1)S(1)}, u32[]{:S(2)}, u32[]{:S(2)}) %collective-permute-start) | collective-permute-done | bytes 524320 | tf_op jit(solution)/shard_map/ppermute | solution.py:34
  15.1 0.8 slice_bitcast_fusion
  15.9 3.7 %collective-permute-start.2 = (bf16[8,2048]{1,0:T(8,128)(2,1)S(1)}, bf16[8,2048]{1,0:T(8,128)(2,1)S(1)}, u32[]{:S(2)}, u32[]{:S(2)}) collective-permute-start(bf16[8,2048]{1,0:T(8,128)(2,1)S(1)} %slice_bitcast_fusion), channel_id=1, source_target_pairs={{0,4},{4,8},{8,12},{12,16},{16,20},{20,24},{24,28},{1,5},{5,9},{9,... | collective-permute-start | bytes 98312 | tf_op jit(solution)/shard_map/ppermute | solution.py:29
  19.5 1.6 %collective-permute-done.2.refs_3_ = bf16[8,2048]{1,0:T(8,128)(2,1)S(1)} collective-permute-done((bf16[8,2048]{1,0:T(8,128)(2,1)S(1)}, bf16[8,2048]{1,0:T(8,128)(2,1)S(1)}, u32[]{:S(2)}, u32[]{:S(2)}) %collective-permute-start.2) | collective-permute-done | bytes 32800 | tf_op jit(solution)/shard_map/ppermute | solution.py:29
  21.1 1.5 %collective-permute-start.3 = (bf16[8,2048]{1,0:T(8,128)(2,1)S(1)}, bf16[8,2048]{1,0:T(8,128)(2,1)S(1)}, u32[]{:S(2)}, u32[]{:S(2)}) collective-permute-start(bf16[8,2048]{1,0:T(8,128)(2,1)S(1)} %collective-permute-done.2.refs_3_), channel_id=1, source_target_pairs={{0,2},{1,3},{2,0},{3,1},{4,6},{5,7},{6,4},{7,5},{8,10},{9,11},{10,... | collective-permute-start | bytes 98312 | tf_op jit(solution)/shard_map/ppermute | solution.py:34
  22.6 0.8 dynamic-slice_bitcast_fusion.refs_5_
  23.4 1.7 %collective-permute-done.3.refs_3_ = bf16[8,2048]{1,0:T(8,128)(2,1)S(1)} collective-permute-done((bf16[8,2048]{1,0:T(8,128)(2,1)S(1)}, bf16[8,2048]{1,0:T(8,128)(2,1)S(1)}, u32[]{:S(2)}, u32[]{:S(2)}) %collective-permute-start.3) | collective-permute-done | bytes 32800 | tf_op jit(solution)/shard_map/ppermute | solution.py:34
  25.1 2.2 %copy-done = bf16[2048,1024]{1,0:T(8,128)(2,1)S(1)} copy-done((bf16[2048,1024]{1,0:T(8,128)(2,1)S(1)}, bf16[2048,1024]{1,0:T(8,128)(2,1)}, u32[]{:S(2)}) %copy-start) | copy-done | bytes 4194328
  27.2 1.0 %copy-done.2 = bf16[1,128,2048]{2,1,0:T(8,128)(2,1)S(1)} copy-done((bf16[1,128,2048]{2,1,0:T(8,128)(2,1)S(1)}, bf16[1,128,2048]{2,1,0:T(8,128)(2,1)}, u32[]{:S(2)}) %copy-start.2) | copy-done | bytes 524312
  28.3 2.4 %project_own.1.refs_7_ = bf16[4,4,144,256]{3,2,1,0:T(8,128)(2,1)} custom-call(s32[1]{0:T(128)} %bitcast.1.refs_0_, bf16[128,2048]{1,0:T(8,128)(2,1)S(1)} %bitcast.11, bf16[128,2048]{1,0:T(8,128)(2,1)S(1)} %collective-permute-done.5.refs_2_, bf16[8,2048]{1,0:T(8,128)(2,1)S(1)} %collective-permute-done.2.refs_3_, ...), custom_call_target="tpu_custom_call" | custom-call | flops 1073741824 | bytes 6291456 | tf_op jit(solution)/shard_map/project_own/pallas_call | solution.py:116
  30.7 2.4 %project_other.1 = bf16[4,4,144,256]{3,2,1,0:T(8,128)(2,1)} custom-call(s32[1]{0:T(128)} %bitcast.1.refs_0_, bf16[128,2048]{1,0:T(8,128)(2,1)S(1)} %collective-permute-done.refs_1_, bf16[128,2048]{1,0:T(8,128)(2,1)S(1)} %collective-permute-done.1.refs_2_, bf16[8,2048]{1,0:T(8,128)(2,1)S(1)} %collective-permute-done.3.refs_3_, ...), custom_call_target="tpu_custom_call", output_to_operand_aliasing={{}: (7, {})} | custom-call | flops 1073741824 | bytes 6291456 | tf_op jit(solution)/shard_map/project_other/pallas_call | solution.py:116
  33.1 5.8 %all-to-all-start = ((bf16[16,144,256]{2,1,0:T(8,128)(2,1)}), bf16[16,144,256]{2,1,0:T(8,128)(2,1)}, u32[]{:S(2)}, u32[]{:S(2)}) async-start(bf16[16,144,256]{2,1,0:T(8,128)(2,1)} %bitcast.5), calls=%async_computation | async-start | bytes 2359296 | tf_op jit(solution)/shard_map/all_to_all | solution.py:422
  38.9 17.7 %all-to-all-done.refs_3_ = bf16[16,144,256]{2,1,0:T(8,128)(2,1)} async-done(((bf16[16,144,256]{2,1,0:T(8,128)(2,1)}), bf16[16,144,256]{2,1,0:T(8,128)(2,1)}, u32[]{:S(2)}, u32[]{:S(2)}) %all-to-all-start) | async-done | bytes 1179680 | tf_op jit(solution)/shard_map/all_to_all | solution.py:422
  56.6 14.1 %prepare.1 = (f32[4,4,256,128]{3,2,1,0:T(8,128)}, f32[4,4,256,128]{3,2,1,0:T(8,128)}, bf16[4,128,128]{2,1,0:T(8,128)(2,1)}) custom-call(s32[1]{0:T(128)} %bitcast.refs_0_.place, f32[16]{0:T(128)} %refs_1_.1, f32[16]{0:T(128)} %refs_2_.1, bf16[16,144,256]{2,1,0:T(8,128)(2,1)} %all-to-all-done.refs_3_, bf16[4,4096]{1,0:T(4,128)(2,1)} %refs_4_.1), custom_call_target="tpu_custom_call" | custom-call | tf_op jit(solution)/shard_map/prepare/pallas_call | solution.py:325
  70.7 5.4 %collective-permute-start.7 = (bf16[4,128,128]{2,1,0:T(8,128)(2,1)}, bf16[4,128,128]{2,1,0:T(8,128)(2,1)}, u32[]{:S(2)}, u32[]{:S(2)}) collective-permute-start(bf16[4,128,128]{2,1,0:T(8,128)(2,1)} %get-tuple-element.14), channel_id=1, source_target_pairs={{0,16},{1,17},{2,18},{3,19},{4,20},{5,21},{6,22},{7,23},{8,24},{9,... | collective-permute-start | bytes 393224 | tf_op jit(solution)/shard_map/ppermute | solution.py:29
  76.1 2.2 %collective-permute-done.7.start = bf16[4,128,128]{2,1,0:T(8,128)(2,1)} collective-permute-done((bf16[4,128,128]{2,1,0:T(8,128)(2,1)}, bf16[4,128,128]{2,1,0:T(8,128)(2,1)}, u32[]{:S(2)}, u32[]{:S(2)}) %collective-permute-start.7) | collective-permute-done | bytes 131104 | tf_op jit(solution)/shard_map/ppermute | solution.py:29
  78.3 4.7 %read.1 = (bf16[128,512]{1,0:T(8,128)(2,1)}, bf16[128,512]{1,0:T(8,128)(2,1)}, bf16[128,512]{1,0:T(8,128)(2,1)}, bf16[128,512]{1,0:T(8,128)(2,1)}) custom-call(s32[1]{0:T(128)} %bitcast.refs_0_.place, f32[4,4,256,128]{3,2,1,0:T(8,128)} %get-tuple-element.12.carry, f32[4,4,256,128]{3,2,1,0:T(8,128)} %get-tuple-element.13.add, ...), custom_call_target="tpu_custom_call" | custom-call | tf_op jit(solution)/shard_map/read/pallas_call | solution.py:370
  83.0 0.9 collective-permute-start.8
  83.9 4.0 %collective-permute-start.9 = (bf16[128,512]{1,0:T(8,128)(2,1)}, bf16[128,512]{1,0:T(8,128)(2,1)}, u32[]{:S(2)}, u32[]{:S(2)}) collective-permute-start(bf16[128,512]{1,0:T(8,128)(2,1)} %get-tuple-element.17), channel_id=1, source_target_pairs={{0,8},{4,12},{8,0},{12,4},{1,9},{5,13},{9,1},{13,5},{2,10},{6,14},... | collective-permute-start | bytes 393224 | tf_op jit(solution)/shard_map/ppermute | solution.py:34
  87.8 0.5 collective-permute-done.8.refs_1_
  88.3 4.2 %collective-permute-done.9.refs_2_ = bf16[128,512]{1,0:T(8,128)(2,1)} collective-permute-done((bf16[128,512]{1,0:T(8,128)(2,1)}, bf16[128,512]{1,0:T(8,128)(2,1)}, u32[]{:S(2)}, u32[]{:S(2)}) %collective-permute-start.9) | collective-permute-done | bytes 131104 | tf_op jit(solution)/shard_map/ppermute | solution.py:34
  92.5 1.5 %collective-permute-done.10.refs_3_ = bf16[128,512]{1,0:T(8,128)(2,1)} collective-permute-done((bf16[128,512]{1,0:T(8,128)(2,1)}, bf16[128,512]{1,0:T(8,128)(2,1)}, u32[]{:S(2)}, u32[]{:S(2)}) %collective-permute-start.10) | collective-permute-done | bytes 131104 | tf_op jit(solution)/shard_map/ppermute | solution.py:34
  94.0 2.0 %assemble.1 = bf16[1,128,2048]{2,1,0:T(8,128)(2,1)} custom-call(s32[1]{0:T(128)} %bitcast.refs_0_.place, bf16[128,512]{1,0:T(8,128)(2,1)} %get-tuple-element.15.refs_0_, bf16[128,512]{1,0:T(8,128)(2,1)} %collective-permute-done.8.refs_1_, bf16[128,512]{1,0:T(8,128)(2,1)} %collective-permute-done.9.refs_2_, bf16[128,512]{1,0:T(8,128)(2,1)} %collective-permute-done.10.refs_3_), custom_call_target="tpu_custom_call" | custom-call | tf_op jit(solution)/shard_map/assemble/pallas_call | solution.py:391
  (13 shorter events, 0.0 us)
Async XLA Ops:
  0.0 15.1 %collective-permute-start = (bf16[128,2048]{1,0:T(8,128)(2,1)}, bf16[128,2048]{1,0:T(8,128)(2,1)S(1)}, u32[]{:S(2)}, u32[]{:S(2)}) collective-permute-start(bf16[128,2048]{1,0:T(8,128)(2,1)} %bitcast.9), channel_id=1, source_target_pairs={{0,2},{1,3},{2,0},{3,1},{4,6},{5,7},{6,4},{7,5},{8,10},{9,11},{10,... | collective-permute-start | bytes 1572872 | tf_op jit(solution)/shard_map/ppermute | solution.py:34
  3.0 22.1 %collective-permute-start.5 = (bf16[128,2048]{1,0:T(8,128)(2,1)}, bf16[128,2048]{1,0:T(8,128)(2,1)S(1)}, u32[]{:S(2)}, u32[]{:S(2)}) collective-permute-start(bf16[128,2048]{1,0:T(8,128)(2,1)} %bitcast.10), channel_id=1, source_target_pairs={{0,1},{1,0},{2,3},{3,2},{4,5},{5,4},{6,7},{7,6},{8,9},{9,8},{10,11... | collective-permute-start | bytes 1572872 | tf_op jit(solution)/shard_map/ppermute | solution.py:34
  15.1 15.6 %collective-permute-start.1 = (bf16[128,2048]{1,0:T(8,128)(2,1)S(1)}, bf16[128,2048]{1,0:T(8,128)(2,1)S(1)}, u32[]{:S(2)}, u32[]{:S(2)}) collective-permute-start(bf16[128,2048]{1,0:T(8,128)(2,1)S(1)} %collective-permute-done.refs_1_), channel_id=1, source_target_pairs={{0,1},{1,0},{2,3},{3,2},{4,5},{5,4},{6,7},{7,6},{8,9},{9,8},{10,11... | collective-permute-start | bytes 1572872 | tf_op jit(solution)/shard_map/ppermute | solution.py:34
  15.9 5.3 %collective-permute-start.2 = (bf16[8,2048]{1,0:T(8,128)(2,1)S(1)}, bf16[8,2048]{1,0:T(8,128)(2,1)S(1)}, u32[]{:S(2)}, u32[]{:S(2)}) collective-permute-start(bf16[8,2048]{1,0:T(8,128)(2,1)S(1)} %slice_bitcast_fusion), channel_id=1, source_target_pairs={{0,4},{4,8},{8,12},{12,16},{16,20},{20,24},{24,28},{1,5},{5,9},{9,... | collective-permute-start | bytes 98312 | tf_op jit(solution)/shard_map/ppermute | solution.py:29
  21.1 3.9 %collective-permute-start.6 = (bf16[8,2048]{1,0:T(8,128)(2,1)S(1)}, bf16[8,2048]{1,0:T(8,128)(2,1)S(1)}, u32[]{:S(2)}, u32[]{:S(2)}) collective-permute-start(bf16[8,2048]{1,0:T(8,128)(2,1)S(1)} %collective-permute-done.2.refs_3_), channel_id=1, source_target_pairs={{0,1},{1,0},{2,3},{3,2},{4,5},{5,4},{6,7},{7,6},{8,9},{9,8},{10,11... | collective-permute-start | bytes 98312 | tf_op jit(solution)/shard_map/ppermute | solution.py:34
  21.1 3.9 %collective-permute-start.3 = (bf16[8,2048]{1,0:T(8,128)(2,1)S(1)}, bf16[8,2048]{1,0:T(8,128)(2,1)S(1)}, u32[]{:S(2)}, u32[]{:S(2)}) collective-permute-start(bf16[8,2048]{1,0:T(8,128)(2,1)S(1)} %collective-permute-done.2.refs_3_), channel_id=1, source_target_pairs={{0,2},{1,3},{2,0},{3,1},{4,6},{5,7},{6,4},{7,5},{8,10},{9,11},{10,... | collective-permute-start | bytes 98312 | tf_op jit(solution)/shard_map/ppermute | solution.py:34
  25.0 5.7 %collective-permute-start.4 = (bf16[8,2048]{1,0:T(8,128)(2,1)S(1)}, bf16[8,2048]{1,0:T(8,128)(2,1)S(1)}, u32[]{:S(2)}, u32[]{:S(2)}) collective-permute-start(bf16[8,2048]{1,0:T(8,128)(2,1)S(1)} %collective-permute-done.3.refs_3_), channel_id=1, source_target_pairs={{0,1},{1,0},{2,3},{3,2},{4,5},{5,4},{6,7},{7,6},{8,9},{9,8},{10,11... | collective-permute-start | bytes 98312 | tf_op jit(solution)/shard_map/ppermute | solution.py:34
  25.0 2.2 %copy-start = (bf16[2048,1024]{1,0:T(8,128)(2,1)S(1)}, bf16[2048,1024]{1,0:T(8,128)(2,1)}, u32[]{:S(2)}) copy-start(bf16[2048,1024]{1,0:T(8,128)(2,1)} %refs_6_.3) | copy-start | bytes 12582916
  27.2 1.0 %copy-start.2 = (bf16[1,128,2048]{2,1,0:T(8,128)(2,1)S(1)}, bf16[1,128,2048]{2,1,0:T(8,128)(2,1)}, u32[]{:S(2)}) copy-start(bf16[1,128,2048]{2,1,0:T(8,128)(2,1)} %param.7) | copy-start | bytes 1572868
  28.3 2.4 %copy-start.1 = (bf16[2048,1024]{1,0:T(8,128)(2,1)S(1)}, bf16[2048,1024]{1,0:T(8,128)(2,1)}, u32[]{:S(2)}) copy-start(bf16[2048,1024]{1,0:T(8,128)(2,1)} %refs_6_.3) | copy-start | bytes 12582916
  33.1 23.5 %all-to-all-start = ((bf16[16,144,256]{2,1,0:T(8,128)(2,1)}), bf16[16,144,256]{2,1,0:T(8,128)(2,1)}, u32[]{:S(2)}, u32[]{:S(2)}) async-start(bf16[16,144,256]{2,1,0:T(8,128)(2,1)} %bitcast.5), calls=%async_computation | async-start | bytes 2359296 | tf_op jit(solution)/shard_map/all_to_all | solution.py:422
  70.7 7.6 %collective-permute-start.7 = (bf16[4,128,128]{2,1,0:T(8,128)(2,1)}, bf16[4,128,128]{2,1,0:T(8,128)(2,1)}, u32[]{:S(2)}, u32[]{:S(2)}) collective-permute-start(bf16[4,128,128]{2,1,0:T(8,128)(2,1)} %get-tuple-element.14), channel_id=1, source_target_pairs={{0,16},{1,17},{2,18},{3,19},{4,20},{5,21},{6,22},{7,23},{8,24},{9,... | collective-permute-start | bytes 393224 | tf_op jit(solution)/shard_map/ppermute | solution.py:29
  83.0 5.3 %collective-permute-start.8 = (bf16[128,512]{1,0:T(8,128)(2,1)}, bf16[128,512]{1,0:T(8,128)(2,1)}, u32[]{:S(2)}, u32[]{:S(2)}) collective-permute-start(bf16[128,512]{1,0:T(8,128)(2,1)} %get-tuple-element.16), channel_id=1, source_target_pairs={{0,4},{4,0},{8,12},{12,8},{1,5},{5,1},{9,13},{13,9},{2,6},{6,2},{1... | collective-permute-start | bytes 393224 | tf_op jit(solution)/shard_map/ppermute | solution.py:34
  83.9 8.6 %collective-permute-start.9 = (bf16[128,512]{1,0:T(8,128)(2,1)}, bf16[128,512]{1,0:T(8,128)(2,1)}, u32[]{:S(2)}, u32[]{:S(2)}) collective-permute-start(bf16[128,512]{1,0:T(8,128)(2,1)} %get-tuple-element.17), channel_id=1, source_target_pairs={{0,8},{4,12},{8,0},{12,4},{1,9},{5,13},{9,1},{13,5},{2,10},{6,14},... | collective-permute-start | bytes 393224 | tf_op jit(solution)/shard_map/ppermute | solution.py:34
  87.8 6.2 %collective-permute-start.10 = (bf16[128,512]{1,0:T(8,128)(2,1)}, bf16[128,512]{1,0:T(8,128)(2,1)}, u32[]{:S(2)}, u32[]{:S(2)}) collective-permute-start(bf16[128,512]{1,0:T(8,128)(2,1)} %get-tuple-element.18), channel_id=1, source_target_pairs={{0,12},{4,8},{8,4},{12,0},{1,13},{5,9},{9,5},{13,1},{2,14},{6,10},... | collective-permute-start | bytes 393224 | tf_op jit(solution)/shard_map/ppermute | solution.py:34

commit v3 on v2

--- a/solution.py
+++ b/solution.py
@@ -16,7 +16,8 @@
 CHUNK = 128
 BASE = 16
 PROJECT_VMEM = 24 << 20
-VMEM_LIMIT = 67_043_328
+VMEM_LIMIT = 24 << 20
+GROUPED = 4
 EXTRA = 16
 RIM = 8
 UNITS = HV // SPLIT
@@ -182,198 +183,268 @@
     return totals
 
 
-def prepare_kernel(seg_product, place, rate, bias, message, taps, carry_out, add_out, final, *rest):
+def activated(extended, slot, message, block, f, half, taps, first):
+    rows = CHUNK
+    lanes = slice(half * HEAD, (half + 1) * HEAD)
+    rim = message[4 * block + f, rows:, lanes].astype(F32)
+    before = message[4 * jnp.maximum(block - 1, 0) + f, rows - EXTRA : rows, lanes].astype(F32)
+    extended[slot, :RIM] = jnp.where(block == 0, rim, before)[EXTRA - RIM :]
+    extended[slot, RIM:] = message[4 * block + f, :rows, lanes].astype(F32)
+    weights = taps[:, pl.ds(pl.multiple_of(first * HEAD, HEAD), HEAD)].astype(F32)
+    total = jnp.zeros((rows, HEAD), F32)
+    for tap in range(KERNEL):
+        begin = RIM - (KERNEL - 1) + tap
+        total = total + weights[tap : tap + 1] * extended[slot, begin : begin + rows]
+    middle = 0.5 * total
+    return middle + middle * jnp.tanh(middle)
+
+
+def unit(vectors):
+    return vectors * lax.rsqrt(jnp.sum(vectors * vectors, axis=-1, keepdims=True) + 1e-06)
+
+
+def prepare_kernel(seg_product, place, rate, bias, taps, message_hbm, *rest):
+    carry_out, add_out, high_out, low_out, ratio_out, growth_out, key_high, key_low = rest[:8]
+    final = rest[8]
     if seg_product:
-        product_out, tail, state, product = rest
+        product_out, message, extended, state, sems, product = rest[9:]
     else:
-        tail, state = rest
-    step = pl.program_id(0)
+        message, extended, state, sems = rest[9:]
     j = place[0]
     rows = CHUNK
-
-    @pl.when(step == 0)
-    def _():
-        state[...] = jnp.zeros_like(state)
-        for f in range(4):
-            tail[f] = message[f, rows + EXTRA - RIM :, :].astype(F32)
+    blocks = carry_out.shape[0]
+
+    def fetch(block):
+        part = pl.ds(4 * block, 4)
+        return pltpu.make_async_copy(message_hbm.at[part], message.at[part], sems.at[block])
+
+    for block in range(blocks):
+        fetch(block).start()
 
     row, column = iota((rows, rows), 0), iota((rows, rows), 1)
     strict, within = row > column, row >= column
     eye = jnp.where(row == column, 1.0, 0.0)
+    upper = jnp.where(row <= column, 1.0, 0.0)
+    lower_eye = jnp.concatenate([jnp.where(within, 1.0, 0.0), eye], axis=0)
+    heads = [SPLIT * h + j for h in range(PAIR)]
+    state[...] = jnp.zeros_like(state)
     if seg_product:
-
-        @pl.when(step == 0)
-        def _():
-            product[...] = jnp.broadcast_to(eye, product.shape)
-
-    def activated(f, half, first):
-        lanes = slice(half * HEAD, (half + 1) * HEAD)
-        here = message[f, :rows, lanes].astype(F32)
-        extended = jnp.concatenate([tail[f, :, lanes], here], axis=0)
-        start = pl.multiple_of(first * HEAD, HEAD)
-        weights = taps[:, pl.ds(start, HEAD)].astype(F32)
-        total = jnp.zeros((rows, HEAD), F32)
-        for tap in range(KERNEL):
-            begin = RIM - (KERNEL - 1) + tap
-            total = total + weights[tap : tap + 1] * extended[begin : begin + rows]
-        tail[f, :, lanes] = here[rows - RIM :]
-        return total / (1.0 + jnp.exp(-total))
-
-    def unit(vectors):
-        return vectors * lax.rsqrt(jnp.sum(vectors * vectors, axis=-1, keepdims=True) + 1e-06)
-
-    decay_rows, strength_rows = [], []
-    for u in range(UNITS):
-        h, a = u // 2, u % 2
-        head = 2 * (SPLIT * h + j) + a
-        lanes = slice(a * HEAD, (a + 1) * HEAD)
-
-        def gate(f):
-            parts = message[f, rows : rows + EXTRA, lanes].astype(F32)
-            return (parts[0:1] + parts[1:2]) + parts[2:3]
-
-        strength_rows.append(1.0 / (1.0 + jnp.exp(-gate(h))))
-        shift = gate(2 + h) + bias[head]
-        soft = jnp.maximum(shift, 0.0) + jnp.log1p(jnp.exp(-jnp.abs(shift)))
-        decay_rows.append(-rate[head] * soft)
-    table = jnp.concatenate(decay_rows + strength_rows, axis=0)
-    upper = jnp.where(row <= column, 1.0, 0.0)
-    cum_rows = jnp.dot(table, upper, precision=HIGHEST, preferred_element_type=F32)
-    lower_eye = jnp.concatenate([jnp.where(within, 1.0, 0.0), eye], axis=0)
-    columns = lax.dot_general(
-        lower_eye, table, (((1,), (1,)), ((), ())), precision=HIGHEST, preferred_element_type=F32
-    )
-
-    heads = [SPLIT * h + j for h in range(PAIR)]
-    queries = [unit(activated(0, h, heads[h])) * HEAD ** (-0.5) for h in range(PAIR)]
-    keys = [unit(activated(1, h, HK + heads[h])) for h in range(PAIR)]
-    keys_t = [key.T for key in keys]
-    scores = [
-        dot3(halves(jnp.concatenate([keys[h], queries[h]], axis=0)), halves(keys_t[h]))
-        for h in range(PAIR)
-    ]
-    growths, strengths, lasts, lowers, mixings = [], [], [], [], []
-    for u in range(UNITS):
-        cum_c = columns[:rows, u : u + 1]
-        strength = columns[rows:, UNITS + u : UNITS + u + 1]
-        cum_r = cum_rows[u : u + 1]
-        ratio = jnp.exp(jnp.minimum(cum_c - cum_r, 0.0))
-        growths.append(jnp.exp(cum_c))
-        strengths.append(strength)
-        lasts.append(cum_rows[u : u + 1, rows - 1 : rows])
-        lowers.append(jnp.where(strict, strength * ratio * scores[u // 2][:rows], 0.0))
-        mixings.append(jnp.where(within, ratio * scores[u // 2][rows:], 0.0))
-    solves = inverses(lowers)
-    weighted = []
-    for u in range(UNITS):
-        h, a = u // 2, u % 2
-        value = activated(2 + h, a, 2 * HK + 2 * heads[h] + a)
-        scaled = jnp.concatenate(
-            [(strengths[u] * growths[u]) * keys[h], strengths[u] * value], axis=1
+        product[...] = jnp.broadcast_to(eye, product.shape)
+
+    def gate_tables(block):
+        decay_rows, strength_rows = [], []
+        for u in range(UNITS):
+            h, a = u // 2, u % 2
+            head = 2 * heads[h] + a
+            lanes = slice(a * HEAD, (a + 1) * HEAD)
+
+            def gate(f):
+                parts = message[4 * block + f, rows : rows + EXTRA, lanes].astype(F32)
+                return (parts[0:1] + parts[1:2]) + parts[2:3]
+
+            strength_rows.append(1.0 / (1.0 + jnp.exp(-gate(h))))
+            shift = gate(2 + h) + bias[head]
+            soft = jnp.maximum(shift, 0.0) + jnp.log1p(jnp.exp(-jnp.abs(shift)))
+            decay_rows.append(-rate[head] * soft)
+        return jnp.concatenate(decay_rows + strength_rows, axis=0)
+
+    def several(index, _):
+        group = [GROUPED * index + i for i in range(GROUPED)]
+        for block in group:
+            fetch(block).wait()
+        tables = jnp.concatenate([gate_tables(block) for block in group], axis=0)
+        sums = jnp.dot(tables, upper, precision=HIGHEST, preferred_element_type=F32)
+        turned = lax.dot_general(
+            lower_eye, tables, (((1,), (1,)), ((), ())), precision=HIGHEST, preferred_element_type=F32
         )
-        weighted.append(halves(dot3(halves(solves[u]), halves(scaled))))
-    mixed = []
-    for u in range(UNITS):
-        trailing = jnp.exp(jnp.minimum(lasts[u] - cum_rows[u : u + 1], 0.0))
-        left = jnp.concatenate([trailing * keys_t[u // 2], mixings[u]], axis=0)
-        mixed.append(dot3(halves(left), weighted[u]))
-    for u in range(UNITS):
-        carry = jnp.exp(lasts[u]) * eye - mixed[u][:rows, :HEAD]
-        carry_out[0, u, :rows] = carry
-        carry_out[0, u, rows:] = growths[u] * queries[u // 2] - mixed[u][rows:, :HEAD]
-        add_out[0, u] = mixed[u][:, HEAD:]
-        carry_parts = halves(carry)
-        state[u] = dot3(carry_parts, halves(state[u])) + mixed[u][:rows, HEAD:]
-        if seg_product:
-            product[u] = dot3(carry_parts, halves(product[u]))
-
-    @pl.when(step == pl.num_programs(0) - 1)
-    def _():
-        final[...] = state[...].astype(final.dtype)
-        if seg_product:
-            product_out[...] = product[...].astype(product_out.dtype)
+        keys, keys_t, scores = [], [], []
+        for i, block in enumerate(group):
+            for h in range(PAIR):
+                slot = (PAIR + UNITS) * i + h
+                key = unit(activated(extended, slot, message, block, 1, h, taps, HK + heads[h]))
+                keys.append(key)
+                keys_t.append(key.T)
+                parts = halves(keys_t[-1])
+                key_high[block, h], key_low[block, h] = parts
+                scores.append(dot3(halves(key), parts))
+        growths, strengths, lasts, trailings, lowers = [], [], [], [], []
+        for i, block in enumerate(group):
+            growth_all = jnp.exp(turned[:rows, 2 * UNITS * i : 2 * UNITS * (i + 1)])
+            growth_out[block] = growth_all
+            for u in range(UNITS):
+                at = 2 * UNITS * i + u
+                cum_c = turned[:rows, at : at + 1]
+                strength = turned[rows:, at + UNITS : at + UNITS + 1]
+                cum_r = sums[at : at + 1]
+                last = sums[at : at + 1, rows - 1 : rows]
+                ratio = jnp.where(within, jnp.exp(jnp.minimum(cum_c - cum_r, 0.0)), 0.0)
+                ratio_out[block, u] = ratio
+                growths.append(growth_all[:, u : u + 1])
+                strengths.append(strength)
+                lasts.append(last)
+                trailings.append(jnp.exp(jnp.minimum(last - cum_r, 0.0)))
+                score = scores[PAIR * i + u // 2]
+                lowers.append(jnp.where(strict, strength * ratio * score, 0.0))
+        solves = inverses(lowers)
+        weighted = []
+        for i, block in enumerate(group):
+            for u in range(UNITS):
+                h, a, at = u // 2, u % 2, UNITS * i + u
+                slot = (PAIR + UNITS) * i + PAIR + u
+                first = 2 * HK + 2 * heads[h] + a
+                value = activated(extended, slot, message, block, 2 + h, a, taps, first)
+                scaled = jnp.concatenate(
+                    [(strengths[at] * growths[at]) * keys[PAIR * i + h], strengths[at] * value],
+                    axis=1,
+                )
+                weighted.append(halves(dot3(halves(solves[at]), halves(scaled))))
+                high_out[block, u], low_out[block, u] = weighted[at]
+        carries, adds = [], []
+        for i, block in enumerate(group):
+            for u in range(UNITS):
+                at = UNITS * i + u
+                left = trailings[at] * keys_t[PAIR * i + u // 2]
+                mixed = dot3(halves(left), weighted[at])
+                carry = jnp.exp(lasts[at]) * eye - mixed[:, :HEAD]
+                carry_out[block, u] = carry
+                add_out[block, u] = mixed[:, HEAD:]
+                carries.append(halves(carry))
+                adds.append(mixed[:, HEAD:])
+        for i in range(GROUPED):
+            for u in range(UNITS):
+                at = UNITS * i + u
+                state[u] = dot3(carries[at], halves(state[u])) + adds[at]
+                if seg_product:
+                    product[u] = dot3(carries[at], halves(product[u]))
+        return 0
+
+    lax.fori_loop(0, blocks // GROUPED, several, 0)
+    final[...] = state[...].astype(final.dtype)
+    if seg_product:
+        product_out[...] = product[...].astype(product_out.dtype)
 
 
 def prepare(place, rate, bias, message, taps, seg_product):
     blocks = message.shape[0] // 4
     rows = message.shape[1] - EXTRA
     assert rows == CHUNK
-    whole = lambda shape: pl.BlockSpec(shape, lambda b, *s: (0,) * len(shape))
     state_shape = (UNITS, HEAD, HEAD)
-    out_shape = [
-        jax.ShapeDtypeStruct((blocks, UNITS, 2 * rows, HEAD), F32),
-        jax.ShapeDtypeStruct((blocks, UNITS, 2 * rows, HEAD), F32),
-        jax.ShapeDtypeStruct(state_shape, BF16),
+    streams = [
+        (state_shape, F32),
+        (state_shape, F32),
+        ((UNITS, rows, 2 * HEAD), BF16),
+        ((UNITS, rows, 2 * HEAD), BF16),
+        ((UNITS, rows, rows), F32),
+        ((rows, 2 * UNITS), F32),
+        ((PAIR, HEAD, rows), BF16),
+        ((PAIR, HEAD, rows), BF16),
     ]
-    stream = pl.BlockSpec((1, UNITS, 2 * rows, HEAD), lambda b, *s: (b, 0, 0, 0))
-    out_specs = [stream, stream, whole(state_shape)]
-    scratch = [pltpu.VMEM((4, RIM, 2 * HEAD), F32), pltpu.VMEM(state_shape, F32)]
+    out_shape = [jax.ShapeDtypeStruct((blocks,) + shape, dtype) for shape, dtype in streams]
+    out_shape.append(jax.ShapeDtypeStruct(state_shape, BF16))
+    scratch = [
+        pltpu.VMEM(message.shape, BF16),
+        pltpu.VMEM(((PAIR + UNITS) * GROUPED, RIM + rows, HEAD), F32),
+        pltpu.VMEM(state_shape, F32),
+        pltpu.SemaphoreType.DMA((blocks,)),
+    ]
     if seg_product:
         out_shape.append(jax.ShapeDtypeStruct(state_shape, F32))
-        out_specs.append(whole(state_shape))
         scratch.append(pltpu.VMEM(state_shape, F32))
-    grid_spec = pltpu.PrefetchScalarGridSpec(
-        num_scalar_prefetch=3,
-        grid=(blocks,),
-        in_specs=[
-            pl.BlockSpec((4, rows + EXTRA, 2 * HEAD), lambda b, *s: (b, 0, 0)),
-            whole(taps.shape),
-        ],
-        out_specs=out_specs,
-        scratch_shapes=scratch,
-    )
+    scalars = pl.BlockSpec(memory_space=pltpu.SMEM)
+    vectors = pl.BlockSpec(memory_space=pltpu.VMEM)
     return pl.pallas_call(
         lambda *refs: prepare_kernel(seg_product, *refs),
-        grid_spec=grid_spec,
+        in_specs=[scalars] * 3 + [vectors, pl.BlockSpec(memory_space=pl.ANY)],
+        out_specs=[vectors] * len(out_shape),
         out_shape=out_shape,
+        scratch_shapes=scratch,
         compiler_params=pltpu.CompilerParams(vmem_limit_bytes=VMEM_LIMIT),
         name="prepare",
-    )(place, rate, bias, message, taps)
-
-
-def read_kernel(place, carry, add, start, gain, *rest):
-    outs, result, state = rest[:-2], rest[-2], rest[-1]
-
-    @pl.when(pl.program_id(0) == 0)
-    def _():
-        state[...] = start[...].astype(F32)
-
-    rows = CHUNK
-    for u in range(UNITS):
-        both = dot3(halves(carry[0, u]), halves(state[u])) + add[0, u]
-        state[u] = both[:rows]
-        reads = both[rows:]
-        mean = jnp.mean(reads * reads, axis=-1, keepdims=True)
-        result[:, u * HEAD : (u + 1) * HEAD] = (
-            reads / jnp.sqrt(mean + 1e-06) * gain[...]
-        ).astype(BF16)
-    slot = jnp.bitwise_xor(pl.program_id(0), place[0])
-    for k, out in enumerate(outs):
-
-        @pl.when(slot == k)
-        def _(out=out):
-            out[...] = result[...]
-
-
-def read(place, carry, add, start, gain):
-    blocks, _, double, _ = carry.shape
-    rows = double // 2
-    whole = lambda shape: pl.BlockSpec(shape, lambda b, *s: (0,) * len(shape))
-    stream = pl.BlockSpec((1, UNITS, double, HEAD), lambda b, *s: (b, 0, 0, 0))
-    grid_spec = pltpu.PrefetchScalarGridSpec(
-        num_scalar_prefetch=1,
-        grid=(blocks,),
-        in_specs=[stream, stream, whole(start.shape), whole(gain.shape)],
-        out_specs=[whole((rows, UNITS * HEAD))] * blocks,
-        scratch_shapes=[pltpu.VMEM((rows, UNITS * HEAD), BF16), pltpu.VMEM(start.shape, F32)],
-    )
+    )(place, rate, bias, taps, message)
+
+
+def local_kernel(place, message, taps, high, low, ratio, growth, key_high, key_low, *rest):
+    query_out, base_out, extended = rest
+    heads = [SPLIT * h + place[0] for h in range(PAIR)]
+
+    def one(block, _):
+        queries, scores = [], []
+        for h in range(PAIR):
+            vectors = unit(activated(extended, h, message, block, 0, h, taps, heads[h]))
+            queries.append(vectors * HEAD ** (-0.5))
+            scores.append(dot3(halves(queries[h]), (key_high[block, h], key_low[block, h])))
+        mixed = []
+        for u in range(UNITS):
+            mixing = ratio[block, u] * scores[u // 2]
+            mixed.append(dot3(halves(mixing), (high[block, u], low[block, u])))
+        for u in range(UNITS):
+            query_out[block, u] = (
+                growth[block, :, u : u + 1] * queries[u // 2] - mixed[u][:, :HEAD]
+            )
+            base_out[block, u] = mixed[u][:, HEAD:]
+        return 0
+
+    lax.fori_loop(0, query_out.shape[0], one, 0)
+
+
+def local(place, message, taps, parts):
+    blocks = message.shape[0] // 4
+    rows = message.shape[1] - EXTRA
+    shape = (blocks, UNITS, rows, HEAD)
+    vectors = pl.BlockSpec(memory_space=pltpu.VMEM)
+    flops = blocks * UNITS * 2 * 3 * rows * rows * 3 * HEAD
+    return pl.pallas_call(
+        local_kernel,
+        in_specs=[pl.BlockSpec(memory_space=pltpu.SMEM)] + [vectors] * (2 + len(parts)),
+        out_specs=[vectors, vectors],
+        out_shape=[jax.ShapeDtypeStruct(shape, F32)] * 2,
+        scratch_shapes=[pltpu.VMEM((PAIR, RIM + rows, HEAD), F32)],
+        cost_estimate=pl.CostEstimate(
+            flops=flops, bytes_accessed=12 << 20, transcendentals=message.size
+        ),
+        compiler_params=pltpu.CompilerParams(vmem_limit_bytes=VMEM_LIMIT),
+        name="local",
+    )(place, message, taps, *parts)
+
+
+def read_kernel(place, carry, add, query, base, start, gain, *rest):
+    outs, state = rest[:-1], rest[-1]
+    state[...] = start[...].astype(F32)
+
+    def one(block, _):
+        results = []
+        for u in range(UNITS):
+            left = jnp.concatenate([carry[block, u], query[block, u]], axis=0)
+            both = dot3(halves(left), halves(state[u]))
+            state[u] = both[:HEAD] + add[block, u]
+            reads = both[HEAD:] + base[block, u]
+            mean = jnp.mean(reads * reads, axis=-1, keepdims=True)
+            results.append((reads / jnp.sqrt(mean + 1e-06) * gain[...]).astype(BF16))
+        slot = jnp.bitwise_xor(block, place[0])
+        for k, out in enumerate(outs):
+
+            @pl.when(slot == k)
+            def _(out=out):
+                for u in range(UNITS):
+                    out[:, u * HEAD : (u + 1) * HEAD] = results[u]
+
+        return 0
+
+    lax.fori_loop(0, carry.shape[0], one, 0)
+
+
+def read(place, carry, add, query, base, start, gain):
+    blocks, _, rows, _ = query.shape
+    vectors = pl.BlockSpec(memory_space=pltpu.VMEM)
     return pl.pallas_call(
         read_kernel,
-        grid_spec=grid_spec,
+        in_specs=[pl.BlockSpec(memory_space=pltpu.SMEM)] + [vectors] * 6,
+        out_specs=[vectors] * blocks,
         out_shape=[jax.ShapeDtypeStruct((rows, UNITS * HEAD), BF16)] * blocks,
+        scratch_shapes=[pltpu.VMEM(start.shape, F32)],
         compiler_params=pltpu.CompilerParams(vmem_limit_bytes=VMEM_LIMIT),
         name="read",
-    )(place, carry, add, start, gain)
+    )(place, carry, add, query, base, start, gain)
 
 
 def assemble_kernel(place, *refs):
@@ -457,18 +528,17 @@
     message = build(tokens, qkv_weight, gate_weight, segments * SPLIT)
     place = lax.axis_index("sq").astype(jnp.int32)[None]
     outs = prepare(place, head_rate, dt_bias, message, conv_weight, segments > 2)
-    carry, add, final = outs[:3]
+    carry, add, parts, final = outs[0], outs[1], outs[2:8], outs[8]
     onward = [(i, i + 1) for i in range(segments - 1)]
-    if segments == 1:
-        start = jnp.zeros_like(final)
-    elif segments == 2:
+    start = jnp.zeros_like(final)
+    if segments == 2:
         start = shifted(final, "seg", onward)
-    else:
-        start = jnp.zeros_like(final)
+    elif segments > 2:
         for _ in range(segments - 1):
-            ahead = jnp.einsum("hij,hjk->hik", outs[3], start.astype(F32), precision=HIGHEST)
+            ahead = jnp.einsum("hij,hjk->hik", outs[9], start.astype(F32), precision=HIGHEST)
             start = shifted((ahead + final.astype(F32)).astype(BF16), "seg", onward)
-    pieces = read(place, carry, add, start, norm_gain[None])
+    query, base = local(place, message, conv_weight, parts)
+    pieces = read(place, carry, add, query, base, start, norm_gain[None])
     received = [pieces[0]] + [swapped(pieces[k], "sq", k) for k in range(1, SPLIT)]
     return assemble(place, received)
 

time: 96.5 us -> 85.4 us (0.88)
  Pallas kernels: 25.6 us -> 17.4 us
  waiting for transfers between devices: 41.4 us -> 39.9 us
    pallas_call x2 -> x3, Pallas kernels: 18.8 us -> 11.7 us  [the longest x1 7.68 us: prepare(): pl.pallas_call(lambda *refs: prepare_kernel(seg_product, *refs), in_specs...]
    ppermute x2, waiting for transfers between devices: 3.74 us -> 1.84 us  [shifted(): return lax.ppermute(value, axes, pairs)]
    pallas_call x1, Pallas kernels: 1.95 us -> 0.86 us  [assemble(): pl.pallas_call(assemble_kernel, in_specs=[pl.BlockSpec(memory_space=pltpu...]
    unnamed x6 -> x16, local copies, waits for them, and re-layouts: 3.23 us -> 3.26 us
  transfers between devices with their start and end apart: 12 -> 12, of which waited for: 8 -> 8; matrix products, arithmetic and copies ran while one was open for 2% -> 1% of each run, Pallas kernels for 2% -> 5%
where the time goes in v3:
time: 85.4 us; the launch traced here: 85 us
  waiting for transfers between devices  39.9 us (47%)
  starting transfers between devices  23.5 us (28%)
  Pallas kernels  17.4 us (20%)
  local copies, waits for them, and re-layouts  4.02 us (5%)
    ppermute x9, waiting for transfers between devices, swapped(): return lax.ppermute(value, axis, [(i, i ^ bit) for i in range(count)])  20.4 us
    all_to_all x1, waiting for transfers between devices, messages_direct(): return lax.all_to_all(message, ('sq', 'fsdp'), 0, 0, tiled=True)  17.6 us
    ppermute x9, starting transfers between devices, swapped(): return lax.ppermute(value, axis, [(i, i ^ bit) for i in range(count)])  9.43 us
    ppermute x2, starting transfers between devices, shifted(): return lax.ppermute(value, axes, pairs)  8.16 us
    pallas_call x1, Pallas kernels, prepare(): pl.pallas_call(lambda *refs: prepare_kernel(seg_product, *refs), in_specs...  7.68 us
    all_to_all x1, starting transfers between devices, messages_direct(): return lax.all_to_all(message, ('sq', 'fsdp'), 0, 0, tiled=True)  5.9 us
    pallas_call x2, Pallas kernels, project(): pl.pallas_call(lambda *refs: project_kernel(other, *refs), in_specs=in_sp...  4.8 us
    unnamed x16, local copies, waits for them, and re-layouts  3.26 us
  transfers between devices with their start and end apart: 12, of which 8 were waited for; matrix products, arithmetic and copies ran while one was open for 1% of the time, Pallas kernels for 5%

profile of v3, /device:TPU:0, one launch (start us, length us, event | category | flops | bytes accessed | tf_op | source)
XLA Modules:
  0.0 85.0 jit_solution(5165920888391226886)
XLA Ops:
  0.0 3.0 %collective-permute-start = (bf16[128,2048]{1,0:T(8,128)(2,1)}, bf16[128,2048]{1,0:T(8,128)(2,1)S(1)}, u32[]{:S(2)}, u32[]{:S(2)}) collective-permute-start(bf16[128,2048]{1,0:T(8,128)(2,1)} %bitcast.9), channel_id=1, source_target_pairs={{0,2},{1,3},{2,0},{3,1},{4,6},{5,7},{6,4},{7,5},{8,10},{9,11},{10,... | collective-permute-start | bytes 1572872 | tf_op jit(solution)/shard_map/ppermute | solution.py:35
  3.0 12.1 %collective-permute-done.refs_1_ = bf16[128,2048]{1,0:T(8,128)(2,1)S(1)} collective-permute-done((bf16[128,2048]{1,0:T(8,128)(2,1)}, bf16[128,2048]{1,0:T(8,128)(2,1)S(1)}, u32[]{:S(2)}, u32[]{:S(2)}) %collective-permute-start) | collective-permute-done | bytes 524320 | tf_op jit(solution)/shard_map/ppermute | solution.py:35
  15.1 0.8 slice_bitcast_fusion
  15.9 3.7 %collective-permute-start.2 = (bf16[8,2048]{1,0:T(8,128)(2,1)S(1)}, bf16[8,2048]{1,0:T(8,128)(2,1)S(1)}, u32[]{:S(2)}, u32[]{:S(2)}) collective-permute-start(bf16[8,2048]{1,0:T(8,128)(2,1)S(1)} %slice_bitcast_fusion), channel_id=1, source_target_pairs={{0,4},{4,8},{8,12},{12,16},{16,20},{20,24},{24,28},{1,5},{5,9},{9,... | collective-permute-start | bytes 98312 | tf_op jit(solution)/shard_map/ppermute | solution.py:30
  19.5 1.6 %collective-permute-done.2.refs_3_ = bf16[8,2048]{1,0:T(8,128)(2,1)S(1)} collective-permute-done((bf16[8,2048]{1,0:T(8,128)(2,1)S(1)}, bf16[8,2048]{1,0:T(8,128)(2,1)S(1)}, u32[]{:S(2)}, u32[]{:S(2)}) %collective-permute-start.2) | collective-permute-done | bytes 32800 | tf_op jit(solution)/shard_map/ppermute | solution.py:30
  21.1 1.5 %collective-permute-start.3 = (bf16[8,2048]{1,0:T(8,128)(2,1)S(1)}, bf16[8,2048]{1,0:T(8,128)(2,1)S(1)}, u32[]{:S(2)}, u32[]{:S(2)}) collective-permute-start(bf16[8,2048]{1,0:T(8,128)(2,1)S(1)} %collective-permute-done.2.refs_3_), channel_id=1, source_target_pairs={{0,2},{1,3},{2,0},{3,1},{4,6},{5,7},{6,4},{7,5},{8,10},{9,11},{10,... | collective-permute-start | bytes 98312 | tf_op jit(solution)/shard_map/ppermute | solution.py:35
  22.6 2.4 %collective-permute-done.3.refs_3_ = bf16[8,2048]{1,0:T(8,128)(2,1)S(1)} collective-permute-done((bf16[8,2048]{1,0:T(8,128)(2,1)S(1)}, bf16[8,2048]{1,0:T(8,128)(2,1)S(1)}, u32[]{:S(2)}, u32[]{:S(2)}) %collective-permute-start.3) | collective-permute-done | bytes 32800 | tf_op jit(solution)/shard_map/ppermute | solution.py:35
  25.1 2.2 %copy-done.1 = bf16[2048,1024]{1,0:T(8,128)(2,1)S(1)} copy-done((bf16[2048,1024]{1,0:T(8,128)(2,1)S(1)}, bf16[2048,1024]{1,0:T(8,128)(2,1)}, u32[]{:S(2)}) %copy-start.1) | copy-done | bytes 4194328
  27.2 1.0 %copy-done.3 = bf16[1,128,2048]{2,1,0:T(8,128)(2,1)S(1)} copy-done((bf16[1,128,2048]{2,1,0:T(8,128)(2,1)S(1)}, bf16[1,128,2048]{2,1,0:T(8,128)(2,1)}, u32[]{:S(2)}) %copy-start.3) | copy-done | bytes 524312
  28.3 2.4 %project_own.1.refs_7_ = bf16[4,4,144,256]{3,2,1,0:T(8,128)(2,1)} custom-call(s32[1]{0:T(128)} %bitcast.1.refs_0_, bf16[128,2048]{1,0:T(8,128)(2,1)S(1)} %bitcast.11, bf16[128,2048]{1,0:T(8,128)(2,1)S(1)} %collective-permute-done.5.refs_2_, bf16[8,2048]{1,0:T(8,128)(2,1)S(1)} %collective-permute-done.2.refs_3_, ...), custom_call_target="tpu_custom_call" | custom-call | flops 1073741824 | bytes 6291456 | tf_op jit(solution)/shard_map/project_own/pallas_call | solution.py:117
  30.7 2.4 %project_other.1 = bf16[4,4,144,256]{3,2,1,0:T(8,128)(2,1)} custom-call(s32[1]{0:T(128)} %bitcast.1.refs_0_, bf16[128,2048]{1,0:T(8,128)(2,1)S(1)} %collective-permute-done.refs_1_, bf16[128,2048]{1,0:T(8,128)(2,1)S(1)} %collective-permute-done.1.refs_2_, bf16[8,2048]{1,0:T(8,128)(2,1)S(1)} %collective-permute-done.3.refs_3_, ...), custom_call_target="tpu_custom_call", output_to_operand_aliasing={{}: (7, {})} | custom-call | flops 1073741824 | bytes 6291456 | tf_op jit(solution)/shard_map/project_other/pallas_call | solution.py:117
  33.2 5.9 %all-to-all-start = ((bf16[16,144,256]{2,1,0:T(8,128)(2,1)}), bf16[16,144,256]{2,1,0:T(8,128)(2,1)S(1)}, u32[]{:S(2)}, u32[]{:S(2)}) async-start(bf16[16,144,256]{2,1,0:T(8,128)(2,1)} %bitcast.5), calls=%async_computation | async-start | bytes 2359296 | tf_op jit(solution)/shard_map/all_to_all | solution.py:493
  39.1 17.6 %all-to-all-done.refs_4_.message = bf16[16,144,256]{2,1,0:T(8,128)(2,1)S(1)} async-done(((bf16[16,144,256]{2,1,0:T(8,128)(2,1)}), bf16[16,144,256]{2,1,0:T(8,128)(2,1)S(1)}, u32[]{:S(2)}, u32[]{:S(2)}) %all-to-all-start) | async-done | bytes 1179680 | tf_op jit(solution)/shard_map/all_to_all | solution.py:493
  56.7 7.7 %prepare.1 = (f32[4,4,128,128]{3,2,1,0:T(8,128)S(1)}, f32[4,4,128,128]{3,2,1,0:T(8,128)S(1)}, bf16[4,4,128,256]{3,2,1,0:T(8,128)(2,1)S(1)}, bf16[4,4,128,256]{3,...) custom-call(s32[1]{0:T(128)} %bitcast.refs_0_.place, ...), custom_call_target="tpu_custom_call" | custom-call | tf_op jit(solution)/shard_map/prepare/pallas_call | solution.py:355
  64.4 4.5 %collective-permute-start.7 = (bf16[4,128,128]{2,1,0:T(8,128)(2,1)S(1)}, bf16[4,128,128]{2,1,0:T(8,128)(2,1)S(1)}, u32[]{:S(2)}, u32[]{:S(2)}) collective-permute-start(bf16[4,128,128]{2,1,0:T(8,128)(2,1)S(1)} %get-tuple-element.30), channel_id=1, source_target_pairs={{0,16},{1,17},{2,18},{3,19},{4,20},{5,21},{6,22},{7,23},{8,24},{9,... | collective-permute-start | bytes 393224 | tf_op jit(solution)/shard_map/ppermute | solution.py:30
  68.9 2.2 %local.1 = (f32[4,4,128,128]{3,2,1,0:T(8,128)S(1)}, f32[4,4,128,128]{3,2,1,0:T(8,128)S(1)}) custom-call(s32[1]{0:T(128)} %bitcast.refs_0_.place, bf16[16,144,256]{2,1,0:T(8,128)(2,1)S(1)} %all-to-all-done.refs_4_.message, bf16[4,4096]{1,0:T(4,128)(2,1)S(1)} %copy-done.4, bf16[4,4,128,256]{3,2,1,0:T(8,128)(2,1)S(1)} %get-tuple-element.22.high, ...), custom_call_target="tpu_custom_call" | custom-call | flops 603979776 | bytes 12582912 | tf_op jit(solution)/shard_map/local/pallas_call | solution.py:396
  71.1 0.3 collective-permute-done.7.start
  71.4 1.9 %read.1 = (bf16[128,512]{1,0:T(8,128)(2,1)S(1)}, bf16[128,512]{1,0:T(8,128)(2,1)S(1)}, bf16[128,512]{1,0:T(8,128)(2,1)S(1)}, bf16[128,512]{1,0:T(8,128)(2,1)S(1)}) custom-call(s32[1]{0:T(128)} %bitcast.refs_0_.place, f32[4,4,128,128]{3,2,1,0:T(8,128)S(1)} %get-tuple-element.20.carry, f32[4,4,128,128]{3,2,1,0:T(8,128)S(1)} %get-tuple-element.21.add, ...), custom_call_target="tpu_custom_call" | custom-call | tf_op jit(solution)/shard_map/read/pallas_call | solution.py:439
  73.3 1.0 %collective-permute-start.8 = (bf16[128,512]{1,0:T(8,128)(2,1)S(1)}, bf16[128,512]{1,0:T(8,128)(2,1)S(1)}, u32[]{:S(2)}, u32[]{:S(2)}) collective-permute-start(bf16[128,512]{1,0:T(8,128)(2,1)S(1)} %get-tuple-element.32), channel_id=1, source_target_pairs={{0,4},{4,0},{8,12},{12,8},{1,5},{5,1},{9,13},{13,9},{2,6},{6,2},{1... | collective-permute-start | bytes 393224 | tf_op jit(solution)/shard_map/ppermute | solution.py:35
  74.3 4.0 %collective-permute-start.9 = (bf16[128,512]{1,0:T(8,128)(2,1)S(1)}, bf16[128,512]{1,0:T(8,128)(2,1)S(1)}, u32[]{:S(2)}, u32[]{:S(2)}) collective-permute-start(bf16[128,512]{1,0:T(8,128)(2,1)S(1)} %get-tuple-element.33), channel_id=1, source_target_pairs={{0,8},{4,12},{8,0},{12,4},{1,9},{5,13},{9,1},{13,5},{2,10},{6,14},... | collective-permute-start | bytes 393224 | tf_op jit(solution)/shard_map/ppermute | solution.py:35
  78.2 0.1 collective-permute-done.8.refs_1_
  78.3 4.3 %collective-permute-done.9.refs_2_ = bf16[128,512]{1,0:T(8,128)(2,1)S(1)} collective-permute-done((bf16[128,512]{1,0:T(8,128)(2,1)S(1)}, bf16[128,512]{1,0:T(8,128)(2,1)S(1)}, u32[]{:S(2)}, u32[]{:S(2)}) %collective-permute-start.9) | collective-permute-done | bytes 131104 | tf_op jit(solution)/shard_map/ppermute | solution.py:35
  82.6 1.5 %collective-permute-done.10.refs_3_ = bf16[128,512]{1,0:T(8,128)(2,1)S(1)} collective-permute-done((bf16[128,512]{1,0:T(8,128)(2,1)S(1)}, bf16[128,512]{1,0:T(8,128)(2,1)S(1)}, u32[]{:S(2)}, u32[]{:S(2)}) %collective-permute-start.10) | collective-permute-done | bytes 131104 | tf_op jit(solution)/shard_map/ppermute | solution.py:35
  84.1 0.9 %assemble.1 = bf16[1,128,2048]{2,1,0:T(8,128)(2,1)} custom-call(s32[1]{0:T(128)} %bitcast.refs_0_.place, bf16[128,512]{1,0:T(8,128)(2,1)S(1)} %get-tuple-element.31.refs_0_, bf16[128,512]{1,0:T(8,128)(2,1)S(1)} %collective-permute-done.8.refs_1_, bf16[128,512]{1,0:T(8,128)(2,1)S(1)} %collective-permute-done.9.refs_2_, ...), custom_call_target="tpu_custom_call" | custom-call | tf_op jit(solution)/shard_map/assemble/pallas_call | solution.py:462
  (24 shorter events, 0.1 us)
Async XLA Ops:
  0.0 22.6 %copy-start = (bf16[2048,32]{0,1:T(8,128)(2,1)S(1)}, bf16[2048,32]{0,1:T(8,128)(2,1)}, u32[]{:S(2)}) copy-start(bf16[2048,32]{0,1:T(8,128)(2,1)} %param.9) | copy-start | bytes 393220
  0.0 15.1 %collective-permute-start = (bf16[128,2048]{1,0:T(8,128)(2,1)}, bf16[128,2048]{1,0:T(8,128)(2,1)S(1)}, u32[]{:S(2)}, u32[]{:S(2)}) collective-permute-start(bf16[128,2048]{1,0:T(8,128)(2,1)} %bitcast.9), channel_id=1, source_target_pairs={{0,2},{1,3},{2,0},{3,1},{4,6},{5,7},{6,4},{7,5},{8,10},{9,11},{10,... | collective-permute-start | bytes 1572872 | tf_op jit(solution)/shard_map/ppermute | solution.py:35
  3.0 22.1 %collective-permute-start.5 = (bf16[128,2048]{1,0:T(8,128)(2,1)}, bf16[128,2048]{1,0:T(8,128)(2,1)S(1)}, u32[]{:S(2)}, u32[]{:S(2)}) collective-permute-start(bf16[128,2048]{1,0:T(8,128)(2,1)} %bitcast.10), channel_id=1, source_target_pairs={{0,1},{1,0},{2,3},{3,2},{4,5},{5,4},{6,7},{7,6},{8,9},{9,8},{10,11... | collective-permute-start | bytes 1572872 | tf_op jit(solution)/shard_map/ppermute | solution.py:35
  15.1 15.6 %collective-permute-start.1 = (bf16[128,2048]{1,0:T(8,128)(2,1)S(1)}, bf16[128,2048]{1,0:T(8,128)(2,1)S(1)}, u32[]{:S(2)}, u32[]{:S(2)}) collective-permute-start(bf16[128,2048]{1,0:T(8,128)(2,1)S(1)} %collective-permute-done.refs_1_), channel_id=1, source_target_pairs={{0,1},{1,0},{2,3},{3,2},{4,5},{5,4},{6,7},{7,6},{8,9},{9,8},{10,11... | collective-permute-start | bytes 1572872 | tf_op jit(solution)/shard_map/ppermute | solution.py:35
  15.9 5.3 %collective-permute-start.2 = (bf16[8,2048]{1,0:T(8,128)(2,1)S(1)}, bf16[8,2048]{1,0:T(8,128)(2,1)S(1)}, u32[]{:S(2)}, u32[]{:S(2)}) collective-permute-start(bf16[8,2048]{1,0:T(8,128)(2,1)S(1)} %slice_bitcast_fusion), channel_id=1, source_target_pairs={{0,4},{4,8},{8,12},{12,16},{16,20},{20,24},{24,28},{1,5},{5,9},{9,... | collective-permute-start | bytes 98312 | tf_op jit(solution)/shard_map/ppermute | solution.py:30
  21.1 3.9 %collective-permute-start.6 = (bf16[8,2048]{1,0:T(8,128)(2,1)S(1)}, bf16[8,2048]{1,0:T(8,128)(2,1)S(1)}, u32[]{:S(2)}, u32[]{:S(2)}) collective-permute-start(bf16[8,2048]{1,0:T(8,128)(2,1)S(1)} %collective-permute-done.2.refs_3_), channel_id=1, source_target_pairs={{0,1},{1,0},{2,3},{3,2},{4,5},{5,4},{6,7},{7,6},{8,9},{9,8},{10,11... | collective-permute-start | bytes 98312 | tf_op jit(solution)/shard_map/ppermute | solution.py:35
  21.1 3.9 %collective-permute-start.3 = (bf16[8,2048]{1,0:T(8,128)(2,1)S(1)}, bf16[8,2048]{1,0:T(8,128)(2,1)S(1)}, u32[]{:S(2)}, u32[]{:S(2)}) collective-permute-start(bf16[8,2048]{1,0:T(8,128)(2,1)S(1)} %collective-permute-done.2.refs_3_), channel_id=1, source_target_pairs={{0,2},{1,3},{2,0},{3,1},{4,6},{5,7},{6,4},{7,5},{8,10},{9,11},{10,... | collective-permute-start | bytes 98312 | tf_op jit(solution)/shard_map/ppermute | solution.py:35
  25.0 5.7 %collective-permute-start.4 = (bf16[8,2048]{1,0:T(8,128)(2,1)S(1)}, bf16[8,2048]{1,0:T(8,128)(2,1)S(1)}, u32[]{:S(2)}, u32[]{:S(2)}) collective-permute-start(bf16[8,2048]{1,0:T(8,128)(2,1)S(1)} %collective-permute-done.3.refs_3_), channel_id=1, source_target_pairs={{0,1},{1,0},{2,3},{3,2},{4,5},{5,4},{6,7},{7,6},{8,9},{9,8},{10,11... | collective-permute-start | bytes 98312 | tf_op jit(solution)/shard_map/ppermute | solution.py:35
  25.0 2.2 %copy-start.1 = (bf16[2048,1024]{1,0:T(8,128)(2,1)S(1)}, bf16[2048,1024]{1,0:T(8,128)(2,1)}, u32[]{:S(2)}) copy-start(bf16[2048,1024]{1,0:T(8,128)(2,1)} %refs_6_.3) | copy-start | bytes 12582916
  27.2 1.0 %copy-start.3 = (bf16[1,128,2048]{2,1,0:T(8,128)(2,1)S(1)}, bf16[1,128,2048]{2,1,0:T(8,128)(2,1)}, u32[]{:S(2)}) copy-start(bf16[1,128,2048]{2,1,0:T(8,128)(2,1)} %param.7) | copy-start | bytes 1572868
  28.3 2.4 %copy-start.2 = (bf16[2048,1024]{1,0:T(8,128)(2,1)S(1)}, bf16[2048,1024]{1,0:T(8,128)(2,1)}, u32[]{:S(2)}) copy-start(bf16[2048,1024]{1,0:T(8,128)(2,1)} %refs_6_.3) | copy-start | bytes 12582916
  33.1 23.6 %copy-start.4 = (bf16[4,4096]{1,0:T(4,128)(2,1)S(1)}, bf16[4,4096]{1,0:T(4,128)(2,1)}, u32[]{:S(2)}) copy-start(bf16[4,4096]{1,0:T(4,128)(2,1)} %taps.1) | copy-start | bytes 98308
  33.1 23.6 %copy-start.5 = (f32[16]{0:T(128)S(1)}, f32[16]{0:T(128)}, u32[]{:S(2)}) copy-start(f32[16]{0:T(128)} %refs_1_.1) | copy-start | bytes 196
  33.2 23.6 %copy-start.6 = (f32[16]{0:T(128)S(1)}, f32[16]{0:T(128)}, u32[]{:S(2)}) copy-start(f32[16]{0:T(128)} %refs_2_.1) | copy-start | bytes 196
  33.2 23.5 %all-to-all-start = ((bf16[16,144,256]{2,1,0:T(8,128)(2,1)}), bf16[16,144,256]{2,1,0:T(8,128)(2,1)S(1)}, u32[]{:S(2)}, u32[]{:S(2)}) async-start(bf16[16,144,256]{2,1,0:T(8,128)(2,1)} %bitcast.5), calls=%async_computation | async-start | bytes 2359296 | tf_op jit(solution)/shard_map/all_to_all | solution.py:493
  64.4 7.0 %collective-permute-start.7 = (bf16[4,128,128]{2,1,0:T(8,128)(2,1)S(1)}, bf16[4,128,128]{2,1,0:T(8,128)(2,1)S(1)}, u32[]{:S(2)}, u32[]{:S(2)}) collective-permute-start(bf16[4,128,128]{2,1,0:T(8,128)(2,1)S(1)} %get-tuple-element.30), channel_id=1, source_target_pairs={{0,16},{1,17},{2,18},{3,19},{4,20},{5,21},{6,22},{7,23},{8,24},{9,... | collective-permute-start | bytes 393224 | tf_op jit(solution)/shard_map/ppermute | solution.py:30
  68.9 2.5 %copy-start.7 = (f32[128]{0:T(128)S(1)}, f32[128]{0:T(128)}, u32[]{:S(2)}) copy-start(f32[128]{0:T(128)} %param.13) | copy-start | bytes 1540
  73.3 5.0 %collective-permute-start.8 = (bf16[128,512]{1,0:T(8,128)(2,1)S(1)}, bf16[128,512]{1,0:T(8,128)(2,1)S(1)}, u32[]{:S(2)}, u32[]{:S(2)}) collective-permute-start(bf16[128,512]{1,0:T(8,128)(2,1)S(1)} %get-tuple-element.32), channel_id=1, source_target_pairs={{0,4},{4,0},{8,12},{12,8},{1,5},{5,1},{9,13},{13,9},{2,6},{6,2},{1... | collective-permute-start | bytes 393224 | tf_op jit(solution)/shard_map/ppermute | solution.py:35
  74.3 8.3 %collective-permute-start.9 = (bf16[128,512]{1,0:T(8,128)(2,1)S(1)}, bf16[128,512]{1,0:T(8,128)(2,1)S(1)}, u32[]{:S(2)}, u32[]{:S(2)}) collective-permute-start(bf16[128,512]{1,0:T(8,128)(2,1)S(1)} %get-tuple-element.33), channel_id=1, source_target_pairs={{0,8},{4,12},{8,0},{12,4},{1,9},{5,13},{9,1},{13,5},{2,10},{6,14},... | collective-permute-start | bytes 393224 | tf_op jit(solution)/shard_map/ppermute | solution.py:35
  78.2 5.9 %collective-permute-start.10 = (bf16[128,512]{1,0:T(8,128)(2,1)S(1)}, bf16[128,512]{1,0:T(8,128)(2,1)S(1)}, u32[]{:S(2)}, u32[]{:S(2)}) collective-permute-start(bf16[128,512]{1,0:T(8,128)(2,1)S(1)} %get-tuple-element.34), channel_id=1, source_target_pairs={{0,12},{4,8},{8,4},{12,0},{1,13},{5,9},{9,5},{13,1},{2,14},{6,10},... | collective-permute-start | bytes 393224 | tf_op jit(solution)/shard_map/ppermute | solution.py:35

commit v4 on v3

--- a/solution.py
+++ b/solution.py
@@ -18,7 +18,7 @@
 PROJECT_VMEM = 24 << 20
 VMEM_LIMIT = 24 << 20
 GROUPED = 4
-EXTRA = 16
+EXTRA = 8
 RIM = 8
 UNITS = HV // SPLIT
 F32 = jnp.float32
@@ -35,6 +35,10 @@
     return lax.ppermute(value, axis, [(i, i ^ bit) for i in range(count)])
 
 
+def in_hbm(value):
+    return pltpu.with_memory_space_constraint(value, pltpu.HBM)
+
+
 def dot(a, b):
     return jnp.dot(a, b, preferred_element_type=F32)
 
@@ -62,39 +66,58 @@
     return lax.broadcasted_iota(jnp.int32, shape, dim)
 
 
-def project_kernel(other, place, x0, x1, rim_0, rim_1, gate_t, weight, *rest):
-    out, lhs, stage, sems = rest[-4:]
+def project_kernel(other, place, x0, x1, rim_0, rim_1, gate_hbm, weight_hbm, *rest):
     rows = x0.shape[0]
     me = place[0]
     pair = 1 - me // 2 if other else me // 2
     contiguous = me >= 2
-
-    lhs[:rows, :] = x0[...]
+    loads = []
+
+    def lane(j, a):
+        return pl.multiple_of(jnp.where(contiguous, 2 * j + a, SPLIT * a + j) * HEAD, HEAD)
+
+    def load(source, target, sem):
+        copy = pltpu.make_async_copy(source, target, sem)
+        copy.start()
+        loads.append(copy)
+
+    if other:
+        out, lhs, stage, gates, sems = rest[-5:]
+        weight, gate_t = weight_hbm, gate_hbm
+        lhs[:rows, :] = x0[...]
+    else:
+        out, weight, gate_t, lhs, stage, gates, sems, load_sems = rest
+        load(x0, lhs.at[pl.ds(0, rows)], load_sems.at[0])
+        load(gate_hbm, gate_t, load_sems.at[1])
+        for j in range(SPLIT):
+            for a in range(2):
+                part = pl.ds(lane(j, a), HEAD)
+                load(weight_hbm.at[:, part], weight.at[:, part], load_sems.at[2 + 2 * j + a])
     lhs[rows : 2 * rows, :] = x1[...]
     lhs[2 * rows :, :] = jnp.concatenate([rim_0[...], rim_1[...]], axis=0)
-    raw = lax.dot_general(
+    for copy in loads[:2]:
+        copy.wait()
+    gates[...] = lax.dot_general(
         gate_t[...], lhs[: 2 * rows, :], (((1,), (1,)), ((), ())), preferred_element_type=F32
     )
-    parts = split3(raw)
-    blank = jnp.zeros((EXTRA - RIM - 3, 2 * HEAD), F32)
+    share = gate_t.shape[0] // 4
+    parts = split3(gates[pl.ds(pl.multiple_of(me * share, share), share), :])
+    index = iota((RIM, 2 * HEAD), 0)
     copies = []
     for j in range(SPLIT):
-        lanes = [
-            pl.multiple_of(jnp.where(contiguous, 2 * j + a, SPLIT * a + j) * HEAD, HEAD)
-            for a in range(2)
-        ]
-        columns = jnp.concatenate([weight[:, pl.ds(lane, HEAD)] for lane in lanes], axis=1)
+        for copy in loads[2 + 2 * j : 4 + 2 * j]:
+            copy.wait()
+        columns = jnp.concatenate([weight[:, pl.ds(lane(j, a), HEAD)] for a in range(2)], axis=1)
         mixed = dot(lhs[...], columns)
         for k in range(2):
             target = jnp.bitwise_xor(me % 2, k)
             stage[j, target, :rows, :] = mixed[k * rows : (k + 1) * rows].astype(BF16)
             tokens = slice(k * rows, (k + 1) * rows)
-            gate = [
-                jnp.concatenate([p[2 * j : 2 * j + 1, tokens], p[2 * j + 1 : 2 * j + 2, tokens]], 1)
-                for p in parts
-            ]
-            before = mixed[2 * rows + k * RIM : 2 * rows + (k + 1) * RIM]
-            stage[j, target, rows:, :] = jnp.concatenate(gate + [blank, before], axis=0).astype(BF16)
+            tail = mixed[2 * rows + k * RIM : 2 * rows + (k + 1) * RIM]
+            for part in range(3):
+                gate = [parts[part][2 * j + a : 2 * j + a + 1, tokens] for a in range(2)]
+                tail = jnp.where(index == part, jnp.concatenate(gate, axis=1), tail)
+            stage[j, target, rows:, :] = tail.astype(BF16)
         copy = pltpu.make_async_copy(stage.at[j], out.at[j, pl.ds(2 * pair, 2)], sems.at[j])
         copy.start()
         copies.append(copy)
@@ -102,28 +125,38 @@
         copy.wait()
 
 
-def project(place, xs, rims, gate_t, weight, other, message):
+def project(place, xs, rims, gate_t, weight, message):
+    other = message is not None
     rows, depth = xs[0].shape
     width = weight.shape[1]
+    vectors, anywhere = pl.BlockSpec(memory_space=pltpu.VMEM), pl.BlockSpec(memory_space=pl.ANY)
     operands = [place, *xs, *rims, gate_t, weight]
-    in_specs = [pl.BlockSpec(memory_space=pltpu.SMEM)]
-    in_specs += [pl.BlockSpec(memory_space=pltpu.VMEM)] * (len(operands) - 1)
+    first = vectors if other else pl.BlockSpec(memory_space=pltpu.HBM)
+    in_specs = [pl.BlockSpec(memory_space=pltpu.SMEM), first] + [vectors] * 3 + [first] * 2
+    message_shape = (SPLIT, 4, rows + EXTRA, 2 * HEAD)
+    out_shape = [jax.ShapeDtypeStruct(message_shape, BF16)]
+    out_specs = [anywhere]
+    scratch = [
+        pltpu.VMEM((2 * rows + 2 * RIM, depth), BF16),
+        pltpu.VMEM((SPLIT, 2, rows + EXTRA, 2 * HEAD), BF16),
+        pltpu.VMEM((gate_t.shape[0], 2 * rows), F32),
+        pltpu.SemaphoreType.DMA((SPLIT,)),
+    ]
     aliases = {}
-    if message is not None:
+    if other:
         aliases = {len(operands): 0}
         operands.append(message)
-        in_specs.append(pl.BlockSpec(memory_space=pl.ANY))
-    block = (SPLIT, 2, rows + EXTRA, 2 * HEAD)
+        in_specs.append(anywhere)
+    else:
+        out_shape += [jax.ShapeDtypeStruct(a.shape, a.dtype) for a in (weight, gate_t)]
+        out_specs += [vectors, vectors]
+        scratch.append(pltpu.SemaphoreType.DMA((2 + 2 * SPLIT,)))
     return pl.pallas_call(
         lambda *refs: project_kernel(other, *refs),
         in_specs=in_specs,
-        out_specs=pl.BlockSpec(memory_space=pl.ANY),
-        out_shape=jax.ShapeDtypeStruct((SPLIT, 4, rows + EXTRA, 2 * HEAD), BF16),
-        scratch_shapes=[
-            pltpu.VMEM((2 * rows + 2 * RIM, depth), BF16),
-            pltpu.VMEM(block, BF16),
-            pltpu.SemaphoreType.DMA((SPLIT,)),
-        ],
+        out_specs=out_specs,
+        out_shape=out_shape,
+        scratch_shapes=scratch,
         input_output_aliases=aliases,
         cost_estimate=pl.CostEstimate(
             flops=4 * rows * depth * width,
@@ -187,8 +220,8 @@
     rows = CHUNK
     lanes = slice(half * HEAD, (half + 1) * HEAD)
     rim = message[4 * block + f, rows:, lanes].astype(F32)
-    before = message[4 * jnp.maximum(block - 1, 0) + f, rows - EXTRA : rows, lanes].astype(F32)
-    extended[slot, :RIM] = jnp.where(block == 0, rim, before)[EXTRA - RIM :]
+    before = message[4 * jnp.maximum(block - 1, 0) + f, rows - RIM : rows, lanes].astype(F32)
+    extended[slot, :RIM] = jnp.where(block == 0, rim, before)
     extended[slot, RIM:] = message[4 * block + f, :rows, lanes].astype(F32)
     weights = taps[:, pl.ds(pl.multiple_of(first * HEAD, HEAD), HEAD)].astype(F32)
     total = jnp.zeros((rows, HEAD), F32)
@@ -203,23 +236,16 @@
     return vectors * lax.rsqrt(jnp.sum(vectors * vectors, axis=-1, keepdims=True) + 1e-06)
 
 
-def prepare_kernel(seg_product, place, rate, bias, taps, message_hbm, *rest):
+def prepare_kernel(seg_product, place, rate, bias, taps, message, *rest):
     carry_out, add_out, high_out, low_out, ratio_out, growth_out, key_high, key_low = rest[:8]
     final = rest[8]
     if seg_product:
-        product_out, message, extended, state, sems, product = rest[9:]
+        product_out, extended, state, product = rest[9:]
     else:
-        message, extended, state, sems = rest[9:]
+        extended, state = rest[9:]
     j = place[0]
     rows = CHUNK
     blocks = carry_out.shape[0]
-
-    def fetch(block):
-        part = pl.ds(4 * block, 4)
-        return pltpu.make_async_copy(message_hbm.at[part], message.at[part], sems.at[block])
-
-    for block in range(blocks):
-        fetch(block).start()
 
     row, column = iota((rows, rows), 0), iota((rows, rows), 1)
     strict, within = row > column, row >= column
@@ -250,8 +276,6 @@
 
     def several(index, _):
         group = [GROUPED * index + i for i in range(GROUPED)]
-        for block in group:
-            fetch(block).wait()
         tables = jnp.concatenate([gate_tables(block) for block in group], axis=0)
         sums = jnp.dot(tables, upper, precision=HIGHEST, preferred_element_type=F32)
         turned = lax.dot_general(
@@ -342,10 +366,8 @@
     out_shape = [jax.ShapeDtypeStruct((blocks,) + shape, dtype) for shape, dtype in streams]
     out_shape.append(jax.ShapeDtypeStruct(state_shape, BF16))
     scratch = [
-        pltpu.VMEM(message.shape, BF16),
         pltpu.VMEM(((PAIR + UNITS) * GROUPED, RIM + rows, HEAD), F32),
         pltpu.VMEM(state_shape, F32),
-        pltpu.SemaphoreType.DMA((blocks,)),
     ]
     if seg_product:
         out_shape.append(jax.ShapeDtypeStruct(state_shape, F32))
@@ -354,7 +376,7 @@
     vectors = pl.BlockSpec(memory_space=pltpu.VMEM)
     return pl.pallas_call(
         lambda *refs: prepare_kernel(seg_product, *refs),
-        in_specs=[scalars] * 3 + [vectors, pl.BlockSpec(memory_space=pl.ANY)],
+        in_specs=[scalars] * 3 + [vectors] * 2,
         out_specs=[vectors] * len(out_shape),
         out_shape=out_shape,
         scratch_shapes=scratch,
@@ -478,17 +500,19 @@
     rim_0 = shifted(rim_rows, ("seg", "sq"), [(i, i + 1) for i in range(seq_count - 1)])
     rim_1 = swapped(rim_0, "fsdp", 1)
     rim_2 = swapped(rim_0, "fsdp", 2)
-    share = 2 * HV // 4
-    gate_t = lax.dynamic_slice_in_dim(gate_weight, me * share, share, 1).T
+    gate_t = gate_weight.T
     place = me.astype(jnp.int32)[None]
-    message = project(
-        place, (tokens, near), (rim_0, rim_1), gate_t, qkv_weight, False, None
+    message, weight, gate_t = project(
+        place,
+        (in_hbm(tokens), near),
+        (rim_0, rim_1),
+        in_hbm(gate_t),
+        in_hbm(qkv_weight),
+        None,
     )
     third = swapped(far, "fsdp", 1)
     rim_3 = swapped(rim_2, "fsdp", 1)
-    message = project(
-        place, (far, third), (rim_2, rim_3), gate_t, qkv_weight, True, message
-    )
+    message = project(place, (far, third), (rim_2, rim_3), gate_t, weight, message)[0]
     message = message.reshape((SPLIT * 4,) + message.shape[2:])
     return lax.all_to_all(message, ("sq", "fsdp"), 0, 0, tiled=True)
 
@@ -515,8 +539,8 @@
         value = rows[:, 2 * HK * HEAD :].reshape(count, PAIR, SPLIT, 2 * HEAD)
         return jnp.concatenate([query_key, value.transpose(2, 1, 0, 3)], axis=1)
 
-    blank = jnp.zeros((SPLIT, 4, EXTRA - RIM - 3, 2 * HEAD), BF16)
-    message = jnp.concatenate([by_target(mixed), parts, blank, by_target(rim)], axis=2)
+    rim = by_target(rim)[:, :, 3:]
+    message = jnp.concatenate([by_target(mixed), parts, rim], axis=2)
     message = lax.all_to_all(message, "sq", 0, 0, tiled=True)
     return message.reshape((SPLIT * 4,) + message.shape[2:])
 

time: 85.4 us -> 84 us (0.984)
  local copies, waits for them, and re-layouts: 4.02 us -> 0.79 us
  Pallas kernels: 17.4 us -> 20.1 us
    unnamed x16 -> x8, local copies, waits for them, and re-layouts: 3.26 us -> 0.03 us
    pallas_call x2, Pallas kernels: 4.8 us -> 7.78 us  [project(): pl.pallas_call(lambda *refs: project_kernel(other, *refs), in_specs=in_sp...]
  transfers between devices with their start and end apart: 12 -> 12, of which waited for: 8 -> 8; matrix products, arithmetic and copies ran while one was open for 1% -> 1% of each run, Pallas kernels for 5% -> 9%
where the time goes in v4:
time: 84 us; the launch traced here: 83.7 us
  waiting for transfers between devices  39.2 us (47%)
  starting transfers between devices  23.5 us (28%)
  Pallas kernels  20.1 us (24%)
    ppermute x9, waiting for transfers between devices, swapped(): return lax.ppermute(value, axis, [(i, i ^ bit) for i in range(count)])  20.5 us
    all_to_all x1, waiting for transfers between devices, messages_direct(): return lax.all_to_all(message, ('sq', 'fsdp'), 0, 0, tiled=True)  16.8 us
    ppermute x9, starting transfers between devices, swapped(): return lax.ppermute(value, axis, [(i, i ^ bit) for i in range(count)])  9.43 us
    ppermute x2, starting transfers between devices, shifted(): return lax.ppermute(value, axes, pairs)  8.17 us
    pallas_call x2, Pallas kernels, project(): pl.pallas_call(lambda *refs: project_kernel(other, *refs), in_specs=in_sp...  7.78 us
    pallas_call x1, Pallas kernels, prepare(): pl.pallas_call(lambda *refs: prepare_kernel(seg_product, *refs), in_specs...  7.37 us
    all_to_all x1, starting transfers between devices, messages_direct(): return lax.all_to_all(message, ('sq', 'fsdp'), 0, 0, tiled=True)  5.89 us
    pallas_call x1, Pallas kernels, local(): pl.pallas_call(local_kernel, in_specs=[pl.BlockSpec(memory_space=pltpu.SM...  2.21 us
  transfers between devices with their start and end apart: 12, of which 8 were waited for; matrix products, arithmetic and copies ran while one was open for 1% of the time, Pallas kernels for 9%

profile of v4, /device:TPU:0, one launch (start us, length us, event | category | flops | bytes accessed | tf_op | source)
XLA Modules:
  0.0 83.7 jit_solution(5679761937702159591)
XLA Ops:
  0.0 3.0 %collective-permute-start = (bf16[128,2048]{1,0:T(8,128)(2,1)}, bf16[128,2048]{1,0:T(8,128)(2,1)S(1)}, u32[]{:S(2)}, u32[]{:S(2)}) collective-permute-start(bf16[128,2048]{1,0:T(8,128)(2,1)} %bitcast.9), channel_id=1, source_target_pairs={{0,2},{1,3},{2,0},{3,1},{4,6},{5,7},{6,4},{7,5},{8,10},{9,11},{10,... | collective-permute-start | bytes 1572872 | tf_op jit(solution)/shard_map/ppermute | solution.py:35
  3.0 12.1 %collective-permute-done.refs_1_ = bf16[128,2048]{1,0:T(8,128)(2,1)S(1)} collective-permute-done((bf16[128,2048]{1,0:T(8,128)(2,1)}, bf16[128,2048]{1,0:T(8,128)(2,1)S(1)}, u32[]{:S(2)}, u32[]{:S(2)}) %collective-permute-start) | collective-permute-done | bytes 524320 | tf_op jit(solution)/shard_map/ppermute | solution.py:35
  15.1 0.8 slice_bitcast_fusion
  15.9 3.7 %collective-permute-start.2 = (bf16[8,2048]{1,0:T(8,128)(2,1)S(1)}, bf16[8,2048]{1,0:T(8,128)(2,1)S(1)}, u32[]{:S(2)}, u32[]{:S(2)}) collective-permute-start(bf16[8,2048]{1,0:T(8,128)(2,1)S(1)} %slice_bitcast_fusion), channel_id=1, source_target_pairs={{0,4},{4,8},{8,12},{12,16},{16,20},{20,24},{24,28},{1,5},{5,9},{9,... | collective-permute-start | bytes 98312 | tf_op jit(solution)/shard_map/ppermute | solution.py:30
  19.5 1.6 %collective-permute-done.2.refs_3_ = bf16[8,2048]{1,0:T(8,128)(2,1)S(1)} collective-permute-done((bf16[8,2048]{1,0:T(8,128)(2,1)S(1)}, bf16[8,2048]{1,0:T(8,128)(2,1)S(1)}, u32[]{:S(2)}, u32[]{:S(2)}) %collective-permute-start.2) | collective-permute-done | bytes 32800 | tf_op jit(solution)/shard_map/ppermute | solution.py:30
  21.1 1.5 %collective-permute-start.3 = (bf16[8,2048]{1,0:T(8,128)(2,1)S(1)}, bf16[8,2048]{1,0:T(8,128)(2,1)S(1)}, u32[]{:S(2)}, u32[]{:S(2)}) collective-permute-start(bf16[8,2048]{1,0:T(8,128)(2,1)S(1)} %collective-permute-done.2.refs_3_), channel_id=1, source_target_pairs={{0,2},{1,3},{2,0},{3,1},{4,6},{5,7},{6,4},{7,5},{8,10},{9,11},{10,... | collective-permute-start | bytes 98312 | tf_op jit(solution)/shard_map/ppermute | solution.py:35
  22.6 2.4 %collective-permute-done.3.refs_3_ = bf16[8,2048]{1,0:T(8,128)(2,1)S(1)} collective-permute-done((bf16[8,2048]{1,0:T(8,128)(2,1)S(1)}, bf16[8,2048]{1,0:T(8,128)(2,1)S(1)}, u32[]{:S(2)}, u32[]{:S(2)}) %collective-permute-start.3) | collective-permute-done | bytes 32800 | tf_op jit(solution)/shard_map/ppermute | solution.py:35
  25.0 5.4 %project_own.1 = (bf16[4,4,136,256]{3,2,1,0:T(8,128)(2,1)}, bf16[2048,1024]{1,0:T(8,128)(2,1)S(1)}, bf16[32,2048]{1,0:T(8,128)(2,1)S(1)}) custom-call(s32[1]{0:T(128)} %bitcast.1.refs_0_, bf16[128,2048]{1,0:T(8,128)(2,1)} %bitcast.11, bf16[128,2048]{1,0:T(8,128)(2,1)S(1)} %collective-permute-done.5.refs_2_, ...), custom_call_target="tpu_custom_call" | custom-call | flops 1073741824 | bytes 6291456 | tf_op jit(solution)/shard_map/project_own/pallas_call | solution.py:154
  30.4 2.4 %project_other.1 = bf16[4,4,136,256]{3,2,1,0:T(8,128)(2,1)} custom-call(s32[1]{0:T(128)} %bitcast.1.refs_0_, bf16[128,2048]{1,0:T(8,128)(2,1)S(1)} %collective-permute-done.refs_1_, bf16[128,2048]{1,0:T(8,128)(2,1)S(1)} %collective-permute-done.1.refs_2_, bf16[8,2048]{1,0:T(8,128)(2,1)S(1)} %collective-permute-done.3.refs_3_, ...), custom_call_target="tpu_custom_call", output_to_operand_aliasing={{}: (7, {})} | custom-call | flops 1073741824 | bytes 6291456 | tf_op jit(solution)/shard_map/project_other/pallas_call | solution.py:154
  32.9 0.0 copy-start
  32.9 0.0 copy-start.1
  32.9 5.9 %all-to-all-start = ((bf16[16,136,256]{2,1,0:T(8,128)(2,1)}), bf16[16,136,256]{2,1,0:T(8,128)(2,1)S(1)}, u32[]{:S(2)}, u32[]{:S(2)}) async-start(bf16[16,136,256]{2,1,0:T(8,128)(2,1)} %bitcast.5), calls=%async_computation | async-start | bytes 2228224 | tf_op jit(solution)/shard_map/all_to_all | solution.py:517
  38.8 16.8 %all-to-all-done.refs_4_.message = bf16[16,136,256]{2,1,0:T(8,128)(2,1)S(1)} async-done(((bf16[16,136,256]{2,1,0:T(8,128)(2,1)}), bf16[16,136,256]{2,1,0:T(8,128)(2,1)S(1)}, u32[]{:S(2)}, u32[]{:S(2)}) %all-to-all-start) | async-done | bytes 1114144 | tf_op jit(solution)/shard_map/all_to_all | solution.py:517
  55.6 7.4 %prepare.1 = (f32[4,4,128,128]{3,2,1,0:T(8,128)S(1)}, f32[4,4,128,128]{3,2,1,0:T(8,128)S(1)}, bf16[4,4,128,256]{3,2,1,0:T(8,128)(2,1)S(1)}, bf16[4,4,128,256]{3,...) custom-call(s32[1]{0:T(128)} %bitcast.refs_0_.place, ...), custom_call_target="tpu_custom_call" | custom-call | tf_op jit(solution)/shard_map/prepare/pallas_call | solution.py:377
  63.0 4.5 %collective-permute-start.7 = (bf16[4,128,128]{2,1,0:T(8,128)(2,1)S(1)}, bf16[4,128,128]{2,1,0:T(8,128)(2,1)S(1)}, u32[]{:S(2)}, u32[]{:S(2)}) collective-permute-start(bf16[4,128,128]{2,1,0:T(8,128)(2,1)S(1)} %get-tuple-element.36), channel_id=1, source_target_pairs={{0,16},{1,17},{2,18},{3,19},{4,20},{5,21},{6,22},{7,23},{8,24},{9,... | collective-permute-start | bytes 393224 | tf_op jit(solution)/shard_map/ppermute | solution.py:30
  67.5 2.2 %local.1 = (f32[4,4,128,128]{3,2,1,0:T(8,128)S(1)}, f32[4,4,128,128]{3,2,1,0:T(8,128)S(1)}) custom-call(s32[1]{0:T(128)} %bitcast.refs_0_.place, bf16[16,136,256]{2,1,0:T(8,128)(2,1)S(1)} %all-to-all-done.refs_4_.message, bf16[4,4096]{1,0:T(4,128)(2,1)S(1)} %copy-done, bf16[4,4,128,256]{3,2,1,0:T(8,128)(2,1)S(1)} %get-tuple-element.28.high, ...), custom_call_target="tpu_custom_call" | custom-call | flops 603979776 | bytes 12582912 | tf_op jit(solution)/shard_map/local/pallas_call | solution.py:418
  69.8 0.3 collective-permute-done.7.start
  70.0 1.9 %read.1 = (bf16[128,512]{1,0:T(8,128)(2,1)S(1)}, bf16[128,512]{1,0:T(8,128)(2,1)S(1)}, bf16[128,512]{1,0:T(8,128)(2,1)S(1)}, bf16[128,512]{1,0:T(8,128)(2,1)S(1)}) custom-call(s32[1]{0:T(128)} %bitcast.refs_0_.place, f32[4,4,128,128]{3,2,1,0:T(8,128)S(1)} %get-tuple-element.26.carry, f32[4,4,128,128]{3,2,1,0:T(8,128)S(1)} %get-tuple-element.27.add, ...), custom_call_target="tpu_custom_call" | custom-call | tf_op jit(solution)/shard_map/read/pallas_call | solution.py:461
  71.9 0.9 %collective-permute-start.8 = (bf16[128,512]{1,0:T(8,128)(2,1)S(1)}, bf16[128,512]{1,0:T(8,128)(2,1)S(1)}, u32[]{:S(2)}, u32[]{:S(2)}) collective-permute-start(bf16[128,512]{1,0:T(8,128)(2,1)S(1)} %get-tuple-element.38), channel_id=1, source_target_pairs={{0,4},{4,0},{8,12},{12,8},{1,5},{5,1},{9,13},{13,9},{2,6},{6,2},{1... | collective-permute-start | bytes 393224 | tf_op jit(solution)/shard_map/ppermute | solution.py:35
  72.8 4.0 %collective-permute-start.9 = (bf16[128,512]{1,0:T(8,128)(2,1)S(1)}, bf16[128,512]{1,0:T(8,128)(2,1)S(1)}, u32[]{:S(2)}, u32[]{:S(2)}) collective-permute-start(bf16[128,512]{1,0:T(8,128)(2,1)S(1)} %get-tuple-element.39), channel_id=1, source_target_pairs={{0,8},{4,12},{8,0},{12,4},{1,9},{5,13},{9,1},{13,5},{2,10},{6,14},... | collective-permute-start | bytes 393224 | tf_op jit(solution)/shard_map/ppermute | solution.py:35
  76.9 0.1 collective-permute-done.8.refs_1_
  76.9 4.3 %collective-permute-done.9.refs_2_ = bf16[128,512]{1,0:T(8,128)(2,1)S(1)} collective-permute-done((bf16[128,512]{1,0:T(8,128)(2,1)S(1)}, bf16[128,512]{1,0:T(8,128)(2,1)S(1)}, u32[]{:S(2)}, u32[]{:S(2)}) %collective-permute-start.9) | collective-permute-done | bytes 131104 | tf_op jit(solution)/shard_map/ppermute | solution.py:35
  81.2 1.6 %collective-permute-done.10.refs_3_ = bf16[128,512]{1,0:T(8,128)(2,1)S(1)} collective-permute-done((bf16[128,512]{1,0:T(8,128)(2,1)S(1)}, bf16[128,512]{1,0:T(8,128)(2,1)S(1)}, u32[]{:S(2)}, u32[]{:S(2)}) %collective-permute-start.10) | collective-permute-done | bytes 131104 | tf_op jit(solution)/shard_map/ppermute | solution.py:35
  82.8 0.9 %assemble.1 = bf16[1,128,2048]{2,1,0:T(8,128)(2,1)} custom-call(s32[1]{0:T(128)} %bitcast.refs_0_.place, bf16[128,512]{1,0:T(8,128)(2,1)S(1)} %get-tuple-element.37.refs_0_, bf16[128,512]{1,0:T(8,128)(2,1)S(1)} %collective-permute-done.8.refs_1_, bf16[128,512]{1,0:T(8,128)(2,1)S(1)} %collective-permute-done.9.refs_2_, ...), custom_call_target="tpu_custom_call" | custom-call | tf_op jit(solution)/shard_map/assemble/pallas_call | solution.py:484
  (15 shorter events, 0.0 us)
Async XLA Ops:
  0.0 15.1 %collective-permute-start = (bf16[128,2048]{1,0:T(8,128)(2,1)}, bf16[128,2048]{1,0:T(8,128)(2,1)S(1)}, u32[]{:S(2)}, u32[]{:S(2)}) collective-permute-start(bf16[128,2048]{1,0:T(8,128)(2,1)} %bitcast.9), channel_id=1, source_target_pairs={{0,2},{1,3},{2,0},{3,1},{4,6},{5,7},{6,4},{7,5},{8,10},{9,11},{10,... | collective-permute-start | bytes 1572872 | tf_op jit(solution)/shard_map/ppermute | solution.py:35
  3.0 22.1 %collective-permute-start.5 = (bf16[128,2048]{1,0:T(8,128)(2,1)}, bf16[128,2048]{1,0:T(8,128)(2,1)S(1)}, u32[]{:S(2)}, u32[]{:S(2)}) collective-permute-start(bf16[128,2048]{1,0:T(8,128)(2,1)} %bitcast.10), channel_id=1, source_target_pairs={{0,1},{1,0},{2,3},{3,2},{4,5},{5,4},{6,7},{7,6},{8,9},{9,8},{10,11... | collective-permute-start | bytes 1572872 | tf_op jit(solution)/shard_map/ppermute | solution.py:35
  15.1 15.3 %collective-permute-start.1 = (bf16[128,2048]{1,0:T(8,128)(2,1)S(1)}, bf16[128,2048]{1,0:T(8,128)(2,1)S(1)}, u32[]{:S(2)}, u32[]{:S(2)}) collective-permute-start(bf16[128,2048]{1,0:T(8,128)(2,1)S(1)} %collective-permute-done.refs_1_), channel_id=1, source_target_pairs={{0,1},{1,0},{2,3},{3,2},{4,5},{5,4},{6,7},{7,6},{8,9},{9,8},{10,11... | collective-permute-start | bytes 1572872 | tf_op jit(solution)/shard_map/ppermute | solution.py:35
  15.9 5.3 %collective-permute-start.2 = (bf16[8,2048]{1,0:T(8,128)(2,1)S(1)}, bf16[8,2048]{1,0:T(8,128)(2,1)S(1)}, u32[]{:S(2)}, u32[]{:S(2)}) collective-permute-start(bf16[8,2048]{1,0:T(8,128)(2,1)S(1)} %slice_bitcast_fusion), channel_id=1, source_target_pairs={{0,4},{4,8},{8,12},{12,16},{16,20},{20,24},{24,28},{1,5},{5,9},{9,... | collective-permute-start | bytes 98312 | tf_op jit(solution)/shard_map/ppermute | solution.py:30
  21.1 3.9 %collective-permute-start.3 = (bf16[8,2048]{1,0:T(8,128)(2,1)S(1)}, bf16[8,2048]{1,0:T(8,128)(2,1)S(1)}, u32[]{:S(2)}, u32[]{:S(2)}) collective-permute-start(bf16[8,2048]{1,0:T(8,128)(2,1)S(1)} %collective-permute-done.2.refs_3_), channel_id=1, source_target_pairs={{0,2},{1,3},{2,0},{3,1},{4,6},{5,7},{6,4},{7,5},{8,10},{9,11},{10,... | collective-permute-start | bytes 98312 | tf_op jit(solution)/shard_map/ppermute | solution.py:35
  22.6 2.4 %collective-permute-start.6 = (bf16[8,2048]{1,0:T(8,128)(2,1)S(1)}, bf16[8,2048]{1,0:T(8,128)(2,1)S(1)}, u32[]{:S(2)}, u32[]{:S(2)}) collective-permute-start(bf16[8,2048]{1,0:T(8,128)(2,1)S(1)} %collective-permute-done.2.refs_3_), channel_id=1, source_target_pairs={{0,1},{1,0},{2,3},{3,2},{4,5},{5,4},{6,7},{7,6},{8,9},{9,8},{10,11... | collective-permute-start | bytes 98312 | tf_op jit(solution)/shard_map/ppermute | solution.py:35
  25.0 5.4 %collective-permute-start.4 = (bf16[8,2048]{1,0:T(8,128)(2,1)S(1)}, bf16[8,2048]{1,0:T(8,128)(2,1)S(1)}, u32[]{:S(2)}, u32[]{:S(2)}) collective-permute-start(bf16[8,2048]{1,0:T(8,128)(2,1)S(1)} %collective-permute-done.3.refs_3_), channel_id=1, source_target_pairs={{0,1},{1,0},{2,3},{3,2},{4,5},{5,4},{6,7},{7,6},{8,9},{9,8},{10,11... | collective-permute-start | bytes 98312 | tf_op jit(solution)/shard_map/ppermute | solution.py:35
  32.9 22.8 %copy-start = (bf16[4,4096]{1,0:T(4,128)(2,1)S(1)}, bf16[4,4096]{1,0:T(4,128)(2,1)}, u32[]{:S(2)}) copy-start(bf16[4,4096]{1,0:T(4,128)(2,1)} %taps.1) | copy-start | bytes 98308
  32.9 22.8 %copy-start.1 = (f32[16]{0:T(128)S(1)}, f32[16]{0:T(128)}, u32[]{:S(2)}) copy-start(f32[16]{0:T(128)} %refs_1_.1) | copy-start | bytes 196
  32.9 22.8 %copy-start.2 = (f32[16]{0:T(128)S(1)}, f32[16]{0:T(128)}, u32[]{:S(2)}) copy-start(f32[16]{0:T(128)} %refs_2_.1) | copy-start | bytes 196
  32.9 22.7 %all-to-all-start = ((bf16[16,136,256]{2,1,0:T(8,128)(2,1)}), bf16[16,136,256]{2,1,0:T(8,128)(2,1)S(1)}, u32[]{:S(2)}, u32[]{:S(2)}) async-start(bf16[16,136,256]{2,1,0:T(8,128)(2,1)} %bitcast.5), calls=%async_computation | async-start | bytes 2228224 | tf_op jit(solution)/shard_map/all_to_all | solution.py:517
  63.0 7.0 %collective-permute-start.7 = (bf16[4,128,128]{2,1,0:T(8,128)(2,1)S(1)}, bf16[4,128,128]{2,1,0:T(8,128)(2,1)S(1)}, u32[]{:S(2)}, u32[]{:S(2)}) collective-permute-start(bf16[4,128,128]{2,1,0:T(8,128)(2,1)S(1)} %get-tuple-element.36), channel_id=1, source_target_pairs={{0,16},{1,17},{2,18},{3,19},{4,20},{5,21},{6,22},{7,23},{8,24},{9,... | collective-permute-start | bytes 393224 | tf_op jit(solution)/shard_map/ppermute | solution.py:30
  67.5 2.5 %copy-start.3 = (f32[128]{0:T(128)S(1)}, f32[128]{0:T(128)}, u32[]{:S(2)}) copy-start(f32[128]{0:T(128)} %param.13) | copy-start | bytes 1540
  71.9 5.0 %collective-permute-start.8 = (bf16[128,512]{1,0:T(8,128)(2,1)S(1)}, bf16[128,512]{1,0:T(8,128)(2,1)S(1)}, u32[]{:S(2)}, u32[]{:S(2)}) collective-permute-start(bf16[128,512]{1,0:T(8,128)(2,1)S(1)} %get-tuple-element.38), channel_id=1, source_target_pairs={{0,4},{4,0},{8,12},{12,8},{1,5},{5,1},{9,13},{13,9},{2,6},{6,2},{1... | collective-permute-start | bytes 393224 | tf_op jit(solution)/shard_map/ppermute | solution.py:35
  72.8 8.4 %collective-permute-start.9 = (bf16[128,512]{1,0:T(8,128)(2,1)S(1)}, bf16[128,512]{1,0:T(8,128)(2,1)S(1)}, u32[]{:S(2)}, u32[]{:S(2)}) collective-permute-start(bf16[128,512]{1,0:T(8,128)(2,1)S(1)} %get-tuple-element.39), channel_id=1, source_target_pairs={{0,8},{4,12},{8,0},{12,4},{1,9},{5,13},{9,1},{13,5},{2,10},{6,14},... | collective-permute-start | bytes 393224 | tf_op jit(solution)/shard_map/ppermute | solution.py:35
  76.9 5.9 %collective-permute-start.10 = (bf16[128,512]{1,0:T(8,128)(2,1)S(1)}, bf16[128,512]{1,0:T(8,128)(2,1)S(1)}, u32[]{:S(2)}, u32[]{:S(2)}) collective-permute-start(bf16[128,512]{1,0:T(8,128)(2,1)S(1)} %get-tuple-element.40), channel_id=1, source_target_pairs={{0,12},{4,8},{8,4},{12,0},{1,13},{5,9},{9,5},{13,1},{2,14},{6,10},... | collective-permute-start | bytes 393224 | tf_op jit(solution)/shard_map/ppermute | solution.py:35

commit v5 on v4

--- a/solution.py
+++ b/solution.py
@@ -202,16 +202,33 @@
     return totals
 
 
+def odd_blocks(value, size):
+    return jnp.concatenate([value[r : r + size] for r in range(size, CHUNK, 2 * size)], axis=0)
+
+
+def between(even, odd, size):
+    blocks = []
+    for r in range(0, CHUNK // 2, size):
+        blocks += [even[r : r + size], odd[r : r + size]]
+    return jnp.concatenate(blocks, axis=0)
+
+
 def inverses(lowers):
     totals = base_inverses(lowers)
-    row, column = iota((CHUNK, CHUNK), 0), iota((CHUNK, CHUNK), 1)
+    row, column = iota((CHUNK // 2, CHUNK), 0), iota((CHUNK // 2, CHUNK), 1)
+    blank = jnp.zeros((CHUNK // 2, CHUNK), BF16)
     size = BASE
     while size < CHUNK:
-        inside = (row // (2 * size) == column // (2 * size)) & (row // size > column // size)
+        inside = column // size == 2 * (row // size)
         parts = [halves(total) for total in totals]
-        corners = [halves(jnp.where(inside, lower, 0.0)) for lower in lowers]
+        corners = [halves(jnp.where(inside, odd_blocks(lower, size), 0.0)) for lower in lowers]
         inner = [halves(dot3(c, p)) for c, p in zip(corners, parts)]
-        totals = [t - dot3(p, i) for t, p, i in zip(totals, parts, inner)]
+        for i, total in enumerate(totals):
+            left = [odd_blocks(part, size) for part in parts[i]]
+            right = [between(blank, part, size) for part in inner[i]]
+            odd = odd_blocks(total, size) - dot3(left, right)
+            even = jnp.concatenate([total[r : r + size] for r in range(0, CHUNK, 2 * size)], axis=0)
+            totals[i] = between(even, odd, size)
         size *= 2
     return totals
 
@@ -430,29 +447,21 @@
 
 
 def read_kernel(place, carry, add, query, base, start, gain, *rest):
-    outs, state = rest[:-1], rest[-1]
+    outs, (stage, state) = rest[:-2], rest[-2:]
     state[...] = start[...].astype(F32)
-
-    def one(block, _):
-        results = []
+    for block in range(carry.shape[0]):
+        slot = jnp.bitwise_xor(block, place[0])
         for u in range(UNITS):
             left = jnp.concatenate([carry[block, u], query[block, u]], axis=0)
             both = dot3(halves(left), halves(state[u]))
             state[u] = both[:HEAD] + add[block, u]
             reads = both[HEAD:] + base[block, u]
             mean = jnp.mean(reads * reads, axis=-1, keepdims=True)
-            results.append((reads / jnp.sqrt(mean + 1e-06) * gain[...]).astype(BF16))
-        slot = jnp.bitwise_xor(block, place[0])
-        for k, out in enumerate(outs):
-
-            @pl.when(slot == k)
-            def _(out=out):
-                for u in range(UNITS):
-                    out[:, u * HEAD : (u + 1) * HEAD] = results[u]
-
-        return 0
-
-    lax.fori_loop(0, carry.shape[0], one, 0)
+            stage[slot, :, u * HEAD : (u + 1) * HEAD] = (
+                reads / jnp.sqrt(mean + 1e-06) * gain[...]
+            ).astype(BF16)
+    for k, out in enumerate(outs):
+        out[...] = stage[k]
 
 
 def read(place, carry, add, query, base, start, gain):
@@ -463,7 +472,10 @@
         in_specs=[pl.BlockSpec(memory_space=pltpu.SMEM)] + [vectors] * 6,
         out_specs=[vectors] * blocks,
         out_shape=[jax.ShapeDtypeStruct((rows, UNITS * HEAD), BF16)] * blocks,
-        scratch_shapes=[pltpu.VMEM(start.shape, F32)],
+        scratch_shapes=[
+            pltpu.VMEM((blocks, rows, UNITS * HEAD), BF16),
+            pltpu.VMEM(start.shape, F32),
+        ],
         compiler_params=pltpu.CompilerParams(vmem_limit_bytes=VMEM_LIMIT),
         name="read",
     )(place, carry, add, query, base, start, gain)

time: 84 us -> 83.4 us (level)
  no operation moved by 1% of the time
where the time goes in v5:
time: 83.4 us; the launch traced here: 83.1 us
  waiting for transfers between devices  39.2 us (47%)
  starting transfers between devices  23.5 us (28%)
  Pallas kernels  19.5 us (23%)
    ppermute x9, waiting for transfers between devices, swapped(): return lax.ppermute(value, axis, [(i, i ^ bit) for i in range(count)])  20.5 us
    all_to_all x1, waiting for transfers between devices, messages_direct(): return lax.all_to_all(message, ('sq', 'fsdp'), 0, 0, tiled=True)  16.8 us
    ppermute x9, starting transfers between devices, swapped(): return lax.ppermute(value, axis, [(i, i ^ bit) for i in range(count)])  9.42 us
    ppermute x2, starting transfers between devices, shifted(): return lax.ppermute(value, axes, pairs)  8.17 us
    pallas_call x2, Pallas kernels, project(): pl.pallas_call(lambda *refs: project_kernel(other, *refs), in_specs=in_sp...  7.78 us
    pallas_call x1, Pallas kernels, prepare(): pl.pallas_call(lambda *refs: prepare_kernel(seg_product, *refs), in_specs...  7.37 us
    all_to_all x1, starting transfers between devices, messages_direct(): return lax.all_to_all(message, ('sq', 'fsdp'), 0, 0, tiled=True)  5.89 us
    pallas_call x1, Pallas kernels, local(): pl.pallas_call(local_kernel, in_specs=[pl.BlockSpec(memory_space=pltpu.SM...  2.21 us
  transfers between devices with their start and end apart: 12, of which 8 were waited for; matrix products, arithmetic and copies ran while one was open for 1% of the time, Pallas kernels for 9%

profile of v5, /device:TPU:0, one launch (start us, length us, event | category | flops | bytes accessed | tf_op | source)
XLA Modules:
  0.0 83.1 jit_solution(8168549958793629601)
XLA Ops:
  0.0 3.0 %collective-permute-start = (bf16[128,2048]{1,0:T(8,128)(2,1)}, bf16[128,2048]{1,0:T(8,128)(2,1)S(1)}, u32[]{:S(2)}, u32[]{:S(2)}) collective-permute-start(bf16[128,2048]{1,0:T(8,128)(2,1)} %bitcast.9), channel_id=1, source_target_pairs={{0,2},{1,3},{2,0},{3,1},{4,6},{5,7},{6,4},{7,5},{8,10},{9,11},{10,... | collective-permute-start | bytes 1572872 | tf_op jit(solution)/shard_map/ppermute | solution.py:35
  3.0 12.1 %collective-permute-done.refs_1_ = bf16[128,2048]{1,0:T(8,128)(2,1)S(1)} collective-permute-done((bf16[128,2048]{1,0:T(8,128)(2,1)}, bf16[128,2048]{1,0:T(8,128)(2,1)S(1)}, u32[]{:S(2)}, u32[]{:S(2)}) %collective-permute-start) | collective-permute-done | bytes 524320 | tf_op jit(solution)/shard_map/ppermute | solution.py:35
  15.1 0.8 slice_bitcast_fusion
  15.9 3.7 %collective-permute-start.2 = (bf16[8,2048]{1,0:T(8,128)(2,1)S(1)}, bf16[8,2048]{1,0:T(8,128)(2,1)S(1)}, u32[]{:S(2)}, u32[]{:S(2)}) collective-permute-start(bf16[8,2048]{1,0:T(8,128)(2,1)S(1)} %slice_bitcast_fusion), channel_id=1, source_target_pairs={{0,4},{4,8},{8,12},{12,16},{16,20},{20,24},{24,28},{1,5},{5,9},{9,... | collective-permute-start | bytes 98312 | tf_op jit(solution)/shard_map/ppermute | solution.py:30
  19.5 1.6 %collective-permute-done.2.refs_3_ = bf16[8,2048]{1,0:T(8,128)(2,1)S(1)} collective-permute-done((bf16[8,2048]{1,0:T(8,128)(2,1)S(1)}, bf16[8,2048]{1,0:T(8,128)(2,1)S(1)}, u32[]{:S(2)}, u32[]{:S(2)}) %collective-permute-start.2) | collective-permute-done | bytes 32800 | tf_op jit(solution)/shard_map/ppermute | solution.py:30
  21.1 1.5 %collective-permute-start.3 = (bf16[8,2048]{1,0:T(8,128)(2,1)S(1)}, bf16[8,2048]{1,0:T(8,128)(2,1)S(1)}, u32[]{:S(2)}, u32[]{:S(2)}) collective-permute-start(bf16[8,2048]{1,0:T(8,128)(2,1)S(1)} %collective-permute-done.2.refs_3_), channel_id=1, source_target_pairs={{0,2},{1,3},{2,0},{3,1},{4,6},{5,7},{6,4},{7,5},{8,10},{9,11},{10,... | collective-permute-start | bytes 98312 | tf_op jit(solution)/shard_map/ppermute | solution.py:35
  22.6 2.4 %collective-permute-done.3.refs_3_ = bf16[8,2048]{1,0:T(8,128)(2,1)S(1)} collective-permute-done((bf16[8,2048]{1,0:T(8,128)(2,1)S(1)}, bf16[8,2048]{1,0:T(8,128)(2,1)S(1)}, u32[]{:S(2)}, u32[]{:S(2)}) %collective-permute-start.3) | collective-permute-done | bytes 32800 | tf_op jit(solution)/shard_map/ppermute | solution.py:35
  25.0 5.4 %project_own.1 = (bf16[4,4,136,256]{3,2,1,0:T(8,128)(2,1)}, bf16[2048,1024]{1,0:T(8,128)(2,1)S(1)}, bf16[32,2048]{1,0:T(8,128)(2,1)S(1)}) custom-call(s32[1]{0:T(128)} %bitcast.1.refs_0_, bf16[128,2048]{1,0:T(8,128)(2,1)} %bitcast.11, bf16[128,2048]{1,0:T(8,128)(2,1)S(1)} %collective-permute-done.5.refs_2_, ...), custom_call_target="tpu_custom_call" | custom-call | flops 1073741824 | bytes 6291456 | tf_op jit(solution)/shard_map/project_own/pallas_call | solution.py:154
  30.4 2.4 %project_other.1 = bf16[4,4,136,256]{3,2,1,0:T(8,128)(2,1)} custom-call(s32[1]{0:T(128)} %bitcast.1.refs_0_, bf16[128,2048]{1,0:T(8,128)(2,1)S(1)} %collective-permute-done.refs_1_, bf16[128,2048]{1,0:T(8,128)(2,1)S(1)} %collective-permute-done.1.refs_2_, bf16[8,2048]{1,0:T(8,128)(2,1)S(1)} %collective-permute-done.3.refs_3_, ...), custom_call_target="tpu_custom_call", output_to_operand_aliasing={{}: (7, {})} | custom-call | flops 1073741824 | bytes 6291456 | tf_op jit(solution)/shard_map/project_other/pallas_call | solution.py:154
  32.9 0.0 copy-start
  32.9 0.0 copy-start.1
  32.9 5.9 %all-to-all-start = ((bf16[16,136,256]{2,1,0:T(8,128)(2,1)}), bf16[16,136,256]{2,1,0:T(8,128)(2,1)S(1)}, u32[]{:S(2)}, u32[]{:S(2)}) async-start(bf16[16,136,256]{2,1,0:T(8,128)(2,1)} %bitcast.5), calls=%async_computation | async-start | bytes 2228224 | tf_op jit(solution)/shard_map/all_to_all | solution.py:529
  38.8 16.8 %all-to-all-done.refs_4_.message = bf16[16,136,256]{2,1,0:T(8,128)(2,1)S(1)} async-done(((bf16[16,136,256]{2,1,0:T(8,128)(2,1)}), bf16[16,136,256]{2,1,0:T(8,128)(2,1)S(1)}, u32[]{:S(2)}, u32[]{:S(2)}) %all-to-all-start) | async-done | bytes 1114144 | tf_op jit(solution)/shard_map/all_to_all | solution.py:529
  55.6 7.4 %prepare.1 = (f32[4,4,128,128]{3,2,1,0:T(8,128)S(1)}, f32[4,4,128,128]{3,2,1,0:T(8,128)S(1)}, bf16[4,4,128,256]{3,2,1,0:T(8,128)(2,1)S(1)}, bf16[4,4,128,256]{3,...) custom-call(s32[1]{0:T(128)} %bitcast.refs_0_.place, ...), custom_call_target="tpu_custom_call" | custom-call | tf_op jit(solution)/shard_map/prepare/pallas_call | solution.py:394
  63.0 4.5 %collective-permute-start.7 = (bf16[4,128,128]{2,1,0:T(8,128)(2,1)S(1)}, bf16[4,128,128]{2,1,0:T(8,128)(2,1)S(1)}, u32[]{:S(2)}, u32[]{:S(2)}) collective-permute-start(bf16[4,128,128]{2,1,0:T(8,128)(2,1)S(1)} %get-tuple-element.36), channel_id=1, source_target_pairs={{0,16},{1,17},{2,18},{3,19},{4,20},{5,21},{6,22},{7,23},{8,24},{9,... | collective-permute-start | bytes 393224 | tf_op jit(solution)/shard_map/ppermute | solution.py:30
  67.5 2.2 %local.1 = (f32[4,4,128,128]{3,2,1,0:T(8,128)S(1)}, f32[4,4,128,128]{3,2,1,0:T(8,128)S(1)}) custom-call(s32[1]{0:T(128)} %bitcast.refs_0_.place, bf16[16,136,256]{2,1,0:T(8,128)(2,1)S(1)} %all-to-all-done.refs_4_.message, bf16[4,4096]{1,0:T(4,128)(2,1)S(1)} %copy-done, bf16[4,4,128,256]{3,2,1,0:T(8,128)(2,1)S(1)} %get-tuple-element.28.high, ...), custom_call_target="tpu_custom_call" | custom-call | flops 603979776 | bytes 12582912 | tf_op jit(solution)/shard_map/local/pallas_call | solution.py:435
  69.8 0.3 collective-permute-done.7.start
  70.0 1.3 %read.1 = (bf16[128,512]{1,0:T(8,128)(2,1)S(1)}, bf16[128,512]{1,0:T(8,128)(2,1)S(1)}, bf16[128,512]{1,0:T(8,128)(2,1)S(1)}, bf16[128,512]{1,0:T(8,128)(2,1)S(1)}) custom-call(s32[1]{0:T(128)} %bitcast.refs_0_.place, f32[4,4,128,128]{3,2,1,0:T(8,128)S(1)} %get-tuple-element.26.carry, f32[4,4,128,128]{3,2,1,0:T(8,128)S(1)} %get-tuple-element.27.add, ...), custom_call_target="tpu_custom_call" | custom-call | tf_op jit(solution)/shard_map/read/pallas_call | solution.py:470
  71.3 0.9 %collective-permute-start.8 = (bf16[128,512]{1,0:T(8,128)(2,1)S(1)}, bf16[128,512]{1,0:T(8,128)(2,1)S(1)}, u32[]{:S(2)}, u32[]{:S(2)}) collective-permute-start(bf16[128,512]{1,0:T(8,128)(2,1)S(1)} %get-tuple-element.38), channel_id=1, source_target_pairs={{0,4},{4,0},{8,12},{12,8},{1,5},{5,1},{9,13},{13,9},{2,6},{6,2},{1... | collective-permute-start | bytes 393224 | tf_op jit(solution)/shard_map/ppermute | solution.py:35
  72.2 4.0 %collective-permute-start.9 = (bf16[128,512]{1,0:T(8,128)(2,1)S(1)}, bf16[128,512]{1,0:T(8,128)(2,1)S(1)}, u32[]{:S(2)}, u32[]{:S(2)}) collective-permute-start(bf16[128,512]{1,0:T(8,128)(2,1)S(1)} %get-tuple-element.39), channel_id=1, source_target_pairs={{0,8},{4,12},{8,0},{12,4},{1,9},{5,13},{9,1},{13,5},{2,10},{6,14},... | collective-permute-start | bytes 393224 | tf_op jit(solution)/shard_map/ppermute | solution.py:35
  76.2 0.1 collective-permute-done.8.refs_1_
  76.3 4.3 %collective-permute-done.9.refs_2_ = bf16[128,512]{1,0:T(8,128)(2,1)S(1)} collective-permute-done((bf16[128,512]{1,0:T(8,128)(2,1)S(1)}, bf16[128,512]{1,0:T(8,128)(2,1)S(1)}, u32[]{:S(2)}, u32[]{:S(2)}) %collective-permute-start.9) | collective-permute-done | bytes 131104 | tf_op jit(solution)/shard_map/ppermute | solution.py:35
  80.6 1.6 %collective-permute-done.10.refs_3_ = bf16[128,512]{1,0:T(8,128)(2,1)S(1)} collective-permute-done((bf16[128,512]{1,0:T(8,128)(2,1)S(1)}, bf16[128,512]{1,0:T(8,128)(2,1)S(1)}, u32[]{:S(2)}, u32[]{:S(2)}) %collective-permute-start.10) | collective-permute-done | bytes 131104 | tf_op jit(solution)/shard_map/ppermute | solution.py:35
  82.2 0.9 %assemble.1 = bf16[1,128,2048]{2,1,0:T(8,128)(2,1)} custom-call(s32[1]{0:T(128)} %bitcast.refs_0_.place, bf16[128,512]{1,0:T(8,128)(2,1)S(1)} %get-tuple-element.37.refs_0_, bf16[128,512]{1,0:T(8,128)(2,1)S(1)} %collective-permute-done.8.refs_1_, bf16[128,512]{1,0:T(8,128)(2,1)S(1)} %collective-permute-done.9.refs_2_, ...), custom_call_target="tpu_custom_call" | custom-call | tf_op jit(solution)/shard_map/assemble/pallas_call | solution.py:496
  (15 shorter events, 0.0 us)
Async XLA Ops:
  0.0 15.1 %collective-permute-start = (bf16[128,2048]{1,0:T(8,128)(2,1)}, bf16[128,2048]{1,0:T(8,128)(2,1)S(1)}, u32[]{:S(2)}, u32[]{:S(2)}) collective-permute-start(bf16[128,2048]{1,0:T(8,128)(2,1)} %bitcast.9), channel_id=1, source_target_pairs={{0,2},{1,3},{2,0},{3,1},{4,6},{5,7},{6,4},{7,5},{8,10},{9,11},{10,... | collective-permute-start | bytes 1572872 | tf_op jit(solution)/shard_map/ppermute | solution.py:35
  3.0 22.1 %collective-permute-start.5 = (bf16[128,2048]{1,0:T(8,128)(2,1)}, bf16[128,2048]{1,0:T(8,128)(2,1)S(1)}, u32[]{:S(2)}, u32[]{:S(2)}) collective-permute-start(bf16[128,2048]{1,0:T(8,128)(2,1)} %bitcast.10), channel_id=1, source_target_pairs={{0,1},{1,0},{2,3},{3,2},{4,5},{5,4},{6,7},{7,6},{8,9},{9,8},{10,11... | collective-permute-start | bytes 1572872 | tf_op jit(solution)/shard_map/ppermute | solution.py:35
  15.1 15.3 %collective-permute-start.1 = (bf16[128,2048]{1,0:T(8,128)(2,1)S(1)}, bf16[128,2048]{1,0:T(8,128)(2,1)S(1)}, u32[]{:S(2)}, u32[]{:S(2)}) collective-permute-start(bf16[128,2048]{1,0:T(8,128)(2,1)S(1)} %collective-permute-done.refs_1_), channel_id=1, source_target_pairs={{0,1},{1,0},{2,3},{3,2},{4,5},{5,4},{6,7},{7,6},{8,9},{9,8},{10,11... | collective-permute-start | bytes 1572872 | tf_op jit(solution)/shard_map/ppermute | solution.py:35
  15.9 5.3 %collective-permute-start.2 = (bf16[8,2048]{1,0:T(8,128)(2,1)S(1)}, bf16[8,2048]{1,0:T(8,128)(2,1)S(1)}, u32[]{:S(2)}, u32[]{:S(2)}) collective-permute-start(bf16[8,2048]{1,0:T(8,128)(2,1)S(1)} %slice_bitcast_fusion), channel_id=1, source_target_pairs={{0,4},{4,8},{8,12},{12,16},{16,20},{20,24},{24,28},{1,5},{5,9},{9,... | collective-permute-start | bytes 98312 | tf_op jit(solution)/shard_map/ppermute | solution.py:30
  21.1 3.9 %collective-permute-start.3 = (bf16[8,2048]{1,0:T(8,128)(2,1)S(1)}, bf16[8,2048]{1,0:T(8,128)(2,1)S(1)}, u32[]{:S(2)}, u32[]{:S(2)}) collective-permute-start(bf16[8,2048]{1,0:T(8,128)(2,1)S(1)} %collective-permute-done.2.refs_3_), channel_id=1, source_target_pairs={{0,2},{1,3},{2,0},{3,1},{4,6},{5,7},{6,4},{7,5},{8,10},{9,11},{10,... | collective-permute-start | bytes 98312 | tf_op jit(solution)/shard_map/ppermute | solution.py:35
  22.6 2.4 %collective-permute-start.6 = (bf16[8,2048]{1,0:T(8,128)(2,1)S(1)}, bf16[8,2048]{1,0:T(8,128)(2,1)S(1)}, u32[]{:S(2)}, u32[]{:S(2)}) collective-permute-start(bf16[8,2048]{1,0:T(8,128)(2,1)S(1)} %collective-permute-done.2.refs_3_), channel_id=1, source_target_pairs={{0,1},{1,0},{2,3},{3,2},{4,5},{5,4},{6,7},{7,6},{8,9},{9,8},{10,11... | collective-permute-start | bytes 98312 | tf_op jit(solution)/shard_map/ppermute | solution.py:35
  25.0 5.4 %collective-permute-start.4 = (bf16[8,2048]{1,0:T(8,128)(2,1)S(1)}, bf16[8,2048]{1,0:T(8,128)(2,1)S(1)}, u32[]{:S(2)}, u32[]{:S(2)}) collective-permute-start(bf16[8,2048]{1,0:T(8,128)(2,1)S(1)} %collective-permute-done.3.refs_3_), channel_id=1, source_target_pairs={{0,1},{1,0},{2,3},{3,2},{4,5},{5,4},{6,7},{7,6},{8,9},{9,8},{10,11... | collective-permute-start | bytes 98312 | tf_op jit(solution)/shard_map/ppermute | solution.py:35
  32.9 22.8 %copy-start = (bf16[4,4096]{1,0:T(4,128)(2,1)S(1)}, bf16[4,4096]{1,0:T(4,128)(2,1)}, u32[]{:S(2)}) copy-start(bf16[4,4096]{1,0:T(4,128)(2,1)} %taps.1) | copy-start | bytes 98308
  32.9 22.8 %copy-start.1 = (f32[16]{0:T(128)S(1)}, f32[16]{0:T(128)}, u32[]{:S(2)}) copy-start(f32[16]{0:T(128)} %refs_1_.1) | copy-start | bytes 196
  32.9 22.8 %copy-start.2 = (f32[16]{0:T(128)S(1)}, f32[16]{0:T(128)}, u32[]{:S(2)}) copy-start(f32[16]{0:T(128)} %refs_2_.1) | copy-start | bytes 196
  32.9 22.7 %all-to-all-start = ((bf16[16,136,256]{2,1,0:T(8,128)(2,1)}), bf16[16,136,256]{2,1,0:T(8,128)(2,1)S(1)}, u32[]{:S(2)}, u32[]{:S(2)}) async-start(bf16[16,136,256]{2,1,0:T(8,128)(2,1)} %bitcast.5), calls=%async_computation | async-start | bytes 2228224 | tf_op jit(solution)/shard_map/all_to_all | solution.py:529
  63.0 7.0 %collective-permute-start.7 = (bf16[4,128,128]{2,1,0:T(8,128)(2,1)S(1)}, bf16[4,128,128]{2,1,0:T(8,128)(2,1)S(1)}, u32[]{:S(2)}, u32[]{:S(2)}) collective-permute-start(bf16[4,128,128]{2,1,0:T(8,128)(2,1)S(1)} %get-tuple-element.36), channel_id=1, source_target_pairs={{0,16},{1,17},{2,18},{3,19},{4,20},{5,21},{6,22},{7,23},{8,24},{9,... | collective-permute-start | bytes 393224 | tf_op jit(solution)/shard_map/ppermute | solution.py:30
  67.5 2.5 %copy-start.3 = (f32[128]{0:T(128)S(1)}, f32[128]{0:T(128)}, u32[]{:S(2)}) copy-start(f32[128]{0:T(128)} %param.13) | copy-start | bytes 1540
  71.3 5.0 %collective-permute-start.8 = (bf16[128,512]{1,0:T(8,128)(2,1)S(1)}, bf16[128,512]{1,0:T(8,128)(2,1)S(1)}, u32[]{:S(2)}, u32[]{:S(2)}) collective-permute-start(bf16[128,512]{1,0:T(8,128)(2,1)S(1)} %get-tuple-element.38), channel_id=1, source_target_pairs={{0,4},{4,0},{8,12},{12,8},{1,5},{5,1},{9,13},{13,9},{2,6},{6,2},{1... | collective-permute-start | bytes 393224 | tf_op jit(solution)/shard_map/ppermute | solution.py:35
  72.2 8.4 %collective-permute-start.9 = (bf16[128,512]{1,0:T(8,128)(2,1)S(1)}, bf16[128,512]{1,0:T(8,128)(2,1)S(1)}, u32[]{:S(2)}, u32[]{:S(2)}) collective-permute-start(bf16[128,512]{1,0:T(8,128)(2,1)S(1)} %get-tuple-element.39), channel_id=1, source_target_pairs={{0,8},{4,12},{8,0},{12,4},{1,9},{5,13},{9,1},{13,5},{2,10},{6,14},... | collective-permute-start | bytes 393224 | tf_op jit(solution)/shard_map/ppermute | solution.py:35
  76.2 6.0 %collective-permute-start.10 = (bf16[128,512]{1,0:T(8,128)(2,1)S(1)}, bf16[128,512]{1,0:T(8,128)(2,1)S(1)}, u32[]{:S(2)}, u32[]{:S(2)}) collective-permute-start(bf16[128,512]{1,0:T(8,128)(2,1)S(1)} %get-tuple-element.40), channel_id=1, source_target_pairs={{0,12},{4,8},{8,4},{12,0},{1,13},{5,9},{9,5},{13,1},{2,14},{6,10},... | collective-permute-start | bytes 393224 | tf_op jit(solution)/shard_map/ppermute | solution.py:35

commit v6 on v5

--- a/solution.py
+++ b/solution.py
@@ -53,6 +53,12 @@
     both = dot(jnp.concatenate(a, axis=1), right)
     width = b[0].shape[1]
     return both[:, :width] + both[:, width:]
+
+
+def dot3_stacked(a, b):
+    rows, width = a[0].shape[0], b[0].shape[1]
+    both = dot(jnp.concatenate(a, axis=0), jnp.concatenate(b, axis=1))
+    return both[:rows, :width] + (both[:rows, width:] + both[rows:, :width])
 
 
 def split3(a):
@@ -222,11 +228,11 @@
         inside = column // size == 2 * (row // size)
         parts = [halves(total) for total in totals]
         corners = [halves(jnp.where(inside, odd_blocks(lower, size), 0.0)) for lower in lowers]
-        inner = [halves(dot3(c, p)) for c, p in zip(corners, parts)]
+        inner = [halves(dot3_stacked(c, p)) for c, p in zip(corners, parts)]
         for i, total in enumerate(totals):
             left = [odd_blocks(part, size) for part in parts[i]]
             right = [between(blank, part, size) for part in inner[i]]
-            odd = odd_blocks(total, size) - dot3(left, right)
+            odd = odd_blocks(total, size) - dot3_stacked(left, right)
             even = jnp.concatenate([total[r : r + size] for r in range(0, CHUNK, 2 * size)], axis=0)
             totals[i] = between(even, odd, size)
         size *= 2
@@ -307,7 +313,7 @@
                 keys_t.append(key.T)
                 parts = halves(keys_t[-1])
                 key_high[block, h], key_low[block, h] = parts
-                scores.append(dot3(halves(key), parts))
+                scores.append(dot3_stacked(halves(key), parts))
         growths, strengths, lasts, trailings, lowers = [], [], [], [], []
         for i, block in enumerate(group):
             growth_all = jnp.exp(turned[:rows, 2 * UNITS * i : 2 * UNITS * (i + 1)])
@@ -354,7 +360,7 @@
         for i in range(GROUPED):
             for u in range(UNITS):
                 at = UNITS * i + u
-                state[u] = dot3(carries[at], halves(state[u])) + adds[at]
+                state[u] = dot3_stacked(carries[at], halves(state[u])) + adds[at]
                 if seg_product:
                     product[u] = dot3(carries[at], halves(product[u]))
         return 0

time: 83.4 us -> 83.1 us (level)
  no operation moved by 1% of the time
where the time goes in v6:
time: 83.1 us; the launch traced here: 82.8 us
  waiting for transfers between devices  39.2 us (47%)
  starting transfers between devices  23.5 us (28%)
  Pallas kernels  19.2 us (23%)
    ppermute x9, waiting for transfers between devices, swapped(): return lax.ppermute(value, axis, [(i, i ^ bit) for i in range(count)])  20.5 us
    all_to_all x1, waiting for transfers between devices, messages_direct(): return lax.all_to_all(message, ('sq', 'fsdp'), 0, 0, tiled=True)  16.8 us
    ppermute x9, starting transfers between devices, swapped(): return lax.ppermute(value, axis, [(i, i ^ bit) for i in range(count)])  9.42 us
    ppermute x2, starting transfers between devices, shifted(): return lax.ppermute(value, axes, pairs)  8.17 us
    pallas_call x2, Pallas kernels, project(): pl.pallas_call(lambda *refs: project_kernel(other, *refs), in_specs=in_sp...  7.78 us
    pallas_call x1, Pallas kernels, prepare(): pl.pallas_call(lambda *refs: prepare_kernel(seg_product, *refs), in_specs...  7.09 us
    all_to_all x1, starting transfers between devices, messages_direct(): return lax.all_to_all(message, ('sq', 'fsdp'), 0, 0, tiled=True)  5.89 us
    pallas_call x1, Pallas kernels, local(): pl.pallas_call(local_kernel, in_specs=[pl.BlockSpec(memory_space=pltpu.SM...  2.21 us
  transfers between devices with their start and end apart: 12, of which 8 were waited for; matrix products, arithmetic and copies ran while one was open for 1% of the time, Pallas kernels for 9%

profile of v6, /device:TPU:0, one launch (start us, length us, event | category | flops | bytes accessed | tf_op | source)
XLA Modules:
  0.0 82.8 jit_solution(10676269245710657346)
XLA Ops:
  0.0 3.0 %collective-permute-start = (bf16[128,2048]{1,0:T(8,128)(2,1)}, bf16[128,2048]{1,0:T(8,128)(2,1)S(1)}, u32[]{:S(2)}, u32[]{:S(2)}) collective-permute-start(bf16[128,2048]{1,0:T(8,128)(2,1)} %bitcast.9), channel_id=1, source_target_pairs={{0,2},{1,3},{2,0},{3,1},{4,6},{5,7},{6,4},{7,5},{8,10},{9,11},{10,... | collective-permute-start | bytes 1572872 | tf_op jit(solution)/shard_map/ppermute | solution.py:35
  3.0 12.1 %collective-permute-done.refs_1_ = bf16[128,2048]{1,0:T(8,128)(2,1)S(1)} collective-permute-done((bf16[128,2048]{1,0:T(8,128)(2,1)}, bf16[128,2048]{1,0:T(8,128)(2,1)S(1)}, u32[]{:S(2)}, u32[]{:S(2)}) %collective-permute-start) | collective-permute-done | bytes 524320 | tf_op jit(solution)/shard_map/ppermute | solution.py:35
  15.1 0.8 slice_bitcast_fusion
  15.9 3.7 %collective-permute-start.2 = (bf16[8,2048]{1,0:T(8,128)(2,1)S(1)}, bf16[8,2048]{1,0:T(8,128)(2,1)S(1)}, u32[]{:S(2)}, u32[]{:S(2)}) collective-permute-start(bf16[8,2048]{1,0:T(8,128)(2,1)S(1)} %slice_bitcast_fusion), channel_id=1, source_target_pairs={{0,4},{4,8},{8,12},{12,16},{16,20},{20,24},{24,28},{1,5},{5,9},{9,... | collective-permute-start | bytes 98312 | tf_op jit(solution)/shard_map/ppermute | solution.py:30
  19.5 1.6 %collective-permute-done.2.refs_3_ = bf16[8,2048]{1,0:T(8,128)(2,1)S(1)} collective-permute-done((bf16[8,2048]{1,0:T(8,128)(2,1)S(1)}, bf16[8,2048]{1,0:T(8,128)(2,1)S(1)}, u32[]{:S(2)}, u32[]{:S(2)}) %collective-permute-start.2) | collective-permute-done | bytes 32800 | tf_op jit(solution)/shard_map/ppermute | solution.py:30
  21.1 1.5 %collective-permute-start.3 = (bf16[8,2048]{1,0:T(8,128)(2,1)S(1)}, bf16[8,2048]{1,0:T(8,128)(2,1)S(1)}, u32[]{:S(2)}, u32[]{:S(2)}) collective-permute-start(bf16[8,2048]{1,0:T(8,128)(2,1)S(1)} %collective-permute-done.2.refs_3_), channel_id=1, source_target_pairs={{0,2},{1,3},{2,0},{3,1},{4,6},{5,7},{6,4},{7,5},{8,10},{9,11},{10,... | collective-permute-start | bytes 98312 | tf_op jit(solution)/shard_map/ppermute | solution.py:35
  22.6 2.4 %collective-permute-done.3.refs_3_ = bf16[8,2048]{1,0:T(8,128)(2,1)S(1)} collective-permute-done((bf16[8,2048]{1,0:T(8,128)(2,1)S(1)}, bf16[8,2048]{1,0:T(8,128)(2,1)S(1)}, u32[]{:S(2)}, u32[]{:S(2)}) %collective-permute-start.3) | collective-permute-done | bytes 32800 | tf_op jit(solution)/shard_map/ppermute | solution.py:35
  25.0 5.4 %project_own.1 = (bf16[4,4,136,256]{3,2,1,0:T(8,128)(2,1)}, bf16[2048,1024]{1,0:T(8,128)(2,1)S(1)}, bf16[32,2048]{1,0:T(8,128)(2,1)S(1)}) custom-call(s32[1]{0:T(128)} %bitcast.1.refs_0_, bf16[128,2048]{1,0:T(8,128)(2,1)} %bitcast.11, bf16[128,2048]{1,0:T(8,128)(2,1)S(1)} %collective-permute-done.5.refs_2_, ...), custom_call_target="tpu_custom_call" | custom-call | flops 1073741824 | bytes 6291456 | tf_op jit(solution)/shard_map/project_own/pallas_call | solution.py:160
  30.4 2.4 %project_other.1 = bf16[4,4,136,256]{3,2,1,0:T(8,128)(2,1)} custom-call(s32[1]{0:T(128)} %bitcast.1.refs_0_, bf16[128,2048]{1,0:T(8,128)(2,1)S(1)} %collective-permute-done.refs_1_, bf16[128,2048]{1,0:T(8,128)(2,1)S(1)} %collective-permute-done.1.refs_2_, bf16[8,2048]{1,0:T(8,128)(2,1)S(1)} %collective-permute-done.3.refs_3_, ...), custom_call_target="tpu_custom_call", output_to_operand_aliasing={{}: (7, {})} | custom-call | flops 1073741824 | bytes 6291456 | tf_op jit(solution)/shard_map/project_other/pallas_call | solution.py:160
  32.9 0.0 copy-start
  32.9 0.0 copy-start.1
  32.9 5.9 %all-to-all-start = ((bf16[16,136,256]{2,1,0:T(8,128)(2,1)}), bf16[16,136,256]{2,1,0:T(8,128)(2,1)S(1)}, u32[]{:S(2)}, u32[]{:S(2)}) async-start(bf16[16,136,256]{2,1,0:T(8,128)(2,1)} %bitcast.5), calls=%async_computation | async-start | bytes 2228224 | tf_op jit(solution)/shard_map/all_to_all | solution.py:535
  38.8 16.8 %all-to-all-done.refs_4_.message = bf16[16,136,256]{2,1,0:T(8,128)(2,1)S(1)} async-done(((bf16[16,136,256]{2,1,0:T(8,128)(2,1)}), bf16[16,136,256]{2,1,0:T(8,128)(2,1)S(1)}, u32[]{:S(2)}, u32[]{:S(2)}) %all-to-all-start) | async-done | bytes 1114144 | tf_op jit(solution)/shard_map/all_to_all | solution.py:535
  55.6 7.1 %prepare.1 = (f32[4,4,128,128]{3,2,1,0:T(8,128)S(1)}, f32[4,4,128,128]{3,2,1,0:T(8,128)S(1)}, bf16[4,4,128,256]{3,2,1,0:T(8,128)(2,1)S(1)}, bf16[4,4,128,256]{3,...) custom-call(s32[1]{0:T(128)} %bitcast.refs_0_.place, ...), custom_call_target="tpu_custom_call" | custom-call | tf_op jit(solution)/shard_map/prepare/pallas_call | solution.py:400
  62.7 4.5 %collective-permute-start.7 = (bf16[4,128,128]{2,1,0:T(8,128)(2,1)S(1)}, bf16[4,128,128]{2,1,0:T(8,128)(2,1)S(1)}, u32[]{:S(2)}, u32[]{:S(2)}) collective-permute-start(bf16[4,128,128]{2,1,0:T(8,128)(2,1)S(1)} %get-tuple-element.36), channel_id=1, source_target_pairs={{0,16},{1,17},{2,18},{3,19},{4,20},{5,21},{6,22},{7,23},{8,24},{9,... | collective-permute-start | bytes 393224 | tf_op jit(solution)/shard_map/ppermute | solution.py:30
  67.3 2.2 %local.1 = (f32[4,4,128,128]{3,2,1,0:T(8,128)S(1)}, f32[4,4,128,128]{3,2,1,0:T(8,128)S(1)}) custom-call(s32[1]{0:T(128)} %bitcast.refs_0_.place, bf16[16,136,256]{2,1,0:T(8,128)(2,1)S(1)} %all-to-all-done.refs_4_.message, bf16[4,4096]{1,0:T(4,128)(2,1)S(1)} %copy-done, bf16[4,4,128,256]{3,2,1,0:T(8,128)(2,1)S(1)} %get-tuple-element.28.high, ...), custom_call_target="tpu_custom_call" | custom-call | flops 603979776 | bytes 12582912 | tf_op jit(solution)/shard_map/local/pallas_call | solution.py:441
  69.5 0.3 collective-permute-done.7.start
  69.7 1.3 %read.1 = (bf16[128,512]{1,0:T(8,128)(2,1)S(1)}, bf16[128,512]{1,0:T(8,128)(2,1)S(1)}, bf16[128,512]{1,0:T(8,128)(2,1)S(1)}, bf16[128,512]{1,0:T(8,128)(2,1)S(1)}) custom-call(s32[1]{0:T(128)} %bitcast.refs_0_.place, f32[4,4,128,128]{3,2,1,0:T(8,128)S(1)} %get-tuple-element.26.carry, f32[4,4,128,128]{3,2,1,0:T(8,128)S(1)} %get-tuple-element.27.add, ...), custom_call_target="tpu_custom_call" | custom-call | tf_op jit(solution)/shard_map/read/pallas_call | solution.py:476
  71.0 0.9 %collective-permute-start.8 = (bf16[128,512]{1,0:T(8,128)(2,1)S(1)}, bf16[128,512]{1,0:T(8,128)(2,1)S(1)}, u32[]{:S(2)}, u32[]{:S(2)}) collective-permute-start(bf16[128,512]{1,0:T(8,128)(2,1)S(1)} %get-tuple-element.38), channel_id=1, source_target_pairs={{0,4},{4,0},{8,12},{12,8},{1,5},{5,1},{9,13},{13,9},{2,6},{6,2},{1... | collective-permute-start | bytes 393224 | tf_op jit(solution)/shard_map/ppermute | solution.py:35
  71.9 4.0 %collective-permute-start.9 = (bf16[128,512]{1,0:T(8,128)(2,1)S(1)}, bf16[128,512]{1,0:T(8,128)(2,1)S(1)}, u32[]{:S(2)}, u32[]{:S(2)}) collective-permute-start(bf16[128,512]{1,0:T(8,128)(2,1)S(1)} %get-tuple-element.39), channel_id=1, source_target_pairs={{0,8},{4,12},{8,0},{12,4},{1,9},{5,13},{9,1},{13,5},{2,10},{6,14},... | collective-permute-start | bytes 393224 | tf_op jit(solution)/shard_map/ppermute | solution.py:35
  76.0 0.1 collective-permute-done.8.refs_1_
  76.0 4.3 %collective-permute-done.9.refs_2_ = bf16[128,512]{1,0:T(8,128)(2,1)S(1)} collective-permute-done((bf16[128,512]{1,0:T(8,128)(2,1)S(1)}, bf16[128,512]{1,0:T(8,128)(2,1)S(1)}, u32[]{:S(2)}, u32[]{:S(2)}) %collective-permute-start.9) | collective-permute-done | bytes 131104 | tf_op jit(solution)/shard_map/ppermute | solution.py:35
  80.3 1.6 %collective-permute-done.10.refs_3_ = bf16[128,512]{1,0:T(8,128)(2,1)S(1)} collective-permute-done((bf16[128,512]{1,0:T(8,128)(2,1)S(1)}, bf16[128,512]{1,0:T(8,128)(2,1)S(1)}, u32[]{:S(2)}, u32[]{:S(2)}) %collective-permute-start.10) | collective-permute-done | bytes 131104 | tf_op jit(solution)/shard_map/ppermute | solution.py:35
  81.9 0.9 %assemble.1 = bf16[1,128,2048]{2,1,0:T(8,128)(2,1)} custom-call(s32[1]{0:T(128)} %bitcast.refs_0_.place, bf16[128,512]{1,0:T(8,128)(2,1)S(1)} %get-tuple-element.37.refs_0_, bf16[128,512]{1,0:T(8,128)(2,1)S(1)} %collective-permute-done.8.refs_1_, bf16[128,512]{1,0:T(8,128)(2,1)S(1)} %collective-permute-done.9.refs_2_, ...), custom_call_target="tpu_custom_call" | custom-call | tf_op jit(solution)/shard_map/assemble/pallas_call | solution.py:502
  (15 shorter events, 0.0 us)
Async XLA Ops:
  0.0 15.1 %collective-permute-start = (bf16[128,2048]{1,0:T(8,128)(2,1)}, bf16[128,2048]{1,0:T(8,128)(2,1)S(1)}, u32[]{:S(2)}, u32[]{:S(2)}) collective-permute-start(bf16[128,2048]{1,0:T(8,128)(2,1)} %bitcast.9), channel_id=1, source_target_pairs={{0,2},{1,3},{2,0},{3,1},{4,6},{5,7},{6,4},{7,5},{8,10},{9,11},{10,... | collective-permute-start | bytes 1572872 | tf_op jit(solution)/shard_map/ppermute | solution.py:35
  3.0 22.1 %collective-permute-start.5 = (bf16[128,2048]{1,0:T(8,128)(2,1)}, bf16[128,2048]{1,0:T(8,128)(2,1)S(1)}, u32[]{:S(2)}, u32[]{:S(2)}) collective-permute-start(bf16[128,2048]{1,0:T(8,128)(2,1)} %bitcast.10), channel_id=1, source_target_pairs={{0,1},{1,0},{2,3},{3,2},{4,5},{5,4},{6,7},{7,6},{8,9},{9,8},{10,11... | collective-permute-start | bytes 1572872 | tf_op jit(solution)/shard_map/ppermute | solution.py:35
  15.1 15.3 %collective-permute-start.1 = (bf16[128,2048]{1,0:T(8,128)(2,1)S(1)}, bf16[128,2048]{1,0:T(8,128)(2,1)S(1)}, u32[]{:S(2)}, u32[]{:S(2)}) collective-permute-start(bf16[128,2048]{1,0:T(8,128)(2,1)S(1)} %collective-permute-done.refs_1_), channel_id=1, source_target_pairs={{0,1},{1,0},{2,3},{3,2},{4,5},{5,4},{6,7},{7,6},{8,9},{9,8},{10,11... | collective-permute-start | bytes 1572872 | tf_op jit(solution)/shard_map/ppermute | solution.py:35
  15.9 5.3 %collective-permute-start.2 = (bf16[8,2048]{1,0:T(8,128)(2,1)S(1)}, bf16[8,2048]{1,0:T(8,128)(2,1)S(1)}, u32[]{:S(2)}, u32[]{:S(2)}) collective-permute-start(bf16[8,2048]{1,0:T(8,128)(2,1)S(1)} %slice_bitcast_fusion), channel_id=1, source_target_pairs={{0,4},{4,8},{8,12},{12,16},{16,20},{20,24},{24,28},{1,5},{5,9},{9,... | collective-permute-start | bytes 98312 | tf_op jit(solution)/shard_map/ppermute | solution.py:30
  21.1 3.9 %collective-permute-start.3 = (bf16[8,2048]{1,0:T(8,128)(2,1)S(1)}, bf16[8,2048]{1,0:T(8,128)(2,1)S(1)}, u32[]{:S(2)}, u32[]{:S(2)}) collective-permute-start(bf16[8,2048]{1,0:T(8,128)(2,1)S(1)} %collective-permute-done.2.refs_3_), channel_id=1, source_target_pairs={{0,2},{1,3},{2,0},{3,1},{4,6},{5,7},{6,4},{7,5},{8,10},{9,11},{10,... | collective-permute-start | bytes 98312 | tf_op jit(solution)/shard_map/ppermute | solution.py:35
  22.6 2.4 %collective-permute-start.6 = (bf16[8,2048]{1,0:T(8,128)(2,1)S(1)}, bf16[8,2048]{1,0:T(8,128)(2,1)S(1)}, u32[]{:S(2)}, u32[]{:S(2)}) collective-permute-start(bf16[8,2048]{1,0:T(8,128)(2,1)S(1)} %collective-permute-done.2.refs_3_), channel_id=1, source_target_pairs={{0,1},{1,0},{2,3},{3,2},{4,5},{5,4},{6,7},{7,6},{8,9},{9,8},{10,11... | collective-permute-start | bytes 98312 | tf_op jit(solution)/shard_map/ppermute | solution.py:35
  25.0 5.4 %collective-permute-start.4 = (bf16[8,2048]{1,0:T(8,128)(2,1)S(1)}, bf16[8,2048]{1,0:T(8,128)(2,1)S(1)}, u32[]{:S(2)}, u32[]{:S(2)}) collective-permute-start(bf16[8,2048]{1,0:T(8,128)(2,1)S(1)} %collective-permute-done.3.refs_3_), channel_id=1, source_target_pairs={{0,1},{1,0},{2,3},{3,2},{4,5},{5,4},{6,7},{7,6},{8,9},{9,8},{10,11... | collective-permute-start | bytes 98312 | tf_op jit(solution)/shard_map/ppermute | solution.py:35
  32.9 22.8 %copy-start = (bf16[4,4096]{1,0:T(4,128)(2,1)S(1)}, bf16[4,4096]{1,0:T(4,128)(2,1)}, u32[]{:S(2)}) copy-start(bf16[4,4096]{1,0:T(4,128)(2,1)} %taps.1) | copy-start | bytes 98308
  32.9 22.8 %copy-start.1 = (f32[16]{0:T(128)S(1)}, f32[16]{0:T(128)}, u32[]{:S(2)}) copy-start(f32[16]{0:T(128)} %refs_1_.1) | copy-start | bytes 196
  32.9 22.8 %copy-start.2 = (f32[16]{0:T(128)S(1)}, f32[16]{0:T(128)}, u32[]{:S(2)}) copy-start(f32[16]{0:T(128)} %refs_2_.1) | copy-start | bytes 196
  32.9 22.7 %all-to-all-start = ((bf16[16,136,256]{2,1,0:T(8,128)(2,1)}), bf16[16,136,256]{2,1,0:T(8,128)(2,1)S(1)}, u32[]{:S(2)}, u32[]{:S(2)}) async-start(bf16[16,136,256]{2,1,0:T(8,128)(2,1)} %bitcast.5), calls=%async_computation | async-start | bytes 2228224 | tf_op jit(solution)/shard_map/all_to_all | solution.py:535
  62.7 7.0 %collective-permute-start.7 = (bf16[4,128,128]{2,1,0:T(8,128)(2,1)S(1)}, bf16[4,128,128]{2,1,0:T(8,128)(2,1)S(1)}, u32[]{:S(2)}, u32[]{:S(2)}) collective-permute-start(bf16[4,128,128]{2,1,0:T(8,128)(2,1)S(1)} %get-tuple-element.36), channel_id=1, source_target_pairs={{0,16},{1,17},{2,18},{3,19},{4,20},{5,21},{6,22},{7,23},{8,24},{9,... | collective-permute-start | bytes 393224 | tf_op jit(solution)/shard_map/ppermute | solution.py:30
  67.2 2.5 %copy-start.3 = (f32[128]{0:T(128)S(1)}, f32[128]{0:T(128)}, u32[]{:S(2)}) copy-start(f32[128]{0:T(128)} %param.13) | copy-start | bytes 1540
  71.0 5.0 %collective-permute-start.8 = (bf16[128,512]{1,0:T(8,128)(2,1)S(1)}, bf16[128,512]{1,0:T(8,128)(2,1)S(1)}, u32[]{:S(2)}, u32[]{:S(2)}) collective-permute-start(bf16[128,512]{1,0:T(8,128)(2,1)S(1)} %get-tuple-element.38), channel_id=1, source_target_pairs={{0,4},{4,0},{8,12},{12,8},{1,5},{5,1},{9,13},{13,9},{2,6},{6,2},{1... | collective-permute-start | bytes 393224 | tf_op jit(solution)/shard_map/ppermute | solution.py:35
  71.9 8.4 %collective-permute-start.9 = (bf16[128,512]{1,0:T(8,128)(2,1)S(1)}, bf16[128,512]{1,0:T(8,128)(2,1)S(1)}, u32[]{:S(2)}, u32[]{:S(2)}) collective-permute-start(bf16[128,512]{1,0:T(8,128)(2,1)S(1)} %get-tuple-element.39), channel_id=1, source_target_pairs={{0,8},{4,12},{8,0},{12,4},{1,9},{5,13},{9,1},{13,5},{2,10},{6,14},... | collective-permute-start | bytes 393224 | tf_op jit(solution)/shard_map/ppermute | solution.py:35
  76.0 6.0 %collective-permute-start.10 = (bf16[128,512]{1,0:T(8,128)(2,1)S(1)}, bf16[128,512]{1,0:T(8,128)(2,1)S(1)}, u32[]{:S(2)}, u32[]{:S(2)}) collective-permute-start(bf16[128,512]{1,0:T(8,128)(2,1)S(1)} %get-tuple-element.40), channel_id=1, source_target_pairs={{0,12},{4,8},{8,4},{12,0},{1,13},{5,9},{9,5},{13,1},{2,14},{6,10},... | collective-permute-start | bytes 393224 | tf_op jit(solution)/shard_map/ppermute | solution.py:35
